TPU v7x, 32 devices: a whole 2x2x4 slice. The times are simulated.
32 devices in a mesh: ctx: 8 (over z, y), shard: 4 (over x, core).
Axes of the slice: x: 2, y: 2, z: 4, core: 2. Of those that a mesh axis runs over, the one named last changes fastest.
Arguments:
- inputs: bfloat16 [4, 2048, 1152], P('shard', 'ctx'), may hold values from -6 to 6
- gain_attn: bfloat16 [1152], P('shard'), may hold values from 0.5 to 1.5
- w_query: bfloat16 [1152, 1152], P('shard'), may hold values from -0.1875 to 0.1875
- w_key: bfloat16 [1152, 384], P('shard'), may hold values from -0.1875 to 0.1875
- w_value: bfloat16 [1152, 384], P('shard'), may hold values from -0.1875 to 0.1875
- w_out: bfloat16 [1152, 1152], P('shard'), may hold values from -3 to 3
- gain_mlp: bfloat16 [1152], P('shard'), may hold values from 0.5 to 1.5
- w_gate: bfloat16 [1152, 3072], P('shard'), may hold values from -0.1875 to 0.1875
- w_up: bfloat16 [1152, 3072], P('shard'), may hold values from -0.1875 to 0.1875
- w_down: bfloat16 [3072, 1152], P('shard'), may hold values from -0.109375 to 0.109375
- cotangent: bfloat16 [4, 2048, 1152], P('shard', 'ctx'), may hold values from -6 to 6
Outputs:
- output: bfloat16 [4, 2048, 1152], P('shard', 'ctx')
- grad_inputs: bfloat16 [4, 2048, 1152], P('shard', 'ctx')
- grad_gain_attn: float32 [1152], P('shard')
- grad_w_query: float32 [1152, 1152], P('shard')
- grad_w_key: float32 [1152, 384], P('shard')
- grad_w_value: float32 [1152, 384], P('shard')
- grad_w_out: float32 [1152, 1152], P('shard')
- grad_gain_mlp: float32 [1152], P('shard')
- grad_w_gate: float32 [1152, 3072], P('shard')
- grad_w_up: float32 [1152, 3072], P('shard')
- grad_w_down: float32 [3072, 1152], P('shard')
All inputs are finite; a program needn't handle non-finite values.
Results may differ from a plain program's by a relative error of at most 0.018.
Values may be sent and summed in bfloat16 or wider, within the bound.
No kernel may reach another device: no remote copies, remote signals or barrier semaphores. Data moves between devices by JAX's collectives and lax.ppermute only.
A program may use at most 320 MiB of HBM per device.

v0:
```python
import functools
import math

import jax
import jax.numpy as jnp
from jax import lax
from jax.experimental import pallas as pl
from jax.experimental.pallas import tpu as pltpu
from jax.sharding import PartitionSpec as P

HEAD = 64
BLOCK = 256
EPSILON = 1e-05
LANES = 128
F32 = jnp.float32
BF16 = jnp.bfloat16
SCORE_SCALE = math.log2(math.e) * 0.125
NEGATIVE = -1e30
ALL_VMEM = 60 * 1024 * 1024
PART_VMEM = 32 * 1024 * 1024


def nn(left, right):
    return lax.dot_general(left, right, (((1,), (0,)), ((), ())), preferred_element_type=F32)


def nt(left, right):
    return lax.dot_general(left, right, (((1,), (1,)), ((), ())), preferred_element_type=F32)


def tn(left, right):
    return lax.dot_general(left, right, (((0,), (0,)), ((), ())), preferred_element_type=F32)


def ring_order(count):
    if count % 2:
        return list(range(count))
    return list(range(0, count, 2)) + list(range(count - 1, 0, -2))


def params(limit=ALL_VMEM):
    return pltpu.CompilerParams(vmem_limit_bytes=limit)


def cost(flops, moved, exps=0):
    return pl.CostEstimate(flops=int(flops), bytes_accessed=int(moved), transcendentals=int(exps))


HBM_SPEC = pl.BlockSpec(memory_space=pltpu.HBM)
SMEM_SPEC = pl.BlockSpec(memory_space=pltpu.SMEM)


def block(shape):
    return pl.BlockSpec(shape, lambda *_: (0,) * len(shape), pipeline_mode=pl.Buffered(1))


def call_once(
    kernel, outs, ins, held=(), moved=(), scratch=(), flops=0, limit=PART_VMEM, name=None
):
    return pl.pallas_call(
        kernel,
        out_shape=tuple(jax.ShapeDtypeStruct(shape, dtype) for shape, dtype in outs),
        grid=(1,),
        in_specs=[SMEM_SPEC] * len(held)
        + [block(array.shape) for array in ins]
        + [HBM_SPEC] * len(moved),
        out_specs=tuple(pl.BlockSpec(shape, lambda *_: (0,) * len(shape)) for shape, _ in outs),
        scratch_shapes=list(scratch),
        compiler_params=params(limit),
        cost_estimate=cost(flops, sum(2 * math.prod(shape) for shape, _ in outs) + 4e6),
        name=name,
    )(*held, *ins, *moved)


def swap_halves(tile):
    lane = lax.broadcasted_iota(jnp.int32, tile.shape, 1)
    ahead = pltpu.roll(tile, LANES - HEAD // 2, 1)
    behind = pltpu.roll(tile, HEAD // 2, 1)
    return jnp.where(lane % HEAD < HEAD // 2, ahead, behind)


def fetches(starts, pieces, whole, sems, sizes):
    copies = []
    for index, (piece, size) in enumerate(zip(pieces, sizes)):
        start = pl.multiple_of(starts[index], 16)
        copies.append(
            pltpu.make_async_copy(
                piece.at[pl.ds(0, size), :], whole.at[pl.ds(start, size), :], sems.at[index]
            )
        )
    return copies


def keys_kernel(starts_ref, x_ref, cos_ref, sin_ref, *rest, sizes, kvw):
    pieces = rest[: len(sizes)]
    hidden_ref, kv_ref, one_ref, two_ref, whole, bands, sems, band_sems = rest[len(sizes) :]
    copies = fetches(starts_ref, pieces, whole, sems, sizes)
    rows = sizes[0]
    for index, piece in enumerate(pieces):
        band = pltpu.make_async_copy(
            piece.at[pl.ds(rows, 16), :], bands.at[index], band_sems.at[index]
        )
        band.start()
        copies[index].start()
    x = x_ref[...].astype(F32)
    scale = lax.rsqrt(jnp.mean(x * x, axis=-1, keepdims=True) + EPSILON)
    width = x.shape[1]
    ones = jnp.zeros((8, width), F32)
    twos = jnp.zeros((8, width), F32)
    for index, piece in enumerate(pieces):
        pltpu.make_async_copy(
            piece.at[pl.ds(rows, 16), :], bands.at[index], band_sems.at[index]
        ).wait()
        band = bands[index].astype(F32)[:8, :]
        blank = jnp.zeros((8, width - rows), F32)
        first = jnp.concatenate([band[:, :rows], blank], axis=1)
        second = jnp.concatenate([band[:, rows : 2 * rows], blank], axis=1)
        ones = ones + pltpu.roll(first, starts_ref[index], 1)
        twos = twos + pltpu.roll(second, starts_ref[index], 1)
    one_ref[...] = ones[:1, :]
    two_ref[...] = twos[:1, :]
    hidden = (x * scale * ones[:1, :]).astype(BF16)
    hidden_ref[...] = hidden
    for copy in copies:
        copy.wait()
    pre = nn(hidden, whole[...])
    for start in range(0, kvw, LANES):
        tile = pre[:, start : start + LANES]
        turned = tile * cos_ref[...] + swap_halves(tile) * sin_ref[...]
        kv_ref[:, start : start + LANES] = turned.astype(BF16)
    kv_ref[:, kvw:] = pre[:, kvw:].astype(BF16)


def queries_kernel(starts_ref, hidden_ref, cos_ref, sin_ref, *rest, sizes):
    pieces = rest[: len(sizes)]
    query_ref, whole, sems = rest[len(sizes) :]
    copies = fetches(starts_ref, pieces, whole, sems, sizes)
    for copy in copies:
        copy.start()
    for copy in copies:
        copy.wait()
    pre = nn(hidden_ref[...], whole[...])
    for start in range(0, pre.shape[1], LANES):
        tile = pre[:, start : start + LANES]
        turned = tile * cos_ref[...] + swap_halves(tile) * sin_ref[...]
        query_ref[:, start : start + LANES] = turned.astype(BF16)


def attend_kernel(
    table_ref,
    q_ref,
    kv_ref,
    x_ref,
    gain_ref,
    *rest,
    sizes,
    groups,
    per,
    blocks,
):
    pieces = rest[:-13]
    (
        out_ref,
        attended_ref,
        log_ref,
        mid_ref,
        normed_ref,
        cols_ref,
        acc,
        top,
        total,
        whole,
        scores,
        tall,
        sems,
    ) = rest[-13:]
    step = pl.program_id(0)
    last = table_ref[blocks]
    starts = [table_ref[blocks + 1 + index] for index in range(len(sizes))]
    count = q_ref.shape[0]
    kvw = groups * HEAD

    @pl.when(step == 0)
    def _():
        for copy in fetches(starts, pieces, whole, sems, sizes):
            copy.start()
        turned = q_ref[...].T
        for group in range(groups):
            for member in range(per):
                head = group * per + member
                cols_ref[group, :, member * count : (member + 1) * count] = turned[
                    head * HEAD : (head + 1) * HEAD, :
                ]
        acc[...] = jnp.zeros_like(acc)
        total[...] = jnp.zeros_like(total)
        top[...] = jnp.full_like(top, NEGATIVE)

    @pl.when(step <= last)
    def _():
        def score(group):
            key = kv_ref[:, group * HEAD : (group + 1) * HEAD]
            scores[group % 2] = nn(key, cols_ref[group])

        score(0)
        for group in range(groups):
            if group + 1 < groups:
                score(group + 1)
            value = kv_ref[:, kvw + group * HEAD : kvw + (group + 1) * HEAD]
            raw = scores[group % 2]
            old = top[group : group + 1, :]
            new = jnp.maximum(old, jnp.max(raw, axis=0, keepdims=True))
            shrink = jnp.exp2((old - new) * SCORE_SCALE)
            probs = jnp.exp2((raw - new) * SCORE_SCALE)
            top[group : group + 1, :] = new
            total[group : group + 1, :] = total[group : group + 1, :] * shrink + jnp.sum(
                probs, axis=0, keepdims=True
            )
            acc[group] = acc[group] * shrink + tn(value, probs.astype(BF16))

    @pl.when(step == blocks - 1)
    def _():
        for group in range(groups):
            sums = total[group : group + 1, :]
            log_ref[group : group + 1, :] = top[
                group : group + 1, :
            ] * SCORE_SCALE + jnp.log2(sums)
            rowed = acc[group] / sums
            for member in range(per):
                head = group * per + member
                tall[head * HEAD : (head + 1) * HEAD, :] = rowed[
                    :, member * count : (member + 1) * count
                ]
        out_ref[...] = tall[...]
        attended = tall[...].astype(BF16).T
        attended_ref[...] = attended
        for copy in fetches(starts, pieces, whole, sems, sizes):
            copy.wait()
        mid = x_ref[...].astype(F32) + nn(attended, whole[...])
        mid_ref[...] = mid
        scale = lax.rsqrt(jnp.mean(mid * mid, axis=-1, keepdims=True) + EPSILON)
        normed_ref[...] = (mid * scale * gain_ref[...]).astype(BF16)


def attend_back_kernel(
    table_ref,
    kv_ref,
    cols_ref,
    out_ref,
    log_ref,
    mid_ref,
    gain_ref,
    cot_ref,
    gn_own_ref,
    gn_near_ref,
    gn_far_ref,
    cos_ref,
    sin_ref,
    *rest,
    sizes,
    groups,
    per,
    blocks,
):
    pieces = rest[: len(sizes)]
    (
        gq_ref,
        gkv_ref,
        branch_ref,
        gmid_ref,
        ggain_ref,
        whole,
        d_cols,
        delta,
        acc,
        probs_all,
        tall,
        sems,
    ) = rest[len(sizes) :]
    step = pl.program_id(0)
    last = table_ref[blocks]
    starts = [table_ref[blocks + 1 + index] for index in range(len(sizes))]
    count = kv_ref.shape[0]
    kvw = groups * HEAD

    @pl.when(step == 0)
    def _():
        copies = fetches(starts, pieces, whole, sems, sizes)
        for copy in copies:
            copy.start()
        mid = mid_ref[...]
        incoming = (
            gn_own_ref[...].astype(F32) + gn_near_ref[...].astype(F32)
        ) + gn_far_ref[...].astype(F32)
        gain = gain_ref[...]
        scale = lax.rsqrt(jnp.mean(mid * mid, axis=-1, keepdims=True) + EPSILON)
        weighted = incoming * gain
        inner = jnp.mean(weighted * mid, axis=-1, keepdims=True)
        ggain_ref[...] = jnp.sum(incoming * mid * scale, axis=0, keepdims=True)
        grad_mid = (
            cot_ref[...].astype(F32) + scale * weighted - mid * (scale * scale * scale * inner)
        )
        gmid_ref[...] = grad_mid
        branch = grad_mid.astype(BF16)
        branch_ref[...] = branch
        for copy in copies:
            copy.wait()
        grads = nt(branch, whole[...]).astype(BF16)
        turned = grads.T
        tall[...] = turned.astype(F32) * out_ref[...]
        for group in range(groups):
            for member in range(per):
                head = group * per + member
                span = slice(head * HEAD, (head + 1) * HEAD)
                cols = slice(member * count, (member + 1) * count)
                d_cols[group, :, cols] = turned[span, :]
                delta[group : group + 1, cols] = jnp.sum(tall[span, :], axis=0, keepdims=True)
        acc[...] = jnp.zeros_like(acc)

    @pl.when(step > last)
    def _():
        gkv_ref[...] = jnp.zeros_like(gkv_ref)

    @pl.when(step <= last)
    def _():
        def spans(group):
            return (
                slice(group * HEAD, (group + 1) * HEAD),
                slice(kvw + group * HEAD, kvw + (group + 1) * HEAD),
            )

        def score(group):
            key_span, value_span = spans(group)
            probs_all[group % 2, 0] = nn(kv_ref[:, key_span], cols_ref[group])
            probs_all[group % 2, 1] = nn(kv_ref[:, value_span], d_cols[group])

        score(0)
        for group in range(groups):
            if group + 1 < groups:
                score(group + 1)
            key_span, value_span = spans(group)
            probs = jnp.exp2(
                probs_all[group % 2, 0] * SCORE_SCALE - log_ref[group : group + 1, :]
            )
            grad_scores = (
                probs * (probs_all[group % 2, 1] - delta[group : group + 1, :])
            ).astype(BF16)
            gkv_ref[:, value_span] = nt(probs.astype(BF16), d_cols[group]).astype(BF16)
            gkv_ref[:, key_span] = (nt(grad_scores, cols_ref[group]) * 0.125).astype(BF16)
            acc[group] = acc[group] + tn(kv_ref[:, key_span], grad_scores)

    @pl.when(step == blocks - 1)
    def _():
        for group in range(groups):
            for member in range(per):
                head = group * per + member
                tall[head * HEAD : (head + 1) * HEAD, :] = (
                    acc[group, :, member * count : (member + 1) * count] * 0.125
                )
        for start in range(0, tall.shape[0], LANES):
            tile = tall[start : start + LANES, :].T
            turned = tile * cos_ref[...] - swap_halves(tile) * sin_ref[...]
            gq_ref[:, start : start + LANES] = turned.astype(BF16)


def kv_back_kernel(starts_ref, grad_ref, cos_ref, sin_ref, hidden_ref, out_ref, *rest, kvw):
    outs, full = rest[:-1], rest[-1]
    for start in range(0, kvw, LANES):
        tile = grad_ref[:, start : start + LANES].astype(F32)
        turned = tile * cos_ref[...] - swap_halves(tile) * sin_ref[...]
        out_ref[:, start : start + LANES] = turned.astype(BF16)
    out_ref[:, kvw:] = grad_ref[:, kvw:]
    full[...] = tn(hidden_ref[...], out_ref[...])
    for index, out in enumerate(outs):
        start = pl.multiple_of(starts_ref[index], 8)
        out[...] = full[pl.ds(start, out.shape[0]), :].astype(BF16)


def stack_kernel(*refs):
    parts, out_ref = refs[:-1], refs[-1]
    tile = out_ref.shape[1]
    row = 0
    for index in range(0, len(parts), 3):
        first, second, third = parts[index : index + 3]
        rows, columns = first.shape
        for start in range(0, columns, tile):
            span = slice(start, start + tile)
            total = (
                first[:, span].astype(F32) + second[:, span].astype(F32)
            ) + third[:, span].astype(F32)
            out_ref[row : row + rows, :] = total.astype(BF16)
            row += rows


def inputs_kernel(starts_ref, gq_ref, gkv_ref, x_ref, gain_ref, gmid_ref, *rest, sizes):
    hops = len(sizes)
    grad_ref, ggain_ref, whole_q, whole_kv, q_sems, kv_sems = rest[2 * hops :]
    copies = fetches(starts_ref, rest[:hops], whole_q, q_sems, sizes)
    copies += fetches(starts_ref, rest[hops : 2 * hops], whole_kv, kv_sems, sizes)
    for copy in copies:
        copy.start()
    for copy in copies:
        copy.wait()
    incoming = nt(gq_ref[...], whole_q[...]) + nt(gkv_ref[...], whole_kv[...])
    x = x_ref[...].astype(F32)
    scale = lax.rsqrt(jnp.mean(x * x, axis=-1, keepdims=True) + EPSILON)
    weighted = incoming * gain_ref[...]
    inner = jnp.mean(weighted * x, axis=-1, keepdims=True)
    ggain_ref[...] = jnp.sum(incoming * x * scale, axis=0, keepdims=True)
    grad = gmid_ref[...] + scale * weighted - x * (scale * scale * scale * inner)
    grad_ref[...] = grad.astype(BF16)


def weight_grads_kernel(starts_ref, hidden_ref, query_ref, attended_ref, branch_ref, *rest):
    outs, full = rest[:-1], rest[-1]
    hops = len(outs) // 2
    for index, (left, right) in enumerate(((hidden_ref, query_ref), (attended_ref, branch_ref))):
        full[...] = tn(left[...], right[...])
        for hop, out in enumerate(outs[index * hops : (index + 1) * hops]):
            start = pl.multiple_of(starts_ref[hop], 8)
            out[...] = full[pl.ds(start, out.shape[0]), :].astype(BF16)


def units(normed, cot, gate_mat, up_mat, down_mat):
    gate = nn(normed, gate_mat)
    up = nn(normed, up_mat)
    grad = nt(cot, down_mat)
    sigmoid = 1.0 / (1.0 + jnp.exp(-gate))
    silu = gate * sigmoid
    return (
        (silu * up).astype(BF16),
        (grad * up * (sigmoid * (1.0 + gate * (1.0 - sigmoid)))).astype(BF16),
        (grad * silu).astype(BF16),
    )


def feed_near_kernel(
    starts_ref, own_gate_ref, own_up_ref, near_ref, far_ref, down_ref, *rest, half, lanes
):
    normed_refs, cot_refs = rest[:2], rest[2:4]
    gate_mat_out, up_mat_out, act_out, gate_out, up_out, back_out = rest[4:10]
    gate_mat, up_mat, down_mat, tokens, cots, act, grad_gate, grad_up, back = rest[10:19]
    mat_sems, token_sems, out_sems = rest[19:]
    rows = near_ref.shape[0]
    own = gate_mat.shape[1]
    mats = []

    def place(source, row, column, height, breadth):
        target = gate_mat if column < own else up_mat
        mats.append(
            pltpu.make_async_copy(
                source,
                target.at[pl.ds(pl.multiple_of(row, 16), height), pl.ds(column % own, breadth)],
                mat_sems.at[len(mats)],
            )
        )

    mine = pl.ds(pl.multiple_of(starts_ref[4] * own, LANES), own)
    for index, ref in enumerate((own_gate_ref, own_up_ref)):
        place(ref.at[:, mine], starts_ref[0], index * own, rows, own)
        place(near_ref.at[:, pl.ds(index * own, own)], starts_ref[1], index * own, rows, own)
    for spot in range(far_ref.shape[0]):
        for index in range(2):
            place(
                far_ref.at[spot, pl.ds(index * half, half), :],
                starts_ref[2 + index] + (spot % 2) * half,
                (spot // 2) * lanes,
                half,
                lanes,
            )
    loads = [
        pltpu.make_async_copy(ref, target.at[index], token_sems.at[slot, index])
        for slot, (refs, target) in enumerate(((normed_refs, tokens), (cot_refs, cots)))
        for index, ref in enumerate(refs)
    ]
    loads.append(pltpu.make_async_copy(down_ref, down_mat, token_sems.at[2, 0]))
    for copy in mats + loads:
        copy.start()
    for copy in mats:
        copy.wait()
    outs = [
        pltpu.make_async_copy(source, target, out_sems.at[index])
        for index, (source, target) in enumerate(
            (
                (gate_mat, gate_mat_out),
                (up_mat, up_mat_out),
                (act, act_out),
                (grad_gate, gate_out),
                (grad_up, up_out),
                (back, back_out),
            )
        )
    ]
    for copy in outs[:2]:
        copy.start()
    for copy in loads:
        copy.wait()

    def token_block(index, carry):
        act[index], grad_gate[index], grad_up[index] = units(
            tokens[index], cots[index], gate_mat[...], up_mat[...], down_mat[...]
        )
        back[index] = (
            nt(grad_gate[index], gate_mat[...]) + nt(grad_up[index], up_mat[...])
        ).astype(BF16)
        return carry

    lax.fori_loop(0, 2, token_block, 0)
    for copy in outs[2:]:
        copy.start()
    for copy in outs:
        copy.wait()


def feed_far_kernel(
    starts_ref, gate_mat_ref, up_mat_ref, down_ref, act_in, gate_in, up_in, *rest, per_shard
):
    hops = 4
    normed_refs, cot_refs = rest[:hops], rest[hops : 2 * hops]
    tiles_out, act_out, gate_out, up_out = rest[2 * hops : 2 * hops + 4]
    gate_mat, up_mat, down_mat, tokens, cots, turned, act, grad_gate, grad_up, tiles = rest[
        2 * hops + 4 : 2 * hops + 14
    ]
    mat_sems, token_sems, cot_sems, unit_sems, out_sems, tile_sems = rest[2 * hops + 14 :]
    width, own = gate_mat.shape
    count = tokens.shape[1]
    places, height, tile = tiles.shape
    rows = height // 3
    mats = [
        pltpu.make_async_copy(source, target, mat_sems.at[index])
        for index, (source, target) in enumerate(
            ((gate_mat_ref, gate_mat), (up_mat_ref, up_mat), (down_ref, down_mat))
        )
    ]
    token_copies = [
        pltpu.make_async_copy(ref, tokens.at[index], token_sems.at[index])
        for index, ref in enumerate(normed_refs)
    ]
    cot_copies = [
        pltpu.make_async_copy(ref, cots.at[pl.ds(index * count, count), :], cot_sems.at[index])
        for index, ref in enumerate(cot_refs)
    ]
    unit_copies = [
        pltpu.make_async_copy(source.at[index], target.at[pl.ds(index * count, count), :],
                              unit_sems.at[slot, index])
        for slot, (source, target) in enumerate(
            ((act_in, act), (gate_in, grad_gate), (up_in, grad_up))
        )
        for index in range(2)
    ]
    for copy in mats + token_copies[2:] + cot_copies[2:]:
        copy.start()
    for copy in token_copies[:2] + cot_copies[:2] + unit_copies:
        copy.start()
    for copy in token_copies[:2]:
        copy.wait()
    for index in range(2):
        turned[:, index * count : (index + 1) * count] = tokens[index].T
    for copy in mats + token_copies[2:] + cot_copies[2:]:
        copy.wait()

    def token_block(index, carry):
        span = pl.ds(pl.multiple_of(index * count, count), count)
        normed = tokens[index]
        act[span, :], grad_gate[span, :], grad_up[span, :] = units(
            normed, cots[span, :], gate_mat[...], up_mat[...], down_mat[...]
        )
        turned[:, span] = normed.T
        return carry

    lax.fori_loop(2, hops, token_block, 0)
    late = pl.ds(2 * count, 2 * count)
    outs = [
        pltpu.make_async_copy(source.at[late, :], target, out_sems.at[index])
        for index, (source, target) in enumerate(
            ((act, act_out), (grad_gate, gate_out), (grad_up, up_out))
        )
    ]
    for copy in outs:
        copy.start()
    for copy in cot_copies[:2] + unit_copies:
        copy.wait()

    def tile_copy(spot, slot):
        low, high = ((0, 2 * rows), (2 * rows, 3 * rows))[slot]
        return pltpu.make_async_copy(
            tiles.at[spot, pl.ds(low, high - low), :],
            tiles_out.at[spot, pl.ds(low, high - low), :],
            tile_sems.at[slot, spot],
        )

    def row_block(index, carry):
        left = turned[pl.ds(pl.multiple_of(index * rows, 16), rows), :]
        spot = lax.rem(index + starts_ref[hops], hops) * per_shard
        for slot, ref in ((0, grad_gate), (1, grad_up)):
            grad = nn(left, ref[...])
            for part in range(per_shard):
                tiles[spot + part, slot * rows : (slot + 1) * rows, :] = grad[
                    :, part * tile : (part + 1) * tile
                ].astype(BF16)
        for part in range(per_shard):
            tile_copy(spot + part, 0).start()
        return carry

    lax.fori_loop(0, hops, row_block, 0)
    band = own // places
    turned[:own, :] = act[...].T

    def down_block(index, carry):
        left = turned[pl.ds(pl.multiple_of(index * 2 * band, 16), 2 * band), :]
        grad = nn(left, cots[...])
        for part in range(2):
            for split in range(width // tile):
                start = 2 * rows + split * band
                tiles[2 * index + part, start : start + band, :] = grad[
                    part * band : (part + 1) * band, split * tile : (split + 1) * tile
                ].astype(BF16)
            tile_copy(2 * index + part, 1).start()
        return carry

    lax.fori_loop(0, places // 2, down_block, 0)
    for copy in outs:
        copy.wait()
    for spot in range(places):
        for slot in range(2):
            tile_copy(spot, slot).wait()


def normed_back_kernel(gate_ref, up_ref, gate_mat_ref, up_mat_ref, *outs):
    count = outs[0].shape[0]
    for index, out in enumerate(outs):
        span = slice(index * count, (index + 1) * count)
        out[...] = (
            nt(gate_ref[span, :], gate_mat_ref[...]) + nt(up_ref[span, :], up_mat_ref[...])
        ).astype(BF16)


def widen_kernel(
    shard_ref,
    gate_up_ref,
    down_in_ref,
    mixed_ref,
    gate_ref,
    up_ref,
    down_ref,
    query_ref,
    out_ref,
    stack,
    *,
    rows,
):
    step = pl.program_id(0)
    tile = gate_ref.shape[1]
    band = down_ref.shape[0]
    share = mixed_ref.shape[1]
    gate_ref[...] = gate_up_ref[0, :rows, :].astype(F32)
    up_ref[...] = gate_up_ref[0, rows:, :].astype(F32)
    for split in range(down_ref.shape[1] // tile):
        down_ref[:, split * tile : (split + 1) * tile] = down_in_ref[
            0, split * band : (split + 1) * band, :
        ].astype(F32)
    stack[pl.ds(pl.multiple_of(step * share, 8), share), :] = mixed_ref[0].astype(F32)

    @pl.when(step == pl.num_programs(0) - 1)
    def _():
        cuts = query_ref.shape[1] // tile
        for cut in range(cuts):
            span = slice(cut * tile, (cut + 1) * tile)
            query_ref[:, span] = stack[cut * rows : (cut + 1) * rows, :]
            out_ref[:, span] = stack[(cuts + cut) * rows : (cuts + cut + 1) * rows, :]


def on_device(
    inputs,
    gain_attn,
    w_query,
    w_key,
    w_value,
    w_out,
    gain_mlp,
    w_gate,
    w_up,
    w_down,
    cotangent,
    *,
    n_ctx,
    n_shard,
):
    x = inputs[0]
    cot = cotangent[0]
    count, width = x.shape
    rows, qw = w_query.shape
    kvw = w_key.shape[1]
    ff_own = w_down.shape[0]
    ff = w_gate.shape[1]
    groups = kvw // HEAD
    per = qw // kvw
    blocks = n_ctx
    per_shard = n_ctx // n_shard
    tile = ff_own // per_shard
    assert count == BLOCK and n_shard == 4 and ff_own * n_shard == ff
    aligned = tile % LANES == 0
    order = ring_order(n_ctx)
    places = [order.index(index) for index in range(n_ctx)]
    shard = lax.axis_index("shard")
    ctx = lax.axis_index("ctx")
    shard_arr = shard.astype(jnp.int32)[None]

    def after(value, done):
        return lax.optimization_barrier((value, done))[0]

    def hop(value, distance):
        pairs = [(index, index ^ distance) for index in range(n_shard)]
        return lax.ppermute(value, "shard", pairs)

    def ctx_hop(value, distance):
        pairs = [(index, index ^ distance) for index in range(n_ctx)]
        return lax.ppermute(value, "ctx", pairs)

    def gather(value, done):
        far = hop(after(value, done), 2)
        return [value, hop(value, 1), far, hop(far, 1)]

    def halves(parts):
        third = hop(parts[3], 1)
        first = hop(parts[1], 1)
        across = (parts[2].astype(F32) + third.astype(F32)).astype(BF16)
        return parts[0], first, across

    def reduce(parts):
        own, first, across = halves(parts)
        return [own, first, hop(across, 2)]

    def add(parts):
        return sum(part.astype(F32) for part in parts)

    def scatter(value):
        return lax.psum_scatter(
            value, "ctx", scatter_dimension=0, axis_index_groups=[order], tiled=False
        )

    def collect(value):
        return lax.all_gather(value, "ctx", axis=0, axis_index_groups=[order], tiled=True)

    lane = jnp.arange(LANES, dtype=jnp.int32)
    frequency = jnp.exp((lane % (HEAD // 2)).astype(F32) * (-2.0 * math.log(10000.0) / HEAD))
    positions = (ctx * count + jnp.arange(count, dtype=jnp.int32)).astype(F32)
    angles = positions[:, None] * frequency[None, :]
    cosine = jnp.cos(angles)
    sine = jnp.where(lane % HEAD < HEAD // 2, -1.0, 1.0)[None, :] * jnp.sin(angles)

    gains = jnp.concatenate([gain_attn, gain_mlp])
    gain_rows = jnp.zeros((16, 2 * kvw), BF16).at[0, : 2 * rows].set(gains)
    kv_own = jnp.concatenate([jnp.concatenate([w_key, w_value], axis=1), gain_rows], axis=0)
    far = hop(kv_own, 2)
    kv_weights = [kv_own, hop(kv_own, 1), far, hop(far, 1)]
    starts = jnp.stack(
        [(shard ^ k) * rows for k in range(n_shard)] + [shard]
    ).astype(jnp.int32)
    sizes = (rows,) * n_shard
    table = jnp.concatenate(
        [jnp.array(places, jnp.int32), ctx.astype(jnp.int32)[None], starts]
    )

    def columns(peer):
        start = peer * ff_own
        return jnp.concatenate(
            [
                lax.dynamic_slice_in_dim(w_gate, start, ff_own, 1),
                lax.dynamic_slice_in_dim(w_up, start, ff_own, 1),
            ],
            axis=1,
        )

    half = rows // 2
    lanes = 4 * ff_own // n_ctx
    spot = jnp.array(places, jnp.int32)[ctx]
    chosen = []
    for distance in (2, 3):
        peer = (shard ^ distance) * ff_own
        column = peer + lax.rem(spot // 2 * lanes, ff_own)
        cuts = [
            lax.dynamic_slice(mat, (spot % 2 * half, column), (half, lanes))
            for mat in (w_gate, w_up)
        ]
        chosen.append(jnp.where(spot // 2 * lanes < ff_own, cuts[0], cuts[1]))
    near_columns = columns(shard ^ 1)
    cosine, sine, near_columns, table, starts, *chosen = lax.optimization_barrier(
        (cosine, sine, near_columns, table, starts, *chosen)
    )
    q_weights = gather(w_query, far)
    out_weights = gather(w_out, q_weights[2])

    fetch_sems = pltpu.SemaphoreType.DMA((n_shard,))
    hidden, kv, gain_one, gain_two = call_once(
        functools.partial(keys_kernel, sizes=sizes, kvw=kvw),
        [((count, width), BF16), ((count, 2 * kvw), BF16), ((1, width), F32), ((1, width), F32)],
        [x, cosine, sine],
        held=[starts],
        moved=kv_weights,
        scratch=[
            pltpu.VMEM((width, 2 * kvw), BF16),
            pltpu.VMEM((n_shard, 16, 2 * kvw), BF16),
            fetch_sems,
            fetch_sems,
        ],
        flops=4 * count * width * kvw,
        limit=ALL_VMEM,
        name="keys",
    )
    all_kv = collect(kv)

    (queries,) = call_once(
        functools.partial(queries_kernel, sizes=sizes),
        [((count, qw), BF16)],
        [hidden, cosine, sine],
        held=[starts],
        moved=q_weights,
        scratch=[pltpu.VMEM((width, qw), BF16), fetch_sems],
        flops=2 * count * width * qw,
        name="queries",
    )

    far_tiles = [
        hop(after(part, (out_weights[2], queries)), k) for part, k in zip(chosen, (2, 3))
    ]
    far_tile = jnp.concatenate(far_tiles, axis=0)
    far_rows = collect(after(far_tile, kv)[None])
    near_part = hop(near_columns, 1)
    cot_near = hop(cot, 1)
    cot_far = hop(after(cot, far_tile), 2)

    shared = dict(sizes=sizes, groups=groups, per=per, blocks=blocks)
    fixed = lambda *shape: pl.BlockSpec(shape, lambda step, table: (0,) * len(shape))
    kv_spec = pl.BlockSpec(
        (count, 2 * kvw), lambda step, table: (table[jnp.minimum(step, table[blocks])], 0)
    )
    once = lambda *shape: block(shape)
    weight_specs = [HBM_SPEC] * len(sizes)
    span = per * count
    out_tall, attended, log_total, mid, normed, q_cols = pl.pallas_call(
        functools.partial(attend_kernel, **shared),
        out_shape=(
            jax.ShapeDtypeStruct((qw, count), F32),
            jax.ShapeDtypeStruct((count, qw), BF16),
            jax.ShapeDtypeStruct((8, span), F32),
            jax.ShapeDtypeStruct((count, width), F32),
            jax.ShapeDtypeStruct((count, width), BF16),
            jax.ShapeDtypeStruct((groups, HEAD, span), BF16),
        ),
        grid_spec=pltpu.PrefetchScalarGridSpec(
            num_scalar_prefetch=1,
            grid=(blocks,),
            in_specs=[once(count, qw), kv_spec, once(count, width), once(1, width)]
            + weight_specs,
            out_specs=[
                fixed(qw, count),
                fixed(count, qw),
                fixed(8, span),
                fixed(count, width),
                fixed(count, width),
                fixed(groups, HEAD, span),
            ],
            scratch_shapes=[
                pltpu.VMEM((groups, HEAD, span), F32),
                pltpu.VMEM((8, span), F32),
                pltpu.VMEM((8, span), F32),
                pltpu.VMEM((qw, width), BF16),
                pltpu.VMEM((2, count, span), F32),
                pltpu.VMEM((qw, count), F32),
                pltpu.SemaphoreType.DMA((len(sizes),)),
            ],
        ),
        compiler_params=params(),
        cost_estimate=cost(
            4 * count * count * blocks * qw, 12e6, count * count * blocks * groups * per
        ),
        name="attend",
    )(table, queries, all_kv, x, gain_two, *out_weights)

    normed_far = hop(normed, 2)
    normed_near = hop(normed, 1)
    cot_far = after(cot_far, normed)
    far_rows = after(far_rows, normed)
    all_count = n_shard * count
    if aligned:
        two = ((2, count, ff_own), BF16)
        mats = [((width, ff_own), BF16)] * 2
        pair = (2, count, width)
        gate_mat, up_mat, *near_units, back = pl.pallas_call(
            functools.partial(feed_near_kernel, half=half, lanes=lanes),
            out_shape=tuple(
                jax.ShapeDtypeStruct(*out) for out in [*mats, two, two, two, (pair, BF16)]
            ),
            in_specs=[SMEM_SPEC] + [HBM_SPEC] * 9,
            out_specs=(HBM_SPEC,) * 6,
            scratch_shapes=[
                pltpu.VMEM((width, ff_own), BF16),
                pltpu.VMEM((width, ff_own), BF16),
                pltpu.VMEM((ff_own, width), BF16),
                pltpu.VMEM(pair, BF16),
                pltpu.VMEM(pair, BF16),
                pltpu.VMEM(*two),
                pltpu.VMEM(*two),
                pltpu.VMEM(*two),
                pltpu.VMEM(pair, BF16),
                pltpu.SemaphoreType.DMA((4 + 2 * n_ctx,)),
                pltpu.SemaphoreType.DMA((3, 2)),
                pltpu.SemaphoreType.DMA((6,)),
            ],
            compiler_params=params(),
            cost_estimate=cost(10 * 2 * count * width * ff_own, 12e6),
            name="feed_near",
        )(
            starts,
            w_gate,
            w_up,
            near_part,
            far_rows,
            w_down,
            normed,
            normed_near,
            cot,
            cot_near,
        )
        normed_far, cot_far = lax.optimization_barrier((normed_far, cot_far, back))[:2]
        normed_pieces = [normed, normed_near, normed_far, hop(normed_far, 1)]
        cot_pieces = [cot, cot_near, cot_far, hop(cot_far, 1)]
        late = ((2 * count, ff_own), BF16)
        feed_tiles, *far_units = pl.pallas_call(
            functools.partial(feed_far_kernel, per_shard=per_shard),
            out_shape=tuple(
                jax.ShapeDtypeStruct(*out)
                for out in [((n_ctx, 3 * rows, tile), BF16), late, late, late]
            ),
            in_specs=[SMEM_SPEC] + [HBM_SPEC] * (6 + 2 * n_shard),
            out_specs=(HBM_SPEC,) * 4,
            scratch_shapes=[
                pltpu.VMEM((width, ff_own), BF16),
                pltpu.VMEM((width, ff_own), BF16),
                pltpu.VMEM((ff_own, width), BF16),
                pltpu.VMEM((n_shard, count, width), BF16),
                pltpu.VMEM((all_count, width), BF16),
                pltpu.VMEM((width, all_count), BF16),
                pltpu.VMEM((all_count, ff_own), BF16),
                pltpu.VMEM((all_count, ff_own), BF16),
                pltpu.VMEM((all_count, ff_own), BF16),
                pltpu.VMEM((n_ctx, 3 * rows, tile), BF16),
                pltpu.SemaphoreType.DMA((3,)),
                pltpu.SemaphoreType.DMA((n_shard,)),
                pltpu.SemaphoreType.DMA((n_shard,)),
                pltpu.SemaphoreType.DMA((3, 2)),
                pltpu.SemaphoreType.DMA((3,)),
                pltpu.SemaphoreType.DMA((2, n_ctx)),
            ],
            compiler_params=params(),
            cost_estimate=cost(9 * all_count * width * ff_own, 25e6),
            name="feed_far",
        )(
            starts, gate_mat, up_mat, w_down, *near_units, *normed_pieces, *cot_pieces
        )
        to_own, to_near = back[0], back[1]
        act_parts = [near_units[0].reshape(2 * count, ff_own), far_units[0]]
        grad_gate_far, grad_up_far = far_units[1:]
    else:
        normed_pieces = [normed, normed_near, normed_far, hop(normed_far, 1)]
        cot_pieces = [cot, cot_near, cot_far, hop(cot_far, 1)]
        tiles_of = far_rows.reshape(n_ctx // 2, 2, 2, half, lanes)
        tiles_of = tiles_of.transpose(2, 1, 3, 0, 4).reshape(2, rows, 2 * ff_own)
        gate_mat = jnp.zeros((width, ff_own), BF16)
        up_mat = jnp.zeros((width, ff_own), BF16)
        for part, start in zip((columns(shard), near_part, tiles_of[0], tiles_of[1]), starts):
            gate_mat = lax.dynamic_update_slice_in_dim(gate_mat, part[:, :ff_own], start, 0)
            up_mat = lax.dynamic_update_slice_in_dim(up_mat, part[:, ff_own:], start, 0)
        all_cot = jnp.concatenate(cot_pieces, axis=0)
        all_normed = jnp.concatenate(normed_pieces, axis=0)
        gate = nn(all_normed, gate_mat)
        up = nn(all_normed, up_mat)
        grad_activated = nt(all_cot, w_down)
        sigmoid = jax.nn.sigmoid(gate)
        activated = (gate * sigmoid * up).astype(BF16)
        grad_gate = (grad_activated * up * (sigmoid * (1.0 + gate * (1.0 - sigmoid)))).astype(BF16)
        grad_up = (grad_activated * (gate * sigmoid)).astype(BF16)

        def tiles(grad):
            pieces = grad.astype(BF16).reshape(n_shard, rows, per_shard, tile)
            pieces = pieces.transpose(0, 2, 1, 3)
            return jnp.roll(pieces, shard, axis=0).reshape(n_ctx, rows, tile)

        down = tn(activated, all_cot).astype(BF16)
        down = down.reshape(n_ctx, ff_own // n_ctx, width // tile, tile).transpose(0, 2, 1, 3)
        feed_tiles = jnp.concatenate(
            [
                tiles(tn(all_normed, grad_gate)),
                tiles(tn(all_normed, grad_up)),
                down.reshape(n_ctx, rows, tile),
            ],
            axis=1,
        )
        grad_gate_far, grad_up_far = grad_gate[2 * count :], grad_up[2 * count :]
        back = nt(grad_gate[: 2 * count], gate_mat) + nt(grad_up[: 2 * count], up_mat)
        to_own, to_near = back[:count].astype(BF16), back[count:].astype(BF16)
        act_parts = [activated[: 2 * count], activated[2 * count :]]
    from_near = hop(to_near, 1)
    feed_sum = scatter(feed_tiles)
    down_sum = feed_sum[2 * rows :]
    pairs = []
    for index in range(n_ctx):
        for source in range(n_shard):
            target = (places[index] // per_shard - source) % n_shard
            pairs.append((index * n_shard + source, index * n_shard + target))
    gate_up_sum = lax.ppermute(feed_sum[: 2 * rows], ("ctx", "shard"), pairs)

    to_far, to_third = call_once(
        normed_back_kernel,
        [((count, width), BF16)] * 2,
        [grad_gate_far, grad_up_far, gate_mat, up_mat],
        flops=8 * count * width * ff_own,
        limit=ALL_VMEM,
        name="normed_back",
    )
    third = hop(to_third, 1)
    across = (to_far.astype(F32) + third.astype(F32)).astype(BF16)
    from_far = hop(across, 2)

    part_out = [after(nn(part, w_down).astype(BF16), from_far) for part in act_parts]
    part_out = [part[k * count : (k + 1) * count] for part in part_out for k in range(2)]
    output = (mid + add(reduce(part_out))).astype(BF16)[None]

    place_spec = pl.BlockSpec((count, 2 * kvw), lambda step, table: (table[step], 0))
    grad_query, grad_kv, branch, grad_mid, gain_two_part = pl.pallas_call(
        functools.partial(attend_back_kernel, **shared),
        out_shape=(
            jax.ShapeDtypeStruct((count, qw), BF16),
            jax.ShapeDtypeStruct((blocks * count, 2 * kvw), BF16),
            jax.ShapeDtypeStruct((count, width), BF16),
            jax.ShapeDtypeStruct((count, width), F32),
            jax.ShapeDtypeStruct((1, width), F32),
        ),
        grid_spec=pltpu.PrefetchScalarGridSpec(
            num_scalar_prefetch=1,
            grid=(blocks,),
            in_specs=[
                kv_spec,
                once(groups, HEAD, span),
                once(qw, count),
                once(8, span),
                once(count, width),
                once(1, width),
                once(count, width),
                once(count, width),
                once(count, width),
                once(count, width),
                once(count, LANES),
                once(count, LANES),
            ]
            + weight_specs,
            out_specs=[
                fixed(count, qw),
                place_spec,
                fixed(count, width),
                fixed(count, width),
                fixed(1, width),
            ],
            scratch_shapes=[
                pltpu.VMEM((qw, width), BF16),
                pltpu.VMEM((groups, HEAD, span), BF16),
                pltpu.VMEM((8, span), F32),
                pltpu.VMEM((groups, HEAD, span), F32),
                pltpu.VMEM((2, 2, count, span), F32),
                pltpu.VMEM((qw, count), F32),
                pltpu.SemaphoreType.DMA((len(sizes),)),
            ],
        ),
        compiler_params=params(),
        cost_estimate=cost(
            10 * count * count * blocks * qw, 14e6, count * count * blocks * groups * per
        ),
        name="attend_back",
    )(
        table,
        all_kv,
        q_cols,
        out_tall,
        log_total,
        mid,
        gain_two,
        cot,
        to_own,
        from_near,
        from_far,
        cosine,
        sine,
        *out_weights,
    )
    own_kv = scatter(after(grad_kv, down_sum).reshape(n_ctx, count, 2 * kvw))

    def stack(parts, breadth, name):
        height = sum(part.shape[0] * part.shape[1] for part in parts[::3]) // breadth
        if breadth % LANES:
            wide = jnp.concatenate(
                [add(parts[index : index + 3]) for index in range(0, len(parts), 3)], axis=1
            )
            wide = wide.astype(BF16).reshape(rows, -1, breadth)
            return wide.transpose(1, 0, 2).reshape(height, breadth)
        return call_once(stack_kernel, [((height, breadth), BF16)], parts, flops=1e6, name=name)[0]

    grad_blocks = call_once(
        weight_grads_kernel,
        [((rows, qw), BF16)] * n_shard + [((rows, width), BF16)] * n_shard,
        [hidden, grad_query, attended, branch],
        held=[starts],
        scratch=[pltpu.VMEM((width, qw), F32)],
        flops=4 * count * width * qw,
        limit=ALL_VMEM,
        name="weight_grads",
    )
    parts_query = reduce(grad_blocks[:n_shard])
    parts_out = reduce(grad_blocks[n_shard:])
    mixed = stack(parts_query + parts_out, tile, "stack_mixed")
    mixed_sum = scatter(after(mixed, own_kv).reshape(n_ctx, -1, tile))

    grad_kv_pre, *kv_blocks = call_once(
        functools.partial(kv_back_kernel, kvw=kvw),
        [((count, 2 * kvw), BF16)] + [((rows, 2 * kvw), BF16)] * n_shard,
        [own_kv, cosine, sine, hidden],
        held=[starts],
        scratch=[pltpu.VMEM((width, 2 * kvw), F32)],
        flops=4 * count * width * kvw,
        name="kv_back",
    )
    sum_kv = stack(reduce(kv_blocks), LANES, "stack_kv").reshape(n_ctx, -1, LANES)
    shares = jnp.concatenate([gate_up_sum, down_sum, mixed_sum])
    gathered = collect(after(shares, sum_kv)[None])

    def exchange(value):
        return lax.all_to_all(value, "ctx", split_axis=0, concat_axis=0, tiled=True)

    own_sum = jnp.sum(exchange(sum_kv).astype(F32), axis=0, keepdims=True).astype(BF16)
    both = exchange(jnp.broadcast_to(own_sum, sum_kv.shape))
    both = both.reshape(2 * kvw // LANES, rows, LANES).transpose(1, 0, 2).reshape(rows, 2 * kvw)
    grad_w_key = both[:, :kvw].astype(F32)
    grad_w_value = both[:, kvw:].astype(F32)

    grad_x, gain_one_part = call_once(
        functools.partial(inputs_kernel, sizes=sizes),
        [((count, width), BF16), ((1, width), F32)],
        [grad_query, grad_kv_pre, x, gain_one, grad_mid],
        held=[starts],
        moved=[*q_weights, *kv_weights],
        scratch=[
            pltpu.VMEM((width, qw), BF16),
            pltpu.VMEM((width, 2 * kvw), BF16),
            fetch_sems,
            fetch_sems,
        ],
        flops=2 * count * width * (qw + 2 * kvw),
        name="grad_inputs",
    )

    gain_parts = jnp.concatenate([gain_one_part, gain_two_part], axis=0)
    for distance in [1 << bit for bit in range(n_shard.bit_length() - 1)]:
        gain_parts = gain_parts + hop(gain_parts, distance)
    for distance in [1 << bit for bit in range(n_ctx.bit_length() - 1)]:
        gain_parts = gain_parts + ctx_hop(gain_parts, distance)
    own_gains = lax.dynamic_slice_in_dim(gain_parts, shard * rows, rows, 1)

    if aligned:
        share = mixed_sum.shape[0]
        rolled = lambda step, where: (lax.rem(step + where[0] * per_shard, n_ctx), 0, 0)
        band = ff_own // n_ctx
        grad_w_gate, grad_w_up, grad_w_down, grad_w_query, grad_w_out = pl.pallas_call(
            functools.partial(widen_kernel, rows=rows),
            out_shape=(
                jax.ShapeDtypeStruct((rows, ff), F32),
                jax.ShapeDtypeStruct((rows, ff), F32),
                jax.ShapeDtypeStruct((ff_own, width), F32),
                jax.ShapeDtypeStruct((rows, qw), F32),
                jax.ShapeDtypeStruct((rows, width), F32),
            ),
            grid_spec=pltpu.PrefetchScalarGridSpec(
                num_scalar_prefetch=1,
                grid=(n_ctx,),
                in_specs=[
                    pl.BlockSpec((1, 2 * rows, tile), rolled),
                    pl.BlockSpec((1, rows, tile), lambda step, where: (step, 2, 0)),
                    pl.BlockSpec((1, share, tile), lambda step, where: (step, 3 * rows // share, 0)),
                ],
                out_specs=[
                    pl.BlockSpec((rows, tile), lambda step, where: (0, step)),
                    pl.BlockSpec((rows, tile), lambda step, where: (0, step)),
                    pl.BlockSpec((band, width), lambda step, where: (step, 0)),
                    pl.BlockSpec((rows, qw), lambda step, where: (0, 0)),
                    pl.BlockSpec((rows, width), lambda step, where: (0, 0)),
                ],
                scratch_shapes=[pltpu.VMEM((n_ctx * share, tile), F32)],
            ),
            compiler_params=params(),
            cost_estimate=cost(1e6, 20e6),
            name="widen",
        )(shard_arr, gathered, gathered, gathered)
    else:

        def untile(part):
            back = jnp.roll(part.reshape(n_shard, per_shard, rows, tile), -shard, axis=0)
            back = back.reshape(n_ctx, rows, tile).transpose(1, 0, 2)
            return back.reshape(rows, ff).astype(F32)

        grad_w_gate = untile(gathered[:, :rows])
        grad_w_up = untile(gathered[:, rows : 2 * rows])
        down = gathered[:, 2 * rows : 3 * rows].reshape(n_ctx, width // tile, -1, tile)
        grad_w_down = down.transpose(0, 2, 1, 3).reshape(ff_own, width).astype(F32)
        wide = gathered[:, 3 * rows :].reshape(2 * qw // tile, rows, tile).transpose(1, 0, 2)
        wide = wide.reshape(rows, 2 * qw).astype(F32)
        grad_w_query, grad_w_out = wide[:, :qw], wide[:, qw:]

    return (
        output,
        grad_x[None],
        own_gains[0],
        grad_w_query,
        grad_w_key,
        grad_w_value,
        grad_w_out,
        own_gains[1],
        grad_w_gate,
        grad_w_up,
        grad_w_down,
    )


def solution(mesh):
    tokens = P("shard", "ctx", None)
    split = P("shard", None)
    gain = P("shard")
    placed = (tokens, gain, split, split, split, split, gain, split, split, split, tokens)
    return jax.shard_map(
        functools.partial(on_device, n_ctx=mesh.shape["ctx"], n_shard=mesh.shape["shard"]),
        mesh=mesh,
        in_specs=placed,
        out_specs=(tokens, tokens, gain, split, split, split, split, gain, split, split, split),
        check_vma=False,
    )
```

profile of v0, /device:TPU:9, one launch (start us, length us, event | category | flops | bytes accessed | tf_op | source)
XLA Modules:
  0.0 380.3 jit_solution(5982159823227582358)
XLA Ops:
  8.0 1.1 fusion.2.rest_0_.rest_4_
  9.1 1.3 collective-permute-start.1
  11.3 1.2 dynamic_slice.26
  15.8 1.3 concatenate.28.table_ref
  17.1 1.4 dynamic-slice_select_fusion
  18.5 1.2 constant_dynamic-slice_fusion
  20.7 1.5 collective-permute-start.2
  22.3 1.2 fusion.3
  25.5 4.3 %keys.1 = (bf16[256,1152]{1,0:T(8,128)(2,1)}, bf16[256,768]{1,0:T(8,128)(2,1)}, f32[1,1152]{1,0:T(1,128)}, f32[1,1152]{1,0:T(1,128)}) custom-call(s32[5]{0:T(128)} %stack.23.starts_ref, bf16[256,1152]{1,0:T(8,128)(2,1)} %bitcast.40, f32[256,128]{1,0:T(8,128)} %get-tuple-element.94.cos_ref, f32[256,128]{1,0:T(8,128)} %get-tuple-element.95.sin_ref, ...), custom_call_target="tpu_custom_call" | custom-call | flops 452984832 | bytes 4987648 | tf_op jit(solution)/shard_map/keys/pallas_call | solution.py:60
  29.9 1.3 collective-permute-start.4
  31.4 15.1 %collective-permute-done.4.rest_2_ = bf16[288,1152]{1,0:T(8,128)(2,1)S(1)} collective-permute-done((bf16[288,1152]{1,0:T(8,128)(2,1)S(1)}, bf16[288,1152]{1,0:T(8,128)(2,1)S(1)}, u32[]{:S(2)}, u32[]{:S(2)}) %collective-permute-start.4) | collective-permute-done | bytes 663584 | tf_op jit(solution)/shard_map/ppermute | solution.py:713
  47.3 1.2 collective-permute-start.7
  49.0 1.1 copy-done.18
  50.1 2.6 queries.1.q_ref
  53.5 10.6 %collective-permute-done.7.rest_2_ = bf16[288,1152]{1,0:T(8,128)(2,1)S(1)} collective-permute-done((bf16[288,1152]{1,0:T(8,128)(2,1)}, bf16[288,1152]{1,0:T(8,128)(2,1)S(1)}, u32[]{:S(2)}, u32[]{:S(2)}) %collective-permute-start.7) | collective-permute-done | bytes 663584 | tf_op jit(solution)/shard_map/ppermute | solution.py:713
  64.1 1.2 collective-permute-start.10
  65.3 1.1 collective-permute-start.11
  66.4 1.7 collective-permute-done.10
  68.2 3.1 collective-permute-done.11
  73.3 1.2 collective-permute-start.15
  74.8 1.9 collective-permute-done.8.rest_3_
  76.7 12.4 %attend.1 = (f32[1152,256]{1,0:T(8,128)}, bf16[256,1152]{1,0:T(8,128)(2,1)}, f32[8,768]{1,0:T(8,128)}, f32[256,1152]{1,0:T(8,128)}, bf16[256,1152]{1,0:T(8,128)(2,1)}, /*index=5*/bf16[6,64,768]{2,1,0:T(8,128)(2,1)}) custom-call(s32[14]{0:T(128)} %concatenate.28.table_ref, bf16[256,1152]{1,0:T(8,128)(2,1)} %copy-done.20, ...), custom_call_target="tpu_custom_call" | custom-call | flops 2415919104 | bytes 12000000 | tf_op jit(solution)/shard_map/attend/pallas_call | solution.py:840
  90.5 11.0 %all-gather.8.cloned.1.call-done = bf16[2304,384]{1,0:T(8,128)(2,1)} async-done(((bf16[288,384]{1,0:T(8,128)(2,1)}), bf16[2304,384]{1,0:T(8,128)(2,1)}) %all-gather.8.cloned.1.call-update) | async-done | bytes 1769488 | tf_op jit(solution)/shard_map/all_gather | solution.py:742
  102.4 11.4 %feed_near.1 = (bf16[1152,768]{1,0:T(8,128)(2,1)}, bf16[1152,768]{1,0:T(8,128)(2,1)}, bf16[2,256,768]{2,1,0:T(8,128)(2,1)}, bf16[2,256,768]{2,1,0:T(8,128)(2,1)}...) custom-call(s32[5]{0:T(128)} %stack.23.starts_ref, bf16[288,3072]{1,0:T(8,128)(2,1)} %own_gate_ref.1, ...), custom_call_target="tpu_custom_call" | custom-call | flops 4529848320 | bytes 12000000 | tf_op jit(solution)/shard_map/feed_near/pallas_call | solution.py:889
  113.8 4.4 %collective-permute-start.16 = (bf16[256,1152]{1,0:T(8,128)(2,1)}, bf16[256,1152]{1,0:T(8,128)(2,1)S(1)}, u32[]{:S(2)}, u32[]{:S(2)}) collective-permute-start(bf16[256,1152]{1,0:T(8,128)(2,1)} %collective-permute-done.14.rest_2_), channel_id=1, source_target_pairs={{0,1},{1,0},{2,3},{3,2},{4,5},{5,4},{6,7},{7,6},{8,9},{9,8},{10,11... | collective-permute-start | bytes 1769480 | tf_op jit(solution)/shard_map/ppermute | solution.py:713
  118.3 1.8 collective-permute-done.16.rest_3_
  121.7 17.5 %feed_far.1 = (bf16[8,864,384]{2,1,0:T(8,128)(2,1)}, bf16[512,768]{1,0:T(8,128)(2,1)}, bf16[512,768]{1,0:T(8,128)(2,1)}, bf16[512,768]{1,0:T(8,128)(2,1)}) custom-call(s32[5]{0:T(128)} %stack.23.starts_ref, bf16[1152,768]{1,0:T(8,128)(2,1)} %get-tuple-element.111.gate_mat_ref, bf16[1152,768]{1,0:T(8,128)(2,1)} %get-tuple-element.112.up_mat_ref, ...), custom_call_target="tpu_custom_call" | custom-call | flops 8153726976 | bytes 25000000 | tf_op jit(solution)/shard_map/feed_far/pallas_call | solution.py:929
  139.5 5.7 %normed_back.1 = (bf16[256,1152]{1,0:T(8,128)(2,1)}, bf16[256,1152]{1,0:T(8,128)(2,1)}) custom-call(bf16[512,768]{1,0:T(8,128)(2,1)} %get-tuple-element.120.gate_ref, bf16[512,768]{1,0:T(8,128)(2,1)} %get-tuple-element.121.up_ref, bf16[1152,768]{1,0:T(8,128)(2,1)} %get-tuple-element.111.gate_mat_ref, bf16[1152,768]{1,0:T(8,128)(2,1)} %get-tuple-element.112.up_mat_ref), custom_call_target="tpu_custom_call" | custom-call | flops 1811939328 | bytes 5179648 | tf_op jit(solution)/shard_map/normed_back/pallas_call | solution.py:60
  147.5 1.4 collective-permute-start.19
  149.0 13.3 %collective-permute-done.19.gn_far_ref = bf16[256,1152]{1,0:T(8,128)(2,1)S(1)} collective-permute-done((bf16[256,1152]{1,0:T(8,128)(2,1)S(1)}, bf16[256,1152]{1,0:T(8,128)(2,1)S(1)}, u32[]{:S(2)}, u32[]{:S(2)}) %collective-permute-start.19) | collective-permute-done | bytes 589856 | tf_op jit(solution)/shard_map/ppermute | solution.py:713
  163.1 19.4 %attend_back.1 = (bf16[256,1152]{1,0:T(8,128)(2,1)}, bf16[2048,768]{1,0:T(8,128)(2,1)}, bf16[256,1152]{1,0:T(8,128)(2,1)}, f32[256,1152]{1,0:T(8,128)}, f32[1,1152]{1,0:T(1,128)}) custom-call(s32[14]{0:T(128)} %concatenate.28.table_ref, bf16[2048,768]{1,0:T(8,128)(2,1)} %all-gather.6.cloned.1.call-done.kv_ref, ...), custom_call_target="tpu_custom_call" | custom-call | flops 6039797760 | bytes 14000000 | tf_op jit(solution)/shard_map/attend_back/pallas_call | solution.py:1030
  182.5 14.8 %reduce-scatter.7.cloned.1.call-done = bf16[1,864,384]{2,1,0:T(8,128)(2,1)} async-done(((bf16[8,864,384]{2,1,0:T(8,128)(2,1)}), bf16[1,864,384]{2,1,0:T(8,128)(2,1)}) %reduce-scatter.7.cloned.1.call-update) | async-done | bytes 663568 | tf_op jit(solution)/shard_map/reduce_scatter | solution.py:737
  198.3 5.3 %weight_grads.1 = (bf16[288,1152]{1,0:T(8,128)(2,1)}, bf16[288,1152]{1,0:T(8,128)(2,1)}, bf16[288,1152]{1,0:T(8,128)(2,1)}, bf16[288,1152]{1,0:T(8,128)(2,1)}, b...) custom-call(s32[5]{0:T(128)} %stack.23.starts_ref, ...), custom_call_target="tpu_custom_call" | custom-call | flops 1358954496 | bytes 9308416 | tf_op jit(solution)/shard_map/weight_grads/pallas_call | solution.py:60
  204.8 1.4 collective-permute-done.34
  206.2 1.4 add_convert_fusion
  207.6 1.3 collective-permute-start.35
  209.4 14.5 %collective-permute-done.35.refs_5_ = bf16[288,1152]{1,0:T(8,128)(2,1)S(1)} collective-permute-done((bf16[288,1152]{1,0:T(8,128)(2,1)S(1)}, bf16[288,1152]{1,0:T(8,128)(2,1)S(1)}, u32[]{:S(2)}, u32[]{:S(2)}) %collective-permute-start.35) | collective-permute-done | bytes 663584 | tf_op jit(solution)/shard_map/ppermute | solution.py:713
  224.0 14.1 %collective-permute-done.32.refs_2_ = bf16[288,1152]{1,0:T(8,128)(2,1)S(1)} collective-permute-done((bf16[288,1152]{1,0:T(8,128)(2,1)S(1)}, bf16[288,1152]{1,0:T(8,128)(2,1)S(1)}, u32[]{:S(2)}, u32[]{:S(2)}) %collective-permute-start.32) | collective-permute-done | bytes 663584 | tf_op jit(solution)/shard_map/ppermute | solution.py:713
  238.1 1.6 stack_mixed.1
  242.1 1.6 kv_back.1
  243.7 1.2 collective-permute-start.37
  245.0 1.3 collective-permute-done.37
  246.5 1.3 collective-permute-start.38
  247.8 2.2 collective-permute-start.29
  250.0 8.0 %collective-permute-done.38.refs_2_ = bf16[288,768]{1,0:T(8,128)(2,1)S(1)} collective-permute-done((bf16[288,768]{1,0:T(8,128)(2,1)S(1)}, bf16[288,768]{1,0:T(8,128)(2,1)S(1)}, u32[]{:S(2)}, u32[]{:S(2)}) %collective-permute-start.38) | collective-permute-done | bytes 442400 | tf_op jit(solution)/shard_map/ppermute | solution.py:713
  258.9 4.3 %collective-permute-done.29 = bf16[576,384]{1,0:T(8,128)(2,1)} collective-permute-done((bf16[576,384]{1,0:T(8,128)(2,1)S(1)}, bf16[576,384]{1,0:T(8,128)(2,1)}, u32[]{:S(2)}, u32[]{:S(2)}) %collective-permute-start.29) | collective-permute-done | bytes 442400 | tf_op jit(solution)/shard_map/ppermute | solution.py:1011
  263.3 5.5 %reduce-scatter.11.cloned.1.call-done = bf16[1,216,384]{2,1,0:T(8,128)(2,1)} async-done(((bf16[8,216,384]{2,1,0:T(8,128)(2,1)}), bf16[1,216,384]{2,1,0:T(8,128)(2,1)}) %reduce-scatter.11.cloned.1.call-update) | async-done | bytes 165904
  268.7 2.1 pad_maximum_fusion.1
  270.8 3.0 convolution_convert_fusion
  273.9 4.2 %collective-permute-start.21 = (bf16[256,1152]{1,0:T(8,128)(2,1)S(1)}, bf16[256,1152]{1,0:T(8,128)(2,1)S(1)}, u32[]{:S(2)}, u32[]{:S(2)}) collective-permute-start(bf16[256,1152]{1,0:T(8,128)(2,1)S(1)} %slice.61), channel_id=1, source_target_pairs={{0,1},{1,0},{2,3},{3,2},{4,5},{5,4},{6,7},{7,6},{8,9},{9,8},{10,11... | collective-permute-start | bytes 1769480 | tf_op jit(solution)/shard_map/ppermute | solution.py:713
  278.2 1.2 convolution_convert_fusion.1
  280.4 1.2 copy-done.10
  281.5 5.1 %grad_inputs.1 = (bf16[256,1152]{1,0:T(8,128)(2,1)}, f32[1,1152]{1,0:T(1,128)S(1)}) custom-call(s32[5]{0:T(128)S(1)} %copy-done.22, bf16[256,1152]{1,0:T(8,128)(2,1)S(1)} %copy-done.17, bf16[256,768]{1,0:T(8,128)(2,1)S(1)} %get-tuple-element.134.gkv_ref, bf16[256,1152]{1,0:T(8,128)(2,1)S(1)} %bitcast.42, f32[1,1152]{1,0:T(1,128)S(1)} %copy-done.23, ...), custom_call_target="tpu_custom_call" | custom-call | flops 1132462080 | bytes 4592128 | tf_op jit(solution)/shard_map/grad_inputs/pallas_call | solution.py:60
  287.7 1.2 collective-permute-start.22
  288.9 3.8 all-to-all-start
  293.1 9.5 %collective-permute-done.25 = f32[2,1152]{1,0:T(2,128)S(1)} collective-permute-done((f32[2,1152]{1,0:T(2,128)S(1)}, f32[2,1152]{1,0:T(2,128)S(1)}, u32[]{:S(2)}, u32[]{:S(2)}) %collective-permute-start.25) | collective-permute-done | bytes 9248 | tf_op jit(solution)/shard_map/ppermute | solution.py:713
  303.1 2.6 collective-permute-done.26
  306.2 2.6 collective-permute-done.27
  308.8 1.3 collective-permute-start.28
  311.0 5.2 %all-to-all-start.1 = ((bf16[8,216,128]{2,1,0:T(8,128)(2,1)}), bf16[8,216,128]{2,1,0:T(8,128)(2,1)S(1)}, u32[]{:S(2)}, u32[]{:S(2)}) async-start(bf16[8,216,128]{2,1,0:T(8,128)(2,1)} %broadcast_in_dim.41), calls=%async_computation.3 | async-start | bytes 884736 | tf_op jit(solution)/shard_map/all_to_all | solution.py:1136
  316.2 2.3 fusion.1
  319.2 13.7 %all-to-all-done.1 = bf16[8,216,128]{2,1,0:T(8,128)(2,1)S(1)} async-done(((bf16[8,216,128]{2,1,0:T(8,128)(2,1)}), bf16[8,216,128]{2,1,0:T(8,128)(2,1)S(1)}, u32[]{:S(2)}, u32[]{:S(2)}) %all-to-all-start.1) | async-done | bytes 442400 | tf_op jit(solution)/shard_map/all_to_all | solution.py:1136
  333.9 29.8 %all-gather.10.cloned.1.call-done = bf16[8640,384]{1,0:T(8,128)(2,1)} async-done(((bf16[1080,384]{1,0:T(8,128)(2,1)}), bf16[8640,384]{1,0:T(8,128)(2,1)}) %all-gather.10.cloned.1.call-update) | async-done | bytes 6635536 | tf_op jit(solution)/shard_map/all_gather | solution.py:742
  363.7 9.7 %widen.1 = (f32[288,3072]{1,0:T(8,128)}, f32[288,3072]{1,0:T(8,128)}, f32[768,1152]{1,0:T(8,128)}, f32[288,1152]{1,0:T(8,128)}, f32[288,1152]{1,0:T(8,128)}) custom-call(s32[1]{0:T(128)} %bitcast.5.shard_ref, bf16[8,1080,384]{2,1,0:T(8,128)(2,1)} %bitcast.44, bf16[8,1080,384]{2,1,0:T(8,128)(2,1)} %bitcast.45, bf16[8,1080,384]{2,1,0:T(8,128)(2,1)} %bitcast.46), custom_call_target="tpu_custom_call" | custom-call | flops 1000000 | bytes 20000000 | tf_op jit(solution)/shard_map/widen/pallas_call | solution.py:1171
  (172 shorter events, 29.8 us)
Async XLA Ops:
  7.2 69.5 %all-gather.6.cloned.1.call-start = ((), (), s32[]{:S(2)}) async-start(), calls=%async_computation.5 | async-start | bytes 3538944 | tf_op jit(solution)/shard_map/all_gather | solution.py:742
  9.1 15.4 %copy-start = (bf16[304,768]{1,0:T(8,128)(2,1)}, bf16[304,768]{1,0:T(8,128)(2,1)S(1)}, u32[]{:S(2)}) copy-start(bf16[304,768]{1,0:T(8,128)(2,1)S(1)} %fusion.2.rest_0_.rest_4_) | copy-start | bytes 1400836
  9.1 11.6 %collective-permute-start.1 = (bf16[304,768]{1,0:T(8,128)(2,1)S(1)}, bf16[304,768]{1,0:T(8,128)(2,1)S(1)}, u32[]{:S(2)}, u32[]{:S(2)}) collective-permute-start(bf16[304,768]{1,0:T(8,128)(2,1)S(1)} %fusion.2.rest_0_.rest_4_), channel_id=1, source_target_pairs={{0,2},{1,3},{2,0},{3,1},{4,6},{5,7},{6,4},{7,5},{8,10},{9,11},{10,... | collective-permute-start | bytes 1400840 | tf_op jit(solution)/shard_map/ppermute | solution.py:713
  10.4 14.1 %collective-permute-start = (bf16[304,768]{1,0:T(8,128)(2,1)S(1)}, bf16[304,768]{1,0:T(8,128)(2,1)S(1)}, u32[]{:S(2)}, u32[]{:S(2)}) collective-permute-start(bf16[304,768]{1,0:T(8,128)(2,1)S(1)} %fusion.2.rest_0_.rest_4_), channel_id=1, source_target_pairs={{0,1},{1,0},{2,3},{3,2},{4,5},{5,4},{6,7},{7,6},{8,9},{9,8},{10,11... | collective-permute-start | bytes 1400840 | tf_op jit(solution)/shard_map/ppermute | solution.py:713
  20.7 3.8 %collective-permute-start.2 = (bf16[304,768]{1,0:T(8,128)(2,1)S(1)}, bf16[304,768]{1,0:T(8,128)(2,1)S(1)}, u32[]{:S(2)}, u32[]{:S(2)}) collective-permute-start(bf16[304,768]{1,0:T(8,128)(2,1)S(1)} %collective-permute-done.1.rest_2_.rest_6_), channel_id=1, source_target_pairs={{0,1},{1,0},{2,3},{3,2},{4,5},{5,4},{6,7},{7,6},{8,9},{9,8},{10,11... | collective-permute-start | bytes 1400840 | tf_op jit(solution)/shard_map/ppermute | solution.py:713
  24.5 5.4 %copy-start.2 = (bf16[288,1152]{1,0:T(8,128)(2,1)S(1)}, bf16[288,1152]{1,0:T(8,128)(2,1)}, u32[]{:S(2)}) copy-start(bf16[288,1152]{1,0:T(8,128)(2,1)} %rest_0_.7) | copy-start | bytes 1990660
  24.5 24.5 %copy-start.11 = (f32[256,128]{1,0:T(8,128)S(1)}, f32[256,128]{1,0:T(8,128)}, u32[]{:S(2)}) copy-start(f32[256,128]{1,0:T(8,128)} %get-tuple-element.95.sin_ref) | copy-start | bytes 393220
  24.5 24.5 %copy-start.13 = (f32[256,128]{1,0:T(8,128)S(1)}, f32[256,128]{1,0:T(8,128)}, u32[]{:S(2)}) copy-start(f32[256,128]{1,0:T(8,128)} %get-tuple-element.94.cos_ref) | copy-start | bytes 393220
  24.5 24.5 %copy-start.21 = (s32[5]{0:T(128)S(1)}, s32[5]{0:T(128)}, u32[]{:S(2)}) copy-start(s32[5]{0:T(128)} %stack.23.starts_ref) | copy-start | bytes 64
  29.8 71.6 %all-gather.8.cloned.1.call-start = ((), (), s32[]{:S(2)}) async-start(), calls=%async_computation.8 | async-start | bytes 1990656 | tf_op jit(solution)/shard_map/all_gather | solution.py:742
  29.9 16.7 %collective-permute-start.4 = (bf16[288,1152]{1,0:T(8,128)(2,1)S(1)}, bf16[288,1152]{1,0:T(8,128)(2,1)S(1)}, u32[]{:S(2)}, u32[]{:S(2)}) collective-permute-start(bf16[288,1152]{1,0:T(8,128)(2,1)S(1)} %copy-done.2), channel_id=1, source_target_pairs={{0,2},{1,3},{2,0},{3,1},{4,6},{5,7},{6,4},{7,5},{8,10},{9,11},{10,... | collective-permute-start | bytes 1990664 | tf_op jit(solution)/shard_map/ppermute | solution.py:713
  31.2 17.3 %collective-permute-start.3 = (bf16[288,1152]{1,0:T(8,128)(2,1)S(1)}, bf16[288,1152]{1,0:T(8,128)(2,1)S(1)}, u32[]{:S(2)}, u32[]{:S(2)}) collective-permute-start(bf16[288,1152]{1,0:T(8,128)(2,1)S(1)} %copy-done.2), channel_id=1, source_target_pairs={{0,1},{1,0},{2,3},{3,2},{4,5},{5,4},{6,7},{7,6},{8,9},{9,8},{10,11... | collective-permute-start | bytes 1990664 | tf_op jit(solution)/shard_map/ppermute | solution.py:713
  46.6 2.4 collective-permute-start.5
  47.3 16.9 %collective-permute-start.7 = (bf16[288,1152]{1,0:T(8,128)(2,1)}, bf16[288,1152]{1,0:T(8,128)(2,1)S(1)}, u32[]{:S(2)}, u32[]{:S(2)}) collective-permute-start(bf16[288,1152]{1,0:T(8,128)(2,1)} %rest_0_.6), channel_id=1, source_target_pairs={{0,2},{1,3},{2,0},{3,1},{4,6},{5,7},{6,4},{7,5},{8,10},{9,11},{10,... | collective-permute-start | bytes 1990664 | tf_op jit(solution)/shard_map/ppermute | solution.py:713
  64.1 7.2 %copy-start.36 = (bf16[288,1152]{1,0:T(8,128)(2,1)}, bf16[288,1152]{1,0:T(8,128)(2,1)S(1)}, u32[]{:S(2)}) copy-start(bf16[288,1152]{1,0:T(8,128)(2,1)S(1)} %collective-permute-done.7.rest_2_) | copy-start | bytes 1990660
  64.1 4.0 %collective-permute-start.10 = (bf16[144,384]{1,0:T(8,128)(2,1)S(1)}, bf16[144,384]{1,0:T(8,128)(2,1)S(1)}, u32[]{:S(2)}, u32[]{:S(2)}) collective-permute-start(bf16[144,384]{1,0:T(8,128)(2,1)S(1)} %get-tuple-element.104), channel_id=1, source_target_pairs={{0,2},{1,3},{2,0},{3,1},{4,6},{5,7},{6,4},{7,5},{8,10},{9,11},{10,... | collective-permute-start | bytes 331784 | tf_op jit(solution)/shard_map/ppermute | solution.py:713
  65.3 5.9 %collective-permute-start.11 = (bf16[144,384]{1,0:T(8,128)(2,1)S(1)}, bf16[144,384]{1,0:T(8,128)(2,1)S(1)}, u32[]{:S(2)}, u32[]{:S(2)}) collective-permute-start(bf16[144,384]{1,0:T(8,128)(2,1)S(1)} %get-tuple-element.106), channel_id=1, source_target_pairs={{0,3},{1,2},{2,1},{3,0},{4,7},{5,6},{6,5},{7,4},{8,11},{9,10},{10,... | collective-permute-start | bytes 331784 | tf_op jit(solution)/shard_map/ppermute | solution.py:713
  72.0 125.3 %reduce-scatter.7.cloned.1.call-start = ((), (), s32[]{:S(2)}) async-start(), calls=%async_computation.6 | async-start | bytes 5971968 | tf_op jit(solution)/shard_map/reduce_scatter | solution.py:737
  72.3 2.5 collective-permute-start.6
  72.7 4.0 %collective-permute-start.8 = (bf16[288,1152]{1,0:T(8,128)(2,1)}, bf16[288,1152]{1,0:T(8,128)(2,1)}, u32[]{:S(2)}, u32[]{:S(2)}) collective-permute-start(bf16[288,1152]{1,0:T(8,128)(2,1)} %copy-done.36), channel_id=1, source_target_pairs={{0,1},{1,0},{2,3},{3,2},{4,5},{5,4},{6,7},{7,6},{8,9},{9,8},{10,11... | collective-permute-start | bytes 1990664 | tf_op jit(solution)/shard_map/ppermute | solution.py:713
  72.8 28.6 %collective-permute-start.9 = (bf16[288,1536]{1,0:T(8,128)(2,1)}, bf16[288,1536]{1,0:T(8,128)(2,1)S(1)}, u32[]{:S(2)}, u32[]{:S(2)}) collective-permute-start(bf16[288,1536]{1,0:T(8,128)(2,1)} %pad_maximum_fusion), channel_id=1, source_target_pairs={{0,1},{1,0},{2,3},{3,2},{4,5},{5,4},{6,7},{7,6},{8,9},{9,8},{10,11... | collective-permute-start | bytes 2654216 | tf_op jit(solution)/shard_map/ppermute | solution.py:713
  73.2 28.3 %collective-permute-start.13 = (bf16[256,1152]{1,0:T(8,128)(2,1)}, bf16[256,1152]{1,0:T(8,128)(2,1)}, u32[]{:S(2)}, u32[]{:S(2)}) collective-permute-start(bf16[256,1152]{1,0:T(8,128)(2,1)} %bitcast.52), channel_id=1, source_target_pairs={{0,1},{1,0},{2,3},{3,2},{4,5},{5,4},{6,7},{7,6},{8,9},{9,8},{10,11... | collective-permute-start | bytes 1769480 | tf_op jit(solution)/shard_map/ppermute | solution.py:713
  73.3 17.2 %collective-permute-start.15 = (bf16[256,1152]{1,0:T(8,128)(2,1)}, bf16[256,1152]{1,0:T(8,128)(2,1)}, u32[]{:S(2)}, u32[]{:S(2)}) collective-permute-start(bf16[256,1152]{1,0:T(8,128)(2,1)} %bitcast.53), channel_id=1, source_target_pairs={{0,2},{1,3},{2,0},{3,1},{4,6},{5,7},{6,4},{7,5},{8,10},{9,11},{10,... | collective-permute-start | bytes 1769480 | tf_op jit(solution)/shard_map/ppermute | solution.py:713
  89.1 12.4 %collective-permute-start.12 = (bf16[256,1152]{1,0:T(8,128)(2,1)}, bf16[256,1152]{1,0:T(8,128)(2,1)}, u32[]{:S(2)}, u32[]{:S(2)}) collective-permute-start(bf16[256,1152]{1,0:T(8,128)(2,1)} %get-tuple-element.108.rest_0_), channel_id=1, source_target_pairs={{0,1},{1,0},{2,3},{3,2},{4,5},{5,4},{6,7},{7,6},{8,9},{9,8},{10,11... | collective-permute-start | bytes 1769480 | tf_op jit(solution)/shard_map/ppermute | solution.py:713
  89.5 24.3 %collective-permute-start.14 = (bf16[256,1152]{1,0:T(8,128)(2,1)}, bf16[256,1152]{1,0:T(8,128)(2,1)}, u32[]{:S(2)}, u32[]{:S(2)}) collective-permute-start(bf16[256,1152]{1,0:T(8,128)(2,1)} %get-tuple-element.108.rest_0_), channel_id=1, source_target_pairs={{0,2},{1,3},{2,0},{3,1},{4,6},{5,7},{6,4},{7,5},{8,10},{9,11},{10,... | collective-permute-start | bytes 1769480 | tf_op jit(solution)/shard_map/ppermute | solution.py:713
  113.8 6.2 %collective-permute-start.16 = (bf16[256,1152]{1,0:T(8,128)(2,1)}, bf16[256,1152]{1,0:T(8,128)(2,1)S(1)}, u32[]{:S(2)}, u32[]{:S(2)}) collective-permute-start(bf16[256,1152]{1,0:T(8,128)(2,1)} %collective-permute-done.14.rest_2_), channel_id=1, source_target_pairs={{0,1},{1,0},{2,3},{3,2},{4,5},{5,4},{6,7},{7,6},{8,9},{9,8},{10,11... | collective-permute-start | bytes 1769480 | tf_op jit(solution)/shard_map/ppermute | solution.py:713
  118.2 2.7 collective-permute-start.17
  139.2 100.4 %reduce-scatter.9.cloned.1.call-start = ((), (), s32[]{:S(2)}) async-start(), calls=%async_computation.7 | async-start | bytes 3538944 | tf_op jit(solution)/shard_map/reduce_scatter | solution.py:737
  139.5 6.0 %copy-start.28 = (bf16[2,256,1152]{2,1,0:T(8,128)(2,1)S(1)}, bf16[2,256,1152]{2,1,0:T(8,128)(2,1)}, u32[]{:S(2)}) copy-start(bf16[2,256,1152]{2,1,0:T(8,128)(2,1)} %get-tuple-element.117) | copy-start | bytes 3538948
  145.2 2.2 collective-permute-start.18
  146.5 2.5 collective-permute-start.23
  147.5 14.7 %collective-permute-start.19 = (bf16[256,1152]{1,0:T(8,128)(2,1)S(1)}, bf16[256,1152]{1,0:T(8,128)(2,1)S(1)}, u32[]{:S(2)}, u32[]{:S(2)}) collective-permute-start(bf16[256,1152]{1,0:T(8,128)(2,1)S(1)} %add_convert_fusion.4), channel_id=1, source_target_pairs={{0,2},{1,3},{2,0},{3,1},{4,6},{5,7},{6,4},{7,5},{8,10},{9,11},{10,... | collective-permute-start | bytes 1769480 | tf_op jit(solution)/shard_map/ppermute | solution.py:713
  149.0 13.3 %copy-start.37 = (bf16[256,1152]{1,0:T(8,128)(2,1)}, bf16[256,1152]{1,0:T(8,128)(2,1)S(1)}, u32[]{:S(2)}) copy-start(bf16[256,1152]{1,0:T(8,128)(2,1)S(1)} %collective-permute-done.23.gn_near_ref) | copy-start | bytes 1769476
  198.3 70.4 %reduce-scatter.11.cloned.1.call-start = ((), (), s32[]{:S(2)}) async-start(), calls=%async_computation.10 | async-start | bytes 1492992
  203.6 5.3 %copy-start.30 = (bf16[288,1152]{1,0:T(8,128)(2,1)S(1)}, bf16[288,1152]{1,0:T(8,128)(2,1)}, u32[]{:S(2)}) copy-start(bf16[288,1152]{1,0:T(8,128)(2,1)} %get-tuple-element.144) | copy-start | bytes 1990660
  203.6 2.6 collective-permute-start.34
  204.2 4.7 %collective-permute-start.31 = (bf16[288,1152]{1,0:T(8,128)(2,1)}, bf16[288,1152]{1,0:T(8,128)(2,1)S(1)}, u32[]{:S(2)}, u32[]{:S(2)}) collective-permute-start(bf16[288,1152]{1,0:T(8,128)(2,1)} %get-tuple-element.145), channel_id=1, source_target_pairs={{0,1},{1,0},{2,3},{3,2},{4,5},{5,4},{6,7},{7,6},{8,9},{9,8},{10,11... | collective-permute-start | bytes 1990664 | tf_op jit(solution)/shard_map/ppermute | solution.py:713
  204.3 5.1 %collective-permute-start.30 = (bf16[288,1152]{1,0:T(8,128)(2,1)}, bf16[288,1152]{1,0:T(8,128)(2,1)S(1)}, u32[]{:S(2)}, u32[]{:S(2)}) collective-permute-start(bf16[288,1152]{1,0:T(8,128)(2,1)} %get-tuple-element.143), channel_id=1, source_target_pairs={{0,1},{1,0},{2,3},{3,2},{4,5},{5,4},{6,7},{7,6},{8,9},{9,8},{10,11... | collective-permute-start | bytes 1990664 | tf_op jit(solution)/shard_map/ppermute | solution.py:713
  204.8 4.7 %collective-permute-start.33 = (bf16[288,1152]{1,0:T(8,128)(2,1)}, bf16[288,1152]{1,0:T(8,128)(2,1)S(1)}, u32[]{:S(2)}, u32[]{:S(2)}) collective-permute-start(bf16[288,1152]{1,0:T(8,128)(2,1)} %get-tuple-element.147), channel_id=1, source_target_pairs={{0,1},{1,0},{2,3},{3,2},{4,5},{5,4},{6,7},{7,6},{8,9},{9,8},{10,11... | collective-permute-start | bytes 1990664 | tf_op jit(solution)/shard_map/ppermute | solution.py:713
  206.2 31.9 %copy-start.15 = (bf16[288,1152]{1,0:T(8,128)(2,1)S(1)}, bf16[288,1152]{1,0:T(8,128)(2,1)}, u32[]{:S(2)}) copy-start(bf16[288,1152]{1,0:T(8,128)(2,1)} %get-tuple-element.142.refs_0_) | copy-start | bytes 1990660
  206.2 31.9 %copy-start.16 = (bf16[288,1152]{1,0:T(8,128)(2,1)S(1)}, bf16[288,1152]{1,0:T(8,128)(2,1)}, u32[]{:S(2)}) copy-start(bf16[288,1152]{1,0:T(8,128)(2,1)} %get-tuple-element.146.refs_3_) | copy-start | bytes 1990660
  207.6 16.3 %collective-permute-start.35 = (bf16[288,1152]{1,0:T(8,128)(2,1)S(1)}, bf16[288,1152]{1,0:T(8,128)(2,1)S(1)}, u32[]{:S(2)}, u32[]{:S(2)}) collective-permute-start(bf16[288,1152]{1,0:T(8,128)(2,1)S(1)} %add_convert_fusion), channel_id=1, source_target_pairs={{0,2},{1,3},{2,0},{3,1},{4,6},{5,7},{6,4},{7,5},{8,10},{9,11},{10,... | collective-permute-start | bytes 1990664 | tf_op jit(solution)/shard_map/ppermute | solution.py:713
  209.1 29.0 %collective-permute-start.32 = (bf16[288,1152]{1,0:T(8,128)(2,1)S(1)}, bf16[288,1152]{1,0:T(8,128)(2,1)S(1)}, u32[]{:S(2)}, u32[]{:S(2)}) collective-permute-start(bf16[288,1152]{1,0:T(8,128)(2,1)S(1)} %add_convert_fusion.1), channel_id=1, source_target_pairs={{0,2},{1,3},{2,0},{3,1},{4,6},{5,7},{6,4},{7,5},{8,10},{9,11},{10,... | collective-permute-start | bytes 1990664 | tf_op jit(solution)/shard_map/ppermute | solution.py:713
  239.7 124.0 %all-gather.10.cloned.1.call-start = ((), (), s32[]{:S(2)}) async-start(), calls=%async_computation.9 | async-start | bytes 7464960 | tf_op jit(solution)/shard_map/all_gather | solution.py:742
  242.1 5.6 %copy-start.29 = (bf16[1,864,384]{2,1,0:T(8,128)(2,1)S(1)}, bf16[1,864,384]{2,1,0:T(8,128)(2,1)}, u32[]{:S(2)}) copy-start(bf16[1,864,384]{2,1,0:T(8,128)(2,1)} %reduce-scatter.7.cloned.1.call-done) | copy-start | bytes 1990660
  243.7 2.7 collective-permute-start.37
  244.9 5.0 %collective-permute-start.36 = (bf16[288,768]{1,0:T(8,128)(2,1)S(1)}, bf16[288,768]{1,0:T(8,128)(2,1)S(1)}, u32[]{:S(2)}, u32[]{:S(2)}) collective-permute-start(bf16[288,768]{1,0:T(8,128)(2,1)S(1)} %get-tuple-element.152), channel_id=1, source_target_pairs={{0,1},{1,0},{2,3},{3,2},{4,5},{5,4},{6,7},{7,6},{8,9},{9,8},{10,11... | collective-permute-start | bytes 1327112 | tf_op jit(solution)/shard_map/ppermute | solution.py:713
  246.5 11.6 %collective-permute-start.38 = (bf16[288,768]{1,0:T(8,128)(2,1)S(1)}, bf16[288,768]{1,0:T(8,128)(2,1)S(1)}, u32[]{:S(2)}, u32[]{:S(2)}) collective-permute-start(bf16[288,768]{1,0:T(8,128)(2,1)S(1)} %add_convert_fusion.5), channel_id=1, source_target_pairs={{0,2},{1,3},{2,0},{3,1},{4,6},{5,7},{6,4},{7,5},{8,10},{9,11},{10,... | collective-permute-start | bytes 1327112 | tf_op jit(solution)/shard_map/ppermute | solution.py:713
  247.8 15.5 %collective-permute-start.29 = (bf16[576,384]{1,0:T(8,128)(2,1)S(1)}, bf16[576,384]{1,0:T(8,128)(2,1)}, u32[]{:S(2)}, u32[]{:S(2)}) collective-permute-start(bf16[576,384]{1,0:T(8,128)(2,1)S(1)} %slice_bitcast_fusion.2), channel_id=1, source_target_pairs={{0,0},{1,3},{2,2},{3,1},{4,7},{5,6},{6,5},{7,4},{8,8},{9,11},{10,1... | collective-permute-start | bytes 1327112 | tf_op jit(solution)/shard_map/ppermute | solution.py:1011
  270.8 7.3 %copy-start.34 = (bf16[768,1152]{1,0:T(8,128)(2,1)S(1)}, bf16[768,1152]{1,0:T(8,128)(2,1)}, u32[]{:S(2)}) copy-start(bf16[768,1152]{1,0:T(8,128)(2,1)} %down_ref.3) | copy-start | bytes 5308420
  270.8 7.3 %copy-start.41 = (bf16[2,256,768]{2,1,0:T(8,128)(2,1)S(1)}, bf16[2,256,768]{2,1,0:T(8,128)(2,1)}, u32[]{:S(2)}) copy-start(bf16[2,256,768]{2,1,0:T(8,128)(2,1)} %get-tuple-element.110.act_in) | copy-start | bytes 2359300
  273.9 12.8 %collective-permute-start.21 = (bf16[256,1152]{1,0:T(8,128)(2,1)S(1)}, bf16[256,1152]{1,0:T(8,128)(2,1)S(1)}, u32[]{:S(2)}, u32[]{:S(2)}) collective-permute-start(bf16[256,1152]{1,0:T(8,128)(2,1)S(1)} %slice.61), channel_id=1, source_target_pairs={{0,1},{1,0},{2,3},{3,2},{4,5},{5,4},{6,7},{7,6},{8,9},{9,8},{10,11... | collective-permute-start | bytes 1769480 | tf_op jit(solution)/shard_map/ppermute | solution.py:713
  279.4 7.2 %copy-start.26 = (bf16[512,1152]{1,0:T(8,128)(2,1)}, bf16[512,1152]{1,0:T(8,128)(2,1)S(1)}, u32[]{:S(2)}) copy-start(bf16[512,1152]{1,0:T(8,128)(2,1)S(1)} %convolution_convert_fusion.1) | copy-start | bytes 3538948
  280.3 35.9 %collective-permute-start.20 = (bf16[256,1152]{1,0:T(8,128)(2,1)}, bf16[256,1152]{1,0:T(8,128)(2,1)}, u32[]{:S(2)}, u32[]{:S(2)}) collective-permute-start(bf16[256,1152]{1,0:T(8,128)(2,1)} %slice.59), channel_id=1, source_target_pairs={{0,1},{1,0},{2,3},{3,2},{4,5},{5,4},{6,7},{7,6},{8,9},{9,8},{10,11... | collective-permute-start | bytes 1769480 | tf_op jit(solution)/shard_map/ppermute | solution.py:713
  286.6 6.0 %collective-permute-start.24 = (f32[2,1152]{1,0:T(2,128)S(1)}, f32[2,1152]{1,0:T(2,128)S(1)}, u32[]{:S(2)}, u32[]{:S(2)}) collective-permute-start(f32[2,1152]{1,0:T(2,128)S(1)} %pad_maximum_fusion.2), channel_id=1, source_target_pairs={{0,1},{1,0},{2,3},{3,2},{4,5},{5,4},{6,7},{7,6},{8,9},{9,8},{10,11... | collective-permute-start | bytes 27656 | tf_op jit(solution)/shard_map/ppermute | solution.py:713
  287.7 28.5 %copy-start.25 = (f32[256,1152]{1,0:T(8,128)S(1)}, f32[256,1152]{1,0:T(8,128)}, u32[]{:S(2)}) copy-start(f32[256,1152]{1,0:T(8,128)} %get-tuple-element.101.mid_ref) | copy-start | bytes 3538948
  287.7 28.5 %copy-start.27 = (bf16[512,1152]{1,0:T(8,128)(2,1)S(1)}, bf16[512,1152]{1,0:T(8,128)(2,1)}, u32[]{:S(2)}) copy-start(bf16[512,1152]{1,0:T(8,128)(2,1)} %copy-done.26) | copy-start | bytes 3538948
  287.7 28.5 %collective-permute-start.22 = (bf16[256,1152]{1,0:T(8,128)(2,1)}, bf16[256,1152]{1,0:T(8,128)(2,1)}, u32[]{:S(2)}, u32[]{:S(2)}) collective-permute-start(bf16[256,1152]{1,0:T(8,128)(2,1)} %add_convert_fusion.3), channel_id=1, source_target_pairs={{0,2},{1,3},{2,0},{3,1},{4,6},{5,7},{6,4},{7,5},{8,10},{9,11},{10,... | collective-permute-start | bytes 1769480 | tf_op jit(solution)/shard_map/ppermute | solution.py:713
  288.9 21.2 %all-to-all-start = ((bf16[8,216,128]{2,1,0:T(8,128)(2,1)}), bf16[8,216,128]{2,1,0:T(8,128)(2,1)S(1)}, u32[]{:S(2)}, u32[]{:S(2)}) async-start(bf16[8,216,128]{2,1,0:T(8,128)(2,1)} %bitcast.21), calls=%async_computation.2 | async-start | bytes 884736 | tf_op jit(solution)/shard_map/all_to_all | solution.py:1136
  292.7 10.0 %collective-permute-start.25 = (f32[2,1152]{1,0:T(2,128)S(1)}, f32[2,1152]{1,0:T(2,128)S(1)}, u32[]{:S(2)}, u32[]{:S(2)}) collective-permute-start(f32[2,1152]{1,0:T(2,128)S(1)} %fusion.7), channel_id=1, source_target_pairs={{0,2},{1,3},{2,0},{3,1},{4,6},{5,7},{6,4},{7,5},{8,10},{9,11},{10,... | collective-permute-start | bytes 27656 | tf_op jit(solution)/shard_map/ppermute | solution.py:713
  302.6 3.0 collective-permute-start.26
  305.6 3.2 collective-permute-start.27
  308.8 9.7 %collective-permute-start.28 = (f32[2,1152]{1,0:T(2,128)S(1)}, f32[2,1152]{1,0:T(2,128)S(1)}, u32[]{:S(2)}, u32[]{:S(2)}) collective-permute-start(f32[2,1152]{1,0:T(2,128)S(1)} %add.135), channel_id=1, source_target_pairs={{0,16},{4,20},{8,24},{12,28},{16,0},{20,4},{24,8},{28,12},{1,17},{... | collective-permute-start | bytes 27656 | tf_op jit(solution)/shard_map/ppermute | solution.py:717
  311.0 21.8 %all-to-all-start.1 = ((bf16[8,216,128]{2,1,0:T(8,128)(2,1)}), bf16[8,216,128]{2,1,0:T(8,128)(2,1)S(1)}, u32[]{:S(2)}, u32[]{:S(2)}) async-start(bf16[8,216,128]{2,1,0:T(8,128)(2,1)} %broadcast_in_dim.41), calls=%async_computation.3 | async-start | bytes 884736 | tf_op jit(solution)/shard_map/all_to_all | solution.py:1136
  (25 other events, 43.9 us)
Sparse Core Ops, SparseCore 0:
  29.9 38.3 all-gather.5
  72.1 29.2 all-gather.7
  139.4 57.8 reduce-scatter.6
  200.0 38.1 reduce-scatter.8
  241.0 27.6 reduce-scatter.10
  270.9 92.7 all-gather.9
where the time goes:
time: 381 us; the launch traced here: 380 us
  waiting for transfers between devices  184 us (48%)
  Pallas kernels  97.5 us (26%)
  starting transfers between devices  45.2 us (12%)
  local copies, waits for them, and re-layouts  18 us (5%)
  between operations  17.3 us (5%)
  other arithmetic  13.9 us (4%)
  matrix products  4.23 us (1%)
    ppermute x35, waiting for transfers between devices, hop(): return lax.ppermute(value, 'shard', pairs)  99.8 us
    all_gather x3, waiting for transfers between devices, collect(): lax.all_gather(value, 'ctx', axis=0, axis_index_groups=[order], tiled=True)  40.7 us
    ppermute x35, starting transfers between devices, hop(): return lax.ppermute(value, 'shard', pairs)  31 us
    pallas_call x8, Pallas kernels, call_once(): pl.pallas_call(kernel, out_shape=tuple((jax.ShapeDtypeStruct(shape, dtype...  27 us
    pallas_call x1, Pallas kernels, on_device(): pl.pallas_call(functools.partial(attend_back_kernel, **shared), out_shape...  19.4 us
    pallas_call x1, Pallas kernels, on_device(): pl.pallas_call(functools.partial(feed_far_kernel, per_shard=per_shard), o...  17.5 us
    reduce_scatter x2, waiting for transfers between devices, scatter(): lax.psum_scatter(value, 'ctx', scatter_dimension=0, axis_index_groups=[or...  14.8 us
    all_to_all x2, waiting for transfers between devices, exchange(): return lax.all_to_all(value, 'ctx', split_axis=0, concat_axis=0, tiled=True)  13.7 us
  transfers between devices with their start and end apart: 47, of which 26 were waited for; matrix products, arithmetic and copies ran while one was open for 6% of the time, Pallas kernels for 17%

commit v1 on v0

--- a/solution.py
+++ b/solution.py
@@ -33,9 +33,11 @@
 
 
 def ring_order(count):
-    if count % 2:
-        return list(range(count))
     return list(range(0, count, 2)) + list(range(count - 1, 0, -2))
+
+
+def ring_place(index, count):
+    return jnp.where(index % 2 == 0, index // 2, count - 1 - index // 2)
 
 
 def params(limit=ALL_VMEM):
@@ -79,22 +81,28 @@
     return jnp.where(lane % HEAD < HEAD // 2, ahead, behind)
 
 
-def fetches(starts, pieces, whole, sems, sizes):
+def row_start(ids_ref, hop, rows):
+    return pl.multiple_of((ids_ref[0] ^ hop) * rows, 16)
+
+
+def fetches(ids_ref, pieces, whole, sems, sizes, column=0):
     copies = []
     for index, (piece, size) in enumerate(zip(pieces, sizes)):
-        start = pl.multiple_of(starts[index], 16)
+        start = row_start(ids_ref, index, size)
         copies.append(
             pltpu.make_async_copy(
-                piece.at[pl.ds(0, size), :], whole.at[pl.ds(start, size), :], sems.at[index]
+                piece.at[pl.ds(0, size), pl.ds(column, whole.shape[1])],
+                whole.at[pl.ds(start, size), :],
+                sems.at[index],
             )
         )
     return copies
 
 
-def keys_kernel(starts_ref, x_ref, cos_ref, sin_ref, *rest, sizes, kvw):
+def keys_kernel(ids_ref, x_ref, cos_ref, sin_ref, *rest, sizes, kvw):
     pieces = rest[: len(sizes)]
     hidden_ref, kv_ref, one_ref, two_ref, whole, bands, sems, band_sems = rest[len(sizes) :]
-    copies = fetches(starts_ref, pieces, whole, sems, sizes)
+    copies = fetches(ids_ref, pieces, whole, sems, sizes)
     rows = sizes[0]
     for index, piece in enumerate(pieces):
         band = pltpu.make_async_copy(
@@ -115,8 +123,8 @@
         blank = jnp.zeros((8, width - rows), F32)
         first = jnp.concatenate([band[:, :rows], blank], axis=1)
         second = jnp.concatenate([band[:, rows : 2 * rows], blank], axis=1)
-        ones = ones + pltpu.roll(first, starts_ref[index], 1)
-        twos = twos + pltpu.roll(second, starts_ref[index], 1)
+        ones = ones + pltpu.roll(first, (ids_ref[0] ^ index) * rows, 1)
+        twos = twos + pltpu.roll(second, (ids_ref[0] ^ index) * rows, 1)
     one_ref[...] = ones[:1, :]
     two_ref[...] = twos[:1, :]
     hidden = (x * scale * ones[:1, :]).astype(BF16)
@@ -131,10 +139,10 @@
     kv_ref[:, kvw:] = pre[:, kvw:].astype(BF16)
 
 
-def queries_kernel(starts_ref, hidden_ref, cos_ref, sin_ref, *rest, sizes):
+def queries_kernel(ids_ref, hidden_ref, cos_ref, sin_ref, *rest, sizes):
     pieces = rest[: len(sizes)]
     query_ref, whole, sems = rest[len(sizes) :]
-    copies = fetches(starts_ref, pieces, whole, sems, sizes)
+    copies = fetches(ids_ref, pieces, whole, sems, sizes)
     for copy in copies:
         copy.start()
     for copy in copies:
@@ -154,6 +162,7 @@
     gain_ref,
     *rest,
     sizes,
+    column,
     groups,
     per,
     blocks,
@@ -175,14 +184,13 @@
         sems,
     ) = rest[-13:]
     step = pl.program_id(0)
-    last = table_ref[blocks]
-    starts = [table_ref[blocks + 1 + index] for index in range(len(sizes))]
+    last = table_ref[1]
     count = q_ref.shape[0]
     kvw = groups * HEAD
 
     @pl.when(step == 0)
     def _():
-        for copy in fetches(starts, pieces, whole, sems, sizes):
+        for copy in fetches(table_ref, pieces, whole, sems, sizes, column):
             copy.start()
         turned = q_ref[...].T
         for group in range(groups):
@@ -233,7 +241,7 @@
         out_ref[...] = tall[...]
         attended = tall[...].astype(BF16).T
         attended_ref[...] = attended
-        for copy in fetches(starts, pieces, whole, sems, sizes):
+        for copy in fetches(table_ref, pieces, whole, sems, sizes, column):
             copy.wait()
         mid = x_ref[...].astype(F32) + nn(attended, whole[...])
         mid_ref[...] = mid
@@ -257,6 +265,7 @@
     sin_ref,
     *rest,
     sizes,
+    column,
     groups,
     per,
     blocks,
@@ -277,14 +286,13 @@
         sems,
     ) = rest[len(sizes) :]
     step = pl.program_id(0)
-    last = table_ref[blocks]
-    starts = [table_ref[blocks + 1 + index] for index in range(len(sizes))]
+    last = table_ref[1]
     count = kv_ref.shape[0]
     kvw = groups * HEAD
 
     @pl.when(step == 0)
     def _():
-        copies = fetches(starts, pieces, whole, sems, sizes)
+        copies = fetches(table_ref, pieces, whole, sems, sizes, column)
         for copy in copies:
             copy.start()
         mid = mid_ref[...]
@@ -362,7 +370,7 @@
             gq_ref[:, start : start + LANES] = turned.astype(BF16)
 
 
-def kv_back_kernel(starts_ref, grad_ref, cos_ref, sin_ref, hidden_ref, out_ref, *rest, kvw):
+def kv_back_kernel(ids_ref, grad_ref, cos_ref, sin_ref, hidden_ref, out_ref, *rest, kvw):
     outs, full = rest[:-1], rest[-1]
     for start in range(0, kvw, LANES):
         tile = grad_ref[:, start : start + LANES].astype(F32)
@@ -371,7 +379,7 @@
     out_ref[:, kvw:] = grad_ref[:, kvw:]
     full[...] = tn(hidden_ref[...], out_ref[...])
     for index, out in enumerate(outs):
-        start = pl.multiple_of(starts_ref[index], 8)
+        start = row_start(ids_ref, index, out.shape[0])
         out[...] = full[pl.ds(start, out.shape[0]), :].astype(BF16)
 
 
@@ -391,11 +399,11 @@
             row += rows
 
 
-def inputs_kernel(starts_ref, gq_ref, gkv_ref, x_ref, gain_ref, gmid_ref, *rest, sizes):
+def inputs_kernel(ids_ref, gq_ref, gkv_ref, x_ref, gain_ref, gmid_ref, *rest, sizes):
     hops = len(sizes)
     grad_ref, ggain_ref, whole_q, whole_kv, q_sems, kv_sems = rest[2 * hops :]
-    copies = fetches(starts_ref, rest[:hops], whole_q, q_sems, sizes)
-    copies += fetches(starts_ref, rest[hops : 2 * hops], whole_kv, kv_sems, sizes)
+    copies = fetches(ids_ref, rest[:hops], whole_q, q_sems, sizes)
+    copies += fetches(ids_ref, rest[hops : 2 * hops], whole_kv, kv_sems, sizes)
     for copy in copies:
         copy.start()
     for copy in copies:
@@ -410,13 +418,13 @@
     grad_ref[...] = grad.astype(BF16)
 
 
-def weight_grads_kernel(starts_ref, hidden_ref, query_ref, attended_ref, branch_ref, *rest):
+def weight_grads_kernel(ids_ref, hidden_ref, query_ref, attended_ref, branch_ref, *rest):
     outs, full = rest[:-1], rest[-1]
     hops = len(outs) // 2
     for index, (left, right) in enumerate(((hidden_ref, query_ref), (attended_ref, branch_ref))):
         full[...] = tn(left[...], right[...])
         for hop, out in enumerate(outs[index * hops : (index + 1) * hops]):
-            start = pl.multiple_of(starts_ref[hop], 8)
+            start = row_start(ids_ref, hop, out.shape[0])
             out[...] = full[pl.ds(start, out.shape[0]), :].astype(BF16)
 
 
@@ -434,7 +442,7 @@
 
 
 def feed_near_kernel(
-    starts_ref, own_gate_ref, own_up_ref, near_ref, far_ref, down_ref, *rest, half, lanes
+    ids_ref, own_gate_ref, own_up_ref, near_ref, far_ref, down_ref, *rest, half, lanes
 ):
     normed_refs, cot_refs = rest[:2], rest[2:4]
     gate_mat_out, up_mat_out, act_out, gate_out, up_out, back_out = rest[4:10]
@@ -449,26 +457,35 @@
         mats.append(
             pltpu.make_async_copy(
                 source,
-                target.at[pl.ds(pl.multiple_of(row, 16), height), pl.ds(column % own, breadth)],
+                target.at[pl.ds(row, height), pl.ds(column % own, breadth)],
                 mat_sems.at[len(mats)],
             )
         )
 
-    mine = pl.ds(pl.multiple_of(starts_ref[4] * own, LANES), own)
+    mine = pl.ds(pl.multiple_of(ids_ref[0] * own, LANES), own)
     for index, ref in enumerate((own_gate_ref, own_up_ref)):
-        place(ref.at[:, mine], starts_ref[0], index * own, rows, own)
-        place(near_ref.at[:, pl.ds(index * own, own)], starts_ref[1], index * own, rows, own)
+        place(ref.at[:, mine], row_start(ids_ref, 0, rows), index * own, rows, own)
+        place(
+            near_ref.at[:, pl.ds(index * own, own)],
+            row_start(ids_ref, 1, rows),
+            index * own,
+            rows,
+            own,
+        )
     for spot in range(far_ref.shape[0]):
         for index in range(2):
             place(
                 far_ref.at[spot, pl.ds(index * half, half), :],
-                starts_ref[2 + index] + (spot % 2) * half,
+                pl.multiple_of(row_start(ids_ref, 2 + index, rows) + (spot % 2) * half, 16),
                 (spot // 2) * lanes,
                 half,
                 lanes,
             )
+    count = tokens.shape[0] // 2
     loads = [
-        pltpu.make_async_copy(ref, target.at[index], token_sems.at[slot, index])
+        pltpu.make_async_copy(
+            ref, target.at[pl.ds(index * count, count), :], token_sems.at[slot, index]
+        )
         for slot, (refs, target) in enumerate(((normed_refs, tokens), (cot_refs, cots)))
         for index, ref in enumerate(refs)
     ]
@@ -495,16 +512,12 @@
     for copy in loads:
         copy.wait()
 
-    def token_block(index, carry):
-        act[index], grad_gate[index], grad_up[index] = units(
-            tokens[index], cots[index], gate_mat[...], up_mat[...], down_mat[...]
-        )
-        back[index] = (
-            nt(grad_gate[index], gate_mat[...]) + nt(grad_up[index], up_mat[...])
-        ).astype(BF16)
-        return carry
-
-    lax.fori_loop(0, 2, token_block, 0)
+    act[...], grad_gate[...], grad_up[...] = units(
+        tokens[...], cots[...], gate_mat[...], up_mat[...], down_mat[...]
+    )
+    back[...] = (
+        nt(grad_gate[...], gate_mat[...]) + nt(grad_up[...], up_mat[...])
+    ).astype(BF16)
     for copy in outs[2:]:
         copy.start()
     for copy in outs:
@@ -512,7 +525,7 @@
 
 
 def feed_far_kernel(
-    starts_ref, gate_mat_ref, up_mat_ref, down_ref, act_in, gate_in, up_in, *rest, per_shard
+    ids_ref, gate_mat_ref, up_mat_ref, down_ref, act_in, gate_in, up_in, *rest, per_shard
 ):
     hops = 4
     normed_refs, cot_refs = rest[:hops], rest[hops : 2 * hops]
@@ -522,7 +535,7 @@
     ]
     mat_sems, token_sems, cot_sems, unit_sems, out_sems, tile_sems = rest[2 * hops + 14 :]
     width, own = gate_mat.shape
-    count = tokens.shape[1]
+    count = tokens.shape[0] // hops
     places, height, tile = tiles.shape
     rows = height // 3
     mats = [
@@ -532,7 +545,7 @@
         )
     ]
     token_copies = [
-        pltpu.make_async_copy(ref, tokens.at[index], token_sems.at[index])
+        pltpu.make_async_copy(ref, tokens.at[pl.ds(index * count, count), :], token_sems.at[index])
         for index, ref in enumerate(normed_refs)
     ]
     cot_copies = [
@@ -540,12 +553,10 @@
         for index, ref in enumerate(cot_refs)
     ]
     unit_copies = [
-        pltpu.make_async_copy(source.at[index], target.at[pl.ds(index * count, count), :],
-                              unit_sems.at[slot, index])
+        pltpu.make_async_copy(source, target.at[pl.ds(0, 2 * count), :], unit_sems.at[slot])
         for slot, (source, target) in enumerate(
             ((act_in, act), (gate_in, grad_gate), (up_in, grad_up))
         )
-        for index in range(2)
     ]
     for copy in mats + token_copies[2:] + cot_copies[2:]:
         copy.start()
@@ -553,22 +564,15 @@
         copy.start()
     for copy in token_copies[:2]:
         copy.wait()
-    for index in range(2):
-        turned[:, index * count : (index + 1) * count] = tokens[index].T
+    turned[:, : 2 * count] = tokens[: 2 * count, :].T
     for copy in mats + token_copies[2:] + cot_copies[2:]:
         copy.wait()
 
-    def token_block(index, carry):
-        span = pl.ds(pl.multiple_of(index * count, count), count)
-        normed = tokens[index]
-        act[span, :], grad_gate[span, :], grad_up[span, :] = units(
-            normed, cots[span, :], gate_mat[...], up_mat[...], down_mat[...]
-        )
-        turned[:, span] = normed.T
-        return carry
-
-    lax.fori_loop(2, hops, token_block, 0)
     late = pl.ds(2 * count, 2 * count)
+    act[late, :], grad_gate[late, :], grad_up[late, :] = units(
+        tokens[late, :], cots[late, :], gate_mat[...], up_mat[...], down_mat[...]
+    )
+    turned[:, 2 * count :] = tokens[late, :].T
     outs = [
         pltpu.make_async_copy(source.at[late, :], target, out_sems.at[index])
         for index, (source, target) in enumerate(
@@ -589,35 +593,39 @@
         )
 
     def row_block(index, carry):
-        left = turned[pl.ds(pl.multiple_of(index * rows, 16), rows), :]
-        spot = lax.rem(index + starts_ref[hops], hops) * per_shard
+        left = turned[pl.ds(pl.multiple_of(index * 2 * rows, 16), 2 * rows), :]
+        spots = [
+            lax.rem(2 * index + block + ids_ref[0], hops) * per_shard for block in range(2)
+        ]
         for slot, ref in ((0, grad_gate), (1, grad_up)):
             grad = nn(left, ref[...])
+            for block, spot in enumerate(spots):
+                for part in range(per_shard):
+                    tiles[spot + part, slot * rows : (slot + 1) * rows, :] = grad[
+                        block * rows : (block + 1) * rows, part * tile : (part + 1) * tile
+                    ].astype(BF16)
+        for spot in spots:
             for part in range(per_shard):
-                tiles[spot + part, slot * rows : (slot + 1) * rows, :] = grad[
-                    :, part * tile : (part + 1) * tile
-                ].astype(BF16)
-        for part in range(per_shard):
-            tile_copy(spot + part, 0).start()
+                tile_copy(spot + part, 0).start()
         return carry
 
-    lax.fori_loop(0, hops, row_block, 0)
+    lax.fori_loop(0, hops // 2, row_block, 0)
     band = own // places
     turned[:own, :] = act[...].T
 
     def down_block(index, carry):
-        left = turned[pl.ds(pl.multiple_of(index * 2 * band, 16), 2 * band), :]
+        left = turned[pl.ds(pl.multiple_of(index * 4 * band, 16), 4 * band), :]
         grad = nn(left, cots[...])
-        for part in range(2):
+        for part in range(4):
             for split in range(width // tile):
                 start = 2 * rows + split * band
-                tiles[2 * index + part, start : start + band, :] = grad[
+                tiles[4 * index + part, start : start + band, :] = grad[
                     part * band : (part + 1) * band, split * tile : (split + 1) * tile
                 ].astype(BF16)
-            tile_copy(2 * index + part, 1).start()
+            tile_copy(4 * index + part, 1).start()
         return carry
 
-    lax.fori_loop(0, places // 2, down_block, 0)
+    lax.fori_loop(0, places // 4, down_block, 0)
     for copy in outs:
         copy.wait()
     for spot in range(places):
@@ -635,7 +643,7 @@
 
 
 def widen_kernel(
-    shard_ref,
+    ids_ref,
     gate_up_ref,
     down_in_ref,
     mixed_ref,
@@ -649,16 +657,19 @@
     rows,
 ):
     step = pl.program_id(0)
-    tile = gate_ref.shape[1]
-    band = down_ref.shape[0]
+    several, _, tile = gate_up_ref.shape
+    band = down_ref.shape[0] // several
     share = mixed_ref.shape[1]
-    gate_ref[...] = gate_up_ref[0, :rows, :].astype(F32)
-    up_ref[...] = gate_up_ref[0, rows:, :].astype(F32)
-    for split in range(down_ref.shape[1] // tile):
-        down_ref[:, split * tile : (split + 1) * tile] = down_in_ref[
-            0, split * band : (split + 1) * band, :
-        ].astype(F32)
-    stack[pl.ds(pl.multiple_of(step * share, 8), share), :] = mixed_ref[0].astype(F32)
+    for part in range(several):
+        span = slice(part * tile, (part + 1) * tile)
+        gate_ref[:, span] = gate_up_ref[part, :rows, :].astype(F32)
+        up_ref[:, span] = gate_up_ref[part, rows:, :].astype(F32)
+        for split in range(down_ref.shape[1] // tile):
+            down_ref[part * band : (part + 1) * band, split * tile : (split + 1) * tile] = (
+                down_in_ref[part, split * band : (split + 1) * band, :].astype(F32)
+            )
+        start = pl.multiple_of((step * several + part) * share, 8)
+        stack[pl.ds(start, share), :] = mixed_ref[part].astype(F32)
 
     @pl.when(step == pl.num_programs(0) - 1)
     def _():
@@ -697,13 +708,12 @@
     blocks = n_ctx
     per_shard = n_ctx // n_shard
     tile = ff_own // per_shard
-    assert count == BLOCK and n_shard == 4 and ff_own * n_shard == ff
+    assert count == BLOCK and n_shard == 4 and n_ctx % 2 == 0 and ff_own * n_shard == ff
     aligned = tile % LANES == 0
     order = ring_order(n_ctx)
     places = [order.index(index) for index in range(n_ctx)]
     shard = lax.axis_index("shard")
     ctx = lax.axis_index("ctx")
-    shard_arr = shard.astype(jnp.int32)[None]
 
     def after(value, done):
         return lax.optimization_barrier((value, done))[0]
@@ -753,13 +763,13 @@
     kv_own = jnp.concatenate([jnp.concatenate([w_key, w_value], axis=1), gain_rows], axis=0)
     far = hop(kv_own, 2)
     kv_weights = [kv_own, hop(kv_own, 1), far, hop(far, 1)]
-    starts = jnp.stack(
-        [(shard ^ k) * rows for k in range(n_shard)] + [shard]
-    ).astype(jnp.int32)
+    ids = jnp.stack([shard, ctx]).astype(jnp.int32)
     sizes = (rows,) * n_shard
-    table = jnp.concatenate(
-        [jnp.array(places, jnp.int32), ctx.astype(jnp.int32)[None], starts]
-    )
+
+
+    half = rows // 2
+    lanes = 4 * ff_own // n_ctx
+    spot = ring_place(ctx, n_ctx)
 
     def columns(peer):
         start = peer * ff_own
@@ -771,31 +781,28 @@
             axis=1,
         )
 
-    half = rows // 2
-    lanes = 4 * ff_own // n_ctx
-    spot = jnp.array(places, jnp.int32)[ctx]
-    chosen = []
-    for distance in (2, 3):
-        peer = (shard ^ distance) * ff_own
-        column = peer + lax.rem(spot // 2 * lanes, ff_own)
+    def far_columns(peer):
+        column = peer * ff_own + lax.rem(spot // 2 * lanes, ff_own)
         cuts = [
             lax.dynamic_slice(mat, (spot % 2 * half, column), (half, lanes))
             for mat in (w_gate, w_up)
         ]
-        chosen.append(jnp.where(spot // 2 * lanes < ff_own, cuts[0], cuts[1]))
+        return jnp.where(spot // 2 * lanes < ff_own, cuts[0], cuts[1])
+
     near_columns = columns(shard ^ 1)
-    cosine, sine, near_columns, table, starts, *chosen = lax.optimization_barrier(
-        (cosine, sine, near_columns, table, starts, *chosen)
-    )
-    q_weights = gather(w_query, far)
-    out_weights = gather(w_out, q_weights[2])
-
+    far_cut = jnp.concatenate([far_columns(shard ^ distance) for distance in (2, 3)], axis=0)
+    query_own = jnp.concatenate([w_query, far_cut], axis=1)
+    cosine, sine, ids, near_columns, query_own = lax.optimization_barrier(
+        (cosine, sine, ids, near_columns, query_own)
+    )
+    query_weights = gather(query_own, far)
+    out_far = hop(after(w_out, query_weights[2]), 2)
     fetch_sems = pltpu.SemaphoreType.DMA((n_shard,))
     hidden, kv, gain_one, gain_two = call_once(
         functools.partial(keys_kernel, sizes=sizes, kvw=kvw),
         [((count, width), BF16), ((count, 2 * kvw), BF16), ((1, width), F32), ((1, width), F32)],
         [x, cosine, sine],
-        held=[starts],
+        held=[ids],
         moved=kv_weights,
         scratch=[
             pltpu.VMEM((width, 2 * kvw), BF16),
@@ -813,26 +820,25 @@
         functools.partial(queries_kernel, sizes=sizes),
         [((count, qw), BF16)],
         [hidden, cosine, sine],
-        held=[starts],
-        moved=q_weights,
+        held=[ids],
+        moved=query_weights,
         scratch=[pltpu.VMEM((width, qw), BF16), fetch_sems],
         flops=2 * count * width * qw,
         name="queries",
     )
-
-    far_tiles = [
-        hop(after(part, (out_weights[2], queries)), k) for part, k in zip(chosen, (2, 3))
-    ]
-    far_tile = jnp.concatenate(far_tiles, axis=0)
+    out_weights = [w_out, hop(w_out, 1), out_far, hop(after(out_far, queries), 1)]
+    far_tile = jnp.concatenate(
+        [query_weights[2][:half, qw:], query_weights[3][half:, qw:]], axis=0
+    )
     far_rows = collect(after(far_tile, kv)[None])
     near_part = hop(near_columns, 1)
     cot_near = hop(cot, 1)
-    cot_far = hop(after(cot, far_tile), 2)
-
-    shared = dict(sizes=sizes, groups=groups, per=per, blocks=blocks)
+    cot_far = hop(after(cot, (out_weights[2], queries)), 2)
+
+    shared = dict(sizes=sizes, column=0, groups=groups, per=per, blocks=blocks)
     fixed = lambda *shape: pl.BlockSpec(shape, lambda step, table: (0,) * len(shape))
     kv_spec = pl.BlockSpec(
-        (count, 2 * kvw), lambda step, table: (table[jnp.minimum(step, table[blocks])], 0)
+        (count, 2 * kvw), lambda step, table: (ring_place(jnp.minimum(step, table[1]), blocks), 0)
     )
     once = lambda *shape: block(shape)
     weight_specs = [HBM_SPEC] * len(sizes)
@@ -875,7 +881,7 @@
             4 * count * count * blocks * qw, 12e6, count * count * blocks * groups * per
         ),
         name="attend",
-    )(table, queries, all_kv, x, gain_two, *out_weights)
+    )(ids, queries, all_kv, x, gain_two, *out_weights)
 
     normed_far = hop(normed, 2)
     normed_near = hop(normed, 1)
@@ -883,9 +889,9 @@
     far_rows = after(far_rows, normed)
     all_count = n_shard * count
     if aligned:
-        two = ((2, count, ff_own), BF16)
+        two = ((2 * count, ff_own), BF16)
         mats = [((width, ff_own), BF16)] * 2
-        pair = (2, count, width)
+        pair = (2 * count, width)
         gate_mat, up_mat, *near_units, back = pl.pallas_call(
             functools.partial(feed_near_kernel, half=half, lanes=lanes),
             out_shape=tuple(
@@ -911,7 +917,7 @@
             cost_estimate=cost(10 * 2 * count * width * ff_own, 12e6),
             name="feed_near",
         )(
-            starts,
+            ids,
             w_gate,
             w_up,
             near_part,
@@ -938,7 +944,7 @@
                 pltpu.VMEM((width, ff_own), BF16),
                 pltpu.VMEM((width, ff_own), BF16),
                 pltpu.VMEM((ff_own, width), BF16),
-                pltpu.VMEM((n_shard, count, width), BF16),
+                pltpu.VMEM((all_count, width), BF16),
                 pltpu.VMEM((all_count, width), BF16),
                 pltpu.VMEM((width, all_count), BF16),
                 pltpu.VMEM((all_count, ff_own), BF16),
@@ -948,7 +954,7 @@
                 pltpu.SemaphoreType.DMA((3,)),
                 pltpu.SemaphoreType.DMA((n_shard,)),
                 pltpu.SemaphoreType.DMA((n_shard,)),
-                pltpu.SemaphoreType.DMA((3, 2)),
+                pltpu.SemaphoreType.DMA((3,)),
                 pltpu.SemaphoreType.DMA((3,)),
                 pltpu.SemaphoreType.DMA((2, n_ctx)),
             ],
@@ -956,10 +962,10 @@
             cost_estimate=cost(9 * all_count * width * ff_own, 25e6),
             name="feed_far",
         )(
-            starts, gate_mat, up_mat, w_down, *near_units, *normed_pieces, *cot_pieces
-        )
-        to_own, to_near = back[0], back[1]
-        act_parts = [near_units[0].reshape(2 * count, ff_own), far_units[0]]
+            ids, gate_mat, up_mat, w_down, *near_units, *normed_pieces, *cot_pieces
+        )
+        to_own, to_near = back[:count], back[count:]
+        act_parts = [near_units[0], far_units[0]]
         grad_gate_far, grad_up_far = far_units[1:]
     else:
         normed_pieces = [normed, normed_near, normed_far, hop(normed_far, 1)]
@@ -968,7 +974,10 @@
         tiles_of = tiles_of.transpose(2, 1, 3, 0, 4).reshape(2, rows, 2 * ff_own)
         gate_mat = jnp.zeros((width, ff_own), BF16)
         up_mat = jnp.zeros((width, ff_own), BF16)
-        for part, start in zip((columns(shard), near_part, tiles_of[0], tiles_of[1]), starts):
+        for part, start in zip(
+            (columns(shard), near_part, tiles_of[0], tiles_of[1]),
+            [(shard ^ k) * rows for k in range(n_shard)],
+        ):
             gate_mat = lax.dynamic_update_slice_in_dim(gate_mat, part[:, :ff_own], start, 0)
             up_mat = lax.dynamic_update_slice_in_dim(up_mat, part[:, ff_own:], start, 0)
         all_cot = jnp.concatenate(cot_pieces, axis=0)
@@ -1026,7 +1035,9 @@
     part_out = [part[k * count : (k + 1) * count] for part in part_out for k in range(2)]
     output = (mid + add(reduce(part_out))).astype(BF16)[None]
 
-    place_spec = pl.BlockSpec((count, 2 * kvw), lambda step, table: (table[step], 0))
+    place_spec = pl.BlockSpec(
+        (count, 2 * kvw), lambda step, table: (ring_place(step, blocks), 0)
+    )
     grad_query, grad_kv, branch, grad_mid, gain_two_part = pl.pallas_call(
         functools.partial(attend_back_kernel, **shared),
         out_shape=(
@@ -1077,7 +1088,7 @@
         ),
         name="attend_back",
     )(
-        table,
+        ids,
         all_kv,
         q_cols,
         out_tall,
@@ -1108,7 +1119,7 @@
         weight_grads_kernel,
         [((rows, qw), BF16)] * n_shard + [((rows, width), BF16)] * n_shard,
         [hidden, grad_query, attended, branch],
-        held=[starts],
+        held=[ids],
         scratch=[pltpu.VMEM((width, qw), F32)],
         flops=4 * count * width * qw,
         limit=ALL_VMEM,
@@ -1123,14 +1134,15 @@
         functools.partial(kv_back_kernel, kvw=kvw),
         [((count, 2 * kvw), BF16)] + [((rows, 2 * kvw), BF16)] * n_shard,
         [own_kv, cosine, sine, hidden],
-        held=[starts],
+        held=[ids],
         scratch=[pltpu.VMEM((width, 2 * kvw), F32)],
         flops=4 * count * width * kvw,
         name="kv_back",
     )
     sum_kv = stack(reduce(kv_blocks), LANES, "stack_kv").reshape(n_ctx, -1, LANES)
-    shares = jnp.concatenate([gate_up_sum, down_sum, mixed_sum])
-    gathered = collect(after(shares, sum_kv)[None])
+    shares = jnp.concatenate([gate_up_sum, down_sum, jnp.zeros_like(mixed_sum)])
+    shares = lax.dynamic_update_slice_in_dim(after(shares, sum_kv), mixed_sum, 3 * rows, 0)
+    gathered = collect(shares[None])
 
     def exchange(value):
         return lax.all_to_all(value, "ctx", split_axis=0, concat_axis=0, tiled=True)
@@ -1145,8 +1157,8 @@
         functools.partial(inputs_kernel, sizes=sizes),
         [((count, width), BF16), ((1, width), F32)],
         [grad_query, grad_kv_pre, x, gain_one, grad_mid],
-        held=[starts],
-        moved=[*q_weights, *kv_weights],
+        held=[ids],
+        moved=[*query_weights, *kv_weights],
         scratch=[
             pltpu.VMEM((width, qw), BF16),
             pltpu.VMEM((width, 2 * kvw), BF16),
@@ -1166,7 +1178,7 @@
 
     if aligned:
         share = mixed_sum.shape[0]
-        rolled = lambda step, where: (lax.rem(step + where[0] * per_shard, n_ctx), 0, 0)
+        rolled = lambda step, where: (lax.rem(step + where[0], n_shard), 0, 0)
         band = ff_own // n_ctx
         grad_w_gate, grad_w_up, grad_w_down, grad_w_query, grad_w_out = pl.pallas_call(
             functools.partial(widen_kernel, rows=rows),
@@ -1179,16 +1191,19 @@
             ),
             grid_spec=pltpu.PrefetchScalarGridSpec(
                 num_scalar_prefetch=1,
-                grid=(n_ctx,),
+                grid=(n_shard,),
                 in_specs=[
-                    pl.BlockSpec((1, 2 * rows, tile), rolled),
-                    pl.BlockSpec((1, rows, tile), lambda step, where: (step, 2, 0)),
-                    pl.BlockSpec((1, share, tile), lambda step, where: (step, 3 * rows // share, 0)),
+                    pl.BlockSpec((per_shard, 2 * rows, tile), rolled),
+                    pl.BlockSpec((per_shard, rows, tile), lambda step, where: (step, 2, 0)),
+                    pl.BlockSpec(
+                        (per_shard, share, tile),
+                        lambda step, where: (step, 3 * rows // share, 0),
+                    ),
                 ],
                 out_specs=[
-                    pl.BlockSpec((rows, tile), lambda step, where: (0, step)),
-                    pl.BlockSpec((rows, tile), lambda step, where: (0, step)),
-                    pl.BlockSpec((band, width), lambda step, where: (step, 0)),
+                    pl.BlockSpec((rows, ff_own), lambda step, where: (0, step)),
+                    pl.BlockSpec((rows, ff_own), lambda step, where: (0, step)),
+                    pl.BlockSpec((per_shard * band, width), lambda step, where: (step, 0)),
                     pl.BlockSpec((rows, qw), lambda step, where: (0, 0)),
                     pl.BlockSpec((rows, width), lambda step, where: (0, 0)),
                 ],
@@ -1197,7 +1212,7 @@
             compiler_params=params(),
             cost_estimate=cost(1e6, 20e6),
             name="widen",
-        )(shard_arr, gathered, gathered, gathered)
+        )(ids, gathered, gathered, gathered)
     else:
 
         def untile(part):

time: 381 us -> 384 us (level); the launches traced: 380 us -> 377 us
    unnamed x85 -> x80, local copies, waits for them, and re-layouts: 9.35 us -> 11.2 us
    ppermute x35 -> x33, starting transfers between devices: 31 us -> 29.4 us  [hop(): return lax.ppermute(value, 'shard', pairs)]
    ppermute x35 -> x33, waiting for transfers between devices: 99.8 us -> 98.7 us  [hop(): return lax.ppermute(value, 'shard', pairs)]
  transfers between devices with their start and end apart: 47 -> 45, of which waited for: 26 -> 24; matrix products, arithmetic and copies ran while one was open for 6% -> 6% of each run, Pallas kernels for 17% -> 17%
where the time goes in v1:
time: 384 us; the launch traced here: 377 us
  waiting for transfers between devices  184 us (48%)
  Pallas kernels  94.3 us (25%)
  starting transfers between devices  44.9 us (12%)
  local copies, waits for them, and re-layouts  20.4 us (5%)
  between operations  15.1 us (4%)
  other arithmetic  13.5 us (4%)
  matrix products  4.25 us (1%)
    ppermute x33, waiting for transfers between devices, hop(): return lax.ppermute(value, 'shard', pairs)  98.7 us
    all_gather x3, waiting for transfers between devices, collect(): lax.all_gather(value, 'ctx', axis=0, axis_index_groups=[order], tiled=True)  40.2 us
    ppermute x33, starting transfers between devices, hop(): return lax.ppermute(value, 'shard', pairs)  29.4 us
    pallas_call x8, Pallas kernels, call_once(): pl.pallas_call(kernel, out_shape=tuple((jax.ShapeDtypeStruct(shape, dtype...  25.7 us
    pallas_call x1, Pallas kernels, on_device(): pl.pallas_call(functools.partial(attend_back_kernel, **shared), out_shape...  19.5 us
    reduce_scatter x2, waiting for transfers between devices, scatter(): lax.psum_scatter(value, 'ctx', scatter_dimension=0, axis_index_groups=[or...  16.8 us
    pallas_call x1, Pallas kernels, on_device(): pl.pallas_call(functools.partial(feed_far_kernel, per_shard=per_shard), o...  16.5 us
    all_to_all x2, waiting for transfers between devices, exchange(): return lax.all_to_all(value, 'ctx', split_axis=0, concat_axis=0, tiled=True)  13.7 us
  transfers between devices with their start and end apart: 45, of which 24 were waited for; matrix products, arithmetic and copies ran while one was open for 6% of the time, Pallas kernels for 17%

profile of v1, /device:TPU:9, one launch (start us, length us, event | category | flops | bytes accessed | tf_op | source)
XLA Modules:
  0.0 376.7 jit_solution(5730939872405113681)
XLA Ops:
  8.0 1.1 fusion.2.rest_0_.rest_4_
  9.1 1.3 collective-permute-start.1
  11.4 1.4 dynamic-slice_select_fusion.1
  13.4 1.3 constant_dynamic-slice_fusion
  15.7 5.0 %collective-permute-done.1.rest_2_.rest_6_ = bf16[304,768]{1,0:T(8,128)(2,1)S(1)} collective-permute-done((bf16[304,768]{1,0:T(8,128)(2,1)S(1)}, bf16[304,768]{1,0:T(8,128)(2,1)S(1)}, u32[]{:S(2)}, u32[]{:S(2)}) %collective-permute-start.1) | collective-permute-done | bytes 466976 | tf_op jit(solution)/shard_map/ppermute | solution.py:723
  20.7 1.5 collective-permute-start.2
  22.3 1.3 fusion.3
  24.6 4.3 %keys.1 = (bf16[256,1152]{1,0:T(8,128)(2,1)}, bf16[256,768]{1,0:T(8,128)(2,1)}, f32[1,1152]{1,0:T(1,128)}, f32[1,1152]{1,0:T(1,128)}) custom-call(s32[2]{0:T(128)} %pad_add_fusion.ids_ref.table_ref, bf16[256,1152]{1,0:T(8,128)(2,1)} %bitcast.29, f32[256,128]{1,0:T(8,128)} %get-tuple-element.90.cos_ref, f32[256,128]{1,0:T(8,128)} %get-tuple-element.91.sin_ref, ...), custom_call_target="tpu_custom_call" | custom-call | flops 452984832 | bytes 4987648 | tf_op jit(solution)/shard_map/keys/pallas_call | solution.py:62
  29.0 1.3 collective-permute-start.4
  30.3 19.8 %collective-permute-done.4.rest_2_ = bf16[288,1536]{1,0:T(8,128)(2,1)S(1)} collective-permute-done((bf16[288,1536]{1,0:T(8,128)(2,1)S(1)}, bf16[288,1536]{1,0:T(8,128)(2,1)S(1)}, u32[]{:S(2)}, u32[]{:S(2)}) %collective-permute-start.4) | collective-permute-done | bytes 884768 | tf_op jit(solution)/shard_map/ppermute | solution.py:723
  50.1 1.0 collective-permute-start.5
  51.1 2.0 collective-permute-done.5.rest_3_
  54.4 1.2 collective-permute-start.7
  58.3 1.1 copy-done.16
  59.4 2.0 queries.1.q_ref
  62.1 8.9 %collective-permute-done.7.rest_2_ = bf16[288,1152]{1,0:T(8,128)(2,1)S(1)} collective-permute-done((bf16[288,1152]{1,0:T(8,128)(2,1)}, bf16[288,1152]{1,0:T(8,128)(2,1)S(1)}, u32[]{:S(2)}, u32[]{:S(2)}) %collective-permute-start.7) | collective-permute-done | bytes 663584 | tf_op jit(solution)/shard_map/ppermute | solution.py:723
  73.3 1.2 collective-permute-start.13
  74.5 1.1 collective-permute-done.8.rest_3_
  75.6 12.6 %attend.1 = (f32[1152,256]{1,0:T(8,128)}, bf16[256,1152]{1,0:T(8,128)(2,1)}, f32[8,768]{1,0:T(8,128)}, f32[256,1152]{1,0:T(8,128)}, bf16[256,1152]{1,0:T(8,128)(2,1)}, /*index=5*/bf16[6,64,768]{2,1,0:T(8,128)(2,1)}) custom-call(s32[2]{0:T(128)} %pad_add_fusion.ids_ref.table_ref, bf16[256,1152]{1,0:T(8,128)(2,1)} %copy-done.18, ...), custom_call_target="tpu_custom_call" | custom-call | flops 2415919104 | bytes 12000000 | tf_op jit(solution)/shard_map/attend/pallas_call | solution.py:846
  88.7 1.2 collective-permute-start.12
  89.9 8.9 %all-gather.9.cloned.1.call-done = bf16[2304,384]{1,0:T(8,128)(2,1)} async-done(((bf16[288,384]{1,0:T(8,128)(2,1)}), bf16[2304,384]{1,0:T(8,128)(2,1)}) %all-gather.9.cloned.1.call-update) | async-done | bytes 1769488 | tf_op jit(solution)/shard_map/all_gather | solution.py:752
  98.8 11.0 %feed_near.1 = (bf16[1152,768]{1,0:T(8,128)(2,1)}, bf16[1152,768]{1,0:T(8,128)(2,1)}, bf16[512,768]{1,0:T(8,128)(2,1)}, bf16[512,768]{1,0:T(8,128)(2,1)}, bf16[5...) custom-call(s32[2]{0:T(128)} %pad_add_fusion.ids_ref.table_ref, bf16[288,3072]{1,0:T(8,128)(2,1)} %own_gate_ref.1, ...), custom_call_target="tpu_custom_call" | custom-call | flops 4529848320 | bytes 12000000 | tf_op jit(solution)/shard_map/feed_near/pallas_call | solution.py:895
  109.9 4.5 %collective-permute-start.14 = (bf16[256,1152]{1,0:T(8,128)(2,1)}, bf16[256,1152]{1,0:T(8,128)(2,1)}, u32[]{:S(2)}, u32[]{:S(2)}) collective-permute-start(bf16[256,1152]{1,0:T(8,128)(2,1)} %collective-permute-done.12.rest_2_), channel_id=1, source_target_pairs={{0,1},{1,0},{2,3},{3,2},{4,5},{5,4},{6,7},{7,6},{8,9},{9,8},{10,11... | collective-permute-start | bytes 1769480 | tf_op jit(solution)/shard_map/ppermute | solution.py:723
  114.5 1.9 collective-permute-done.14.rest_3_
  117.2 16.5 %feed_far.1 = (bf16[8,864,384]{2,1,0:T(8,128)(2,1)}, bf16[512,768]{1,0:T(8,128)(2,1)}, bf16[512,768]{1,0:T(8,128)(2,1)}, bf16[512,768]{1,0:T(8,128)(2,1)}) custom-call(s32[2]{0:T(128)} %pad_add_fusion.ids_ref.table_ref, bf16[1152,768]{1,0:T(8,128)(2,1)} %get-tuple-element.105.gate_mat_ref, bf16[1152,768]{1,0:T(8,128)(2,1)} %get-tuple-element.106.up_mat_ref, ...), custom_call_target="tpu_custom_call" | custom-call | flops 8153726976 | bytes 25000000 | tf_op jit(solution)/shard_map/feed_far/pallas_call | solution.py:935
  134.0 5.6 %normed_back.1 = (bf16[256,1152]{1,0:T(8,128)(2,1)}, bf16[256,1152]{1,0:T(8,128)(2,1)}) custom-call(bf16[512,768]{1,0:T(8,128)(2,1)} %get-tuple-element.114.gate_ref, bf16[512,768]{1,0:T(8,128)(2,1)} %get-tuple-element.115.up_ref, bf16[1152,768]{1,0:T(8,128)(2,1)} %get-tuple-element.105.gate_mat_ref, bf16[1152,768]{1,0:T(8,128)(2,1)} %get-tuple-element.106.up_mat_ref), custom_call_target="tpu_custom_call" | custom-call | flops 1811939328 | bytes 5179648 | tf_op jit(solution)/shard_map/normed_back/pallas_call | solution.py:62
  140.0 2.1 fusion.8
  142.5 1.2 collective-permute-start.17
  144.2 13.1 %collective-permute-done.17.gn_far_ref = bf16[256,1152]{1,0:T(8,128)(2,1)S(1)} collective-permute-done((bf16[256,1152]{1,0:T(8,128)(2,1)S(1)}, bf16[256,1152]{1,0:T(8,128)(2,1)S(1)}, u32[]{:S(2)}, u32[]{:S(2)}) %collective-permute-start.17) | collective-permute-done | bytes 589856 | tf_op jit(solution)/shard_map/ppermute | solution.py:723
  158.0 19.5 %attend_back.1 = (bf16[256,1152]{1,0:T(8,128)(2,1)}, bf16[2048,768]{1,0:T(8,128)(2,1)}, bf16[256,1152]{1,0:T(8,128)(2,1)}, f32[256,1152]{1,0:T(8,128)}, f32[1,1152]{1,0:T(1,128)}) custom-call(s32[2]{0:T(128)} %pad_add_fusion.ids_ref.table_ref, bf16[2048,768]{1,0:T(8,128)(2,1)} %all-gather.5.cloned.1.call-done.kv_ref, ...), custom_call_target="tpu_custom_call" | custom-call | flops 6039797760 | bytes 14000000 | tf_op jit(solution)/shard_map/attend_back/pallas_call | solution.py:1041
  177.6 16.8 %reduce-scatter.7.cloned.1.call-done = bf16[1,864,384]{2,1,0:T(8,128)(2,1)} async-done(((bf16[8,864,384]{2,1,0:T(8,128)(2,1)}), bf16[1,864,384]{2,1,0:T(8,128)(2,1)}) %reduce-scatter.7.cloned.1.call-update) | async-done | bytes 663568 | tf_op jit(solution)/shard_map/reduce_scatter | solution.py:747
  194.4 1.6 slice_bitcast_fusion.1
  196.1 5.3 %weight_grads.1 = (bf16[288,1152]{1,0:T(8,128)(2,1)}, bf16[288,1152]{1,0:T(8,128)(2,1)}, bf16[288,1152]{1,0:T(8,128)(2,1)}, bf16[288,1152]{1,0:T(8,128)(2,1)}, b...) custom-call(s32[2]{0:T(128)} %pad_add_fusion.ids_ref.table_ref, ...), custom_call_target="tpu_custom_call" | custom-call | flops 1358954496 | bytes 9308416 | tf_op jit(solution)/shard_map/weight_grads/pallas_call | solution.py:62
  202.6 1.4 collective-permute-done.35
  204.0 1.4 add_convert_fusion
  205.4 1.3 collective-permute-start.36
  207.1 14.5 %collective-permute-done.36.refs_5_ = bf16[288,1152]{1,0:T(8,128)(2,1)S(1)} collective-permute-done((bf16[288,1152]{1,0:T(8,128)(2,1)S(1)}, bf16[288,1152]{1,0:T(8,128)(2,1)S(1)}, u32[]{:S(2)}, u32[]{:S(2)}) %collective-permute-start.36) | collective-permute-done | bytes 663584 | tf_op jit(solution)/shard_map/ppermute | solution.py:723
  221.6 14.1 %collective-permute-done.33.refs_2_ = bf16[288,1152]{1,0:T(8,128)(2,1)S(1)} collective-permute-done((bf16[288,1152]{1,0:T(8,128)(2,1)S(1)}, bf16[288,1152]{1,0:T(8,128)(2,1)S(1)}, u32[]{:S(2)}, u32[]{:S(2)}) %collective-permute-start.33) | collective-permute-done | bytes 663584 | tf_op jit(solution)/shard_map/ppermute | solution.py:723
  235.8 1.6 stack_mixed.1
  239.5 1.1 copy-done.17
  240.5 1.0 copy-done.25
  241.5 1.6 kv_back.1
  243.1 1.3 collective-permute-start.29
  244.5 3.1 collective-permute-start.27
  248.2 8.0 %collective-permute-done.27 = bf16[576,384]{1,0:T(8,128)(2,1)S(1)} collective-permute-done((bf16[576,384]{1,0:T(8,128)(2,1)S(1)}, bf16[576,384]{1,0:T(8,128)(2,1)S(1)}, u32[]{:S(2)}, u32[]{:S(2)}) %collective-permute-start.27) | collective-permute-done | bytes 442400 | tf_op jit(solution)/shard_map/ppermute | solution.py:1020
  256.1 1.1 maximum_maximum_fusion.1
  257.2 5.8 %collective-permute-done.30.refs_2_ = bf16[288,768]{1,0:T(8,128)(2,1)S(1)} collective-permute-done((bf16[288,768]{1,0:T(8,128)(2,1)S(1)}, bf16[288,768]{1,0:T(8,128)(2,1)S(1)}, u32[]{:S(2)}, u32[]{:S(2)}) %collective-permute-start.30) | collective-permute-done | bytes 442400 | tf_op jit(solution)/shard_map/ppermute | solution.py:723
  263.9 1.8 reduce-scatter.11.cloned.1.call-done
  265.8 1.6 constant_dynamic-update-slice_fusion
  267.4 3.0 convolution_convert_fusion
  270.6 4.2 %collective-permute-start.19 = (bf16[256,1152]{1,0:T(8,128)(2,1)S(1)}, bf16[256,1152]{1,0:T(8,128)(2,1)S(1)}, u32[]{:S(2)}, u32[]{:S(2)}) collective-permute-start(bf16[256,1152]{1,0:T(8,128)(2,1)S(1)} %slice.69), channel_id=1, source_target_pairs={{0,1},{1,0},{2,3},{3,2},{4,5},{5,4},{6,7},{7,6},{8,9},{9,8},{10,11... | collective-permute-start | bytes 1769480 | tf_op jit(solution)/shard_map/ppermute | solution.py:723
  274.8 1.2 convolution_convert_fusion.1
  277.9 4.4 %grad_inputs.1 = (bf16[256,1152]{1,0:T(8,128)(2,1)}, f32[1,1152]{1,0:T(1,128)S(1)}) custom-call(s32[2]{0:T(128)S(1)} %copy-done.23, bf16[256,1152]{1,0:T(8,128)(2,1)S(1)} %copy-done.19, bf16[256,768]{1,0:T(8,128)(2,1)S(1)} %copy-done.21, bf16[256,1152]{1,0:T(8,128)(2,1)S(1)} %bitcast.31, f32[1,1152]{1,0:T(1,128)S(1)} %copy-done.24, ...), custom_call_target="tpu_custom_call" | custom-call | flops 1132462080 | bytes 4592128 | tf_op jit(solution)/shard_map/grad_inputs/pallas_call | solution.py:62
  282.8 1.3 collective-permute-start.20
  284.1 3.8 %all-to-all-start = ((bf16[8,216,128]{2,1,0:T(8,128)(2,1)}), bf16[8,216,128]{2,1,0:T(8,128)(2,1)S(1)}, u32[]{:S(2)}, u32[]{:S(2)}) async-start(bf16[8,216,128]{2,1,0:T(8,128)(2,1)} %bitcast.11), calls=%async_computation.2 | async-start | bytes 884736 | tf_op jit(solution)/shard_map/all_to_all | solution.py:1148
  288.4 9.3 %collective-permute-done.23 = f32[2,1152]{1,0:T(2,128)S(1)} collective-permute-done((f32[2,1152]{1,0:T(2,128)S(1)}, f32[2,1152]{1,0:T(2,128)S(1)}, u32[]{:S(2)}, u32[]{:S(2)}) %collective-permute-start.23) | collective-permute-done | bytes 9248 | tf_op jit(solution)/shard_map/ppermute | solution.py:723
  298.3 2.4 collective-permute-done.24
  301.3 2.6 collective-permute-done.25
  303.9 1.4 collective-permute-start.26
  306.2 5.2 %all-to-all-start.1 = ((bf16[8,216,128]{2,1,0:T(8,128)(2,1)}), bf16[8,216,128]{2,1,0:T(8,128)(2,1)S(1)}, u32[]{:S(2)}, u32[]{:S(2)}) async-start(bf16[8,216,128]{2,1,0:T(8,128)(2,1)} %broadcast_in_dim.40), calls=%async_computation.3 | async-start | bytes 884736 | tf_op jit(solution)/shard_map/all_to_all | solution.py:1148
  311.5 2.3 fusion.1
  314.5 13.7 %all-to-all-done.1 = bf16[8,216,128]{2,1,0:T(8,128)(2,1)S(1)} async-done(((bf16[8,216,128]{2,1,0:T(8,128)(2,1)}), bf16[8,216,128]{2,1,0:T(8,128)(2,1)S(1)}, u32[]{:S(2)}, u32[]{:S(2)}) %all-to-all-start.1) | async-done | bytes 442400 | tf_op jit(solution)/shard_map/all_to_all | solution.py:1148
  329.3 31.3 %all-gather.7.cloned.1.call-done.gate_up_ref.down_in_ref.mixed_ref = bf16[8,1080,384]{2,1,0:T(8,128)(2,1)} async-done(((bf16[1,1080,384]{2,1,0:T(8,128)(2,1)}), bf16[8,1080,384]{2,1,0:T(8,128)(2,1)}) %all-gather.7.cloned.1.call-update) | async-done | bytes 6635536 | tf_op jit(solution)/shard_map/all_gather | solution.py:752
  360.6 8.9 %widen.1 = (f32[288,3072]{1,0:T(8,128)}, f32[288,3072]{1,0:T(8,128)}, f32[768,1152]{1,0:T(8,128)}, f32[288,1152]{1,0:T(8,128)}, f32[288,1152]{1,0:T(8,128)}) custom-call(s32[2]{0:T(128)} %pad_add_fusion.ids_ref.table_ref, bf16[8,1080,384]{2,1,0:T(8,128)(2,1)} %all-gather.7.cloned.1.call-done.gate_up_ref.down_in_ref.mixed_ref, ...), custom_call_target="tpu_custom_call" | custom-call | flops 1000000 | bytes 20000000 | tf_op jit(solution)/shard_map/widen/pallas_call | solution.py:1183
  (167 shorter events, 27.3 us)
Async XLA Ops:
  7.2 68.4 %all-gather.5.cloned.1.call-start = ((), (), s32[]{:S(2)}) async-start(), calls=%async_computation.5 | async-start | bytes 3538944 | tf_op jit(solution)/shard_map/all_gather | solution.py:752
  9.1 6.6 %copy-start = (bf16[304,768]{1,0:T(8,128)(2,1)}, bf16[304,768]{1,0:T(8,128)(2,1)S(1)}, u32[]{:S(2)}) copy-start(bf16[304,768]{1,0:T(8,128)(2,1)S(1)} %fusion.2.rest_0_.rest_4_) | copy-start | bytes 1400836
  9.1 11.6 %collective-permute-start.1 = (bf16[304,768]{1,0:T(8,128)(2,1)S(1)}, bf16[304,768]{1,0:T(8,128)(2,1)S(1)}, u32[]{:S(2)}, u32[]{:S(2)}) collective-permute-start(bf16[304,768]{1,0:T(8,128)(2,1)S(1)} %fusion.2.rest_0_.rest_4_), channel_id=1, source_target_pairs={{0,2},{1,3},{2,0},{3,1},{4,6},{5,7},{6,4},{7,5},{8,10},{9,11},{10,... | collective-permute-start | bytes 1400840 | tf_op jit(solution)/shard_map/ppermute | solution.py:723
  10.4 13.2 %collective-permute-start = (bf16[304,768]{1,0:T(8,128)(2,1)S(1)}, bf16[304,768]{1,0:T(8,128)(2,1)S(1)}, u32[]{:S(2)}, u32[]{:S(2)}) collective-permute-start(bf16[304,768]{1,0:T(8,128)(2,1)S(1)} %fusion.2.rest_0_.rest_4_), channel_id=1, source_target_pairs={{0,1},{1,0},{2,3},{3,2},{4,5},{5,4},{6,7},{7,6},{8,9},{9,8},{10,11... | collective-permute-start | bytes 1400840 | tf_op jit(solution)/shard_map/ppermute | solution.py:723
  13.4 10.1 %copy-start.29 = (bf16[288,1152]{1,0:T(8,128)(2,1)S(1)}, bf16[288,1152]{1,0:T(8,128)(2,1)}, u32[]{:S(2)}) copy-start(bf16[288,1152]{1,0:T(8,128)(2,1)} %param.15) | copy-start | bytes 1990660
  20.7 3.0 collective-permute-start.2
  24.6 31.9 %copy-start.22 = (s32[2]{0:T(128)S(1)}, s32[2]{0:T(128)}, u32[]{:S(2)}) copy-start(s32[2]{0:T(128)} %pad_add_fusion.ids_ref.table_ref) | copy-start | bytes 28
  29.0 69.8 %all-gather.9.cloned.1.call-start = ((), (), s32[]{:S(2)}) async-start(), calls=%async_computation.9 | async-start | bytes 1990656 | tf_op jit(solution)/shard_map/all_gather | solution.py:752
  29.0 21.1 %collective-permute-start.4 = (bf16[288,1536]{1,0:T(8,128)(2,1)S(1)}, bf16[288,1536]{1,0:T(8,128)(2,1)S(1)}, u32[]{:S(2)}, u32[]{:S(2)}) collective-permute-start(bf16[288,1536]{1,0:T(8,128)(2,1)S(1)} %maximum_maximum_fusion.rest_0_), channel_id=1, source_target_pairs={{0,2},{1,3},{2,0},{3,1},{4,6},{5,7},{6,4},{7,5},{8,10},{9,11},{10,... | collective-permute-start | bytes 2654216 | tf_op jit(solution)/shard_map/ppermute | solution.py:723
  50.1 3.1 collective-permute-start.5
  53.9 140.4 %reduce-scatter.7.cloned.1.call-start = ((), (), s32[]{:S(2)}) async-start(), calls=%async_computation.6 | async-start | bytes 5971968 | tf_op jit(solution)/shard_map/reduce_scatter | solution.py:747
  54.0 2.5 collective-permute-start.3
  54.4 16.6 %collective-permute-start.7 = (bf16[288,1152]{1,0:T(8,128)(2,1)}, bf16[288,1152]{1,0:T(8,128)(2,1)S(1)}, u32[]{:S(2)}, u32[]{:S(2)}) collective-permute-start(bf16[288,1152]{1,0:T(8,128)(2,1)} %rest_0_.3), channel_id=1, source_target_pairs={{0,2},{1,3},{2,0},{3,1},{4,6},{5,7},{6,4},{7,5},{8,10},{9,11},{10,... | collective-permute-start | bytes 1990664 | tf_op jit(solution)/shard_map/ppermute | solution.py:723
  55.6 18.9 %collective-permute-start.6 = (bf16[288,1152]{1,0:T(8,128)(2,1)}, bf16[288,1152]{1,0:T(8,128)(2,1)}, u32[]{:S(2)}, u32[]{:S(2)}) collective-permute-start(bf16[288,1152]{1,0:T(8,128)(2,1)} %rest_0_.3), channel_id=1, source_target_pairs={{0,1},{1,0},{2,3},{3,2},{4,5},{5,4},{6,7},{7,6},{8,9},{9,8},{10,11... | collective-permute-start | bytes 1990664 | tf_op jit(solution)/shard_map/ppermute | solution.py:723
  71.9 3.7 collective-permute-start.8
  72.8 26.0 %collective-permute-start.9 = (bf16[288,1536]{1,0:T(8,128)(2,1)}, bf16[288,1536]{1,0:T(8,128)(2,1)}, u32[]{:S(2)}, u32[]{:S(2)}) collective-permute-start(bf16[288,1536]{1,0:T(8,128)(2,1)} %pad_maximum_fusion), channel_id=1, source_target_pairs={{0,1},{1,0},{2,3},{3,2},{4,5},{5,4},{6,7},{7,6},{8,9},{9,8},{10,11... | collective-permute-start | bytes 2654216 | tf_op jit(solution)/shard_map/ppermute | solution.py:723
  72.8 26.0 %collective-permute-start.11 = (bf16[256,1152]{1,0:T(8,128)(2,1)}, bf16[256,1152]{1,0:T(8,128)(2,1)}, u32[]{:S(2)}, u32[]{:S(2)}) collective-permute-start(bf16[256,1152]{1,0:T(8,128)(2,1)} %bitcast.4.rest_2_.rest_4_.cot_ref), channel_id=1, source_target_pairs={{0,1},{1,0},{2,3},{3,2},{4,5},{5,4},{6,7},{7,6},{8,9},{9,8},{10,11... | collective-permute-start | bytes 1769480 | tf_op jit(solution)/shard_map/ppermute | solution.py:723
  73.3 16.6 %collective-permute-start.13 = (bf16[256,1152]{1,0:T(8,128)(2,1)}, bf16[256,1152]{1,0:T(8,128)(2,1)}, u32[]{:S(2)}, u32[]{:S(2)}) collective-permute-start(bf16[256,1152]{1,0:T(8,128)(2,1)} %bitcast.4.rest_2_.rest_4_.cot_ref), channel_id=1, source_target_pairs={{0,2},{1,3},{2,0},{3,1},{4,6},{5,7},{6,4},{7,5},{8,10},{9,11},{10,... | collective-permute-start | bytes 1769480 | tf_op jit(solution)/shard_map/ppermute | solution.py:723
  88.2 10.6 %collective-permute-start.10 = (bf16[256,1152]{1,0:T(8,128)(2,1)}, bf16[256,1152]{1,0:T(8,128)(2,1)}, u32[]{:S(2)}, u32[]{:S(2)}) collective-permute-start(bf16[256,1152]{1,0:T(8,128)(2,1)} %get-tuple-element.102.rest_0_), channel_id=1, source_target_pairs={{0,1},{1,0},{2,3},{3,2},{4,5},{5,4},{6,7},{7,6},{8,9},{9,8},{10,11... | collective-permute-start | bytes 1769480 | tf_op jit(solution)/shard_map/ppermute | solution.py:723
  88.7 21.2 %collective-permute-start.12 = (bf16[256,1152]{1,0:T(8,128)(2,1)}, bf16[256,1152]{1,0:T(8,128)(2,1)}, u32[]{:S(2)}, u32[]{:S(2)}) collective-permute-start(bf16[256,1152]{1,0:T(8,128)(2,1)} %get-tuple-element.102.rest_0_), channel_id=1, source_target_pairs={{0,2},{1,3},{2,0},{3,1},{4,6},{5,7},{6,4},{7,5},{8,10},{9,11},{10,... | collective-permute-start | bytes 1769480 | tf_op jit(solution)/shard_map/ppermute | solution.py:723
  109.9 6.5 %collective-permute-start.14 = (bf16[256,1152]{1,0:T(8,128)(2,1)}, bf16[256,1152]{1,0:T(8,128)(2,1)}, u32[]{:S(2)}, u32[]{:S(2)}) collective-permute-start(bf16[256,1152]{1,0:T(8,128)(2,1)} %collective-permute-done.12.rest_2_), channel_id=1, source_target_pairs={{0,1},{1,0},{2,3},{3,2},{4,5},{5,4},{6,7},{7,6},{8,9},{9,8},{10,11... | collective-permute-start | bytes 1769480 | tf_op jit(solution)/shard_map/ppermute | solution.py:723
  114.4 2.8 collective-permute-start.15
  133.8 103.6 %reduce-scatter.9.cloned.1.call-start = ((), (), s32[]{:S(2)}) async-start(), calls=%async_computation.7 | async-start | bytes 3538944 | tf_op jit(solution)/shard_map/reduce_scatter | solution.py:747
  139.6 2.7 collective-permute-start.16
  142.1 2.0 collective-permute-start.21
  142.5 14.8 %collective-permute-start.17 = (bf16[256,1152]{1,0:T(8,128)(2,1)S(1)}, bf16[256,1152]{1,0:T(8,128)(2,1)S(1)}, u32[]{:S(2)}, u32[]{:S(2)}) collective-permute-start(bf16[256,1152]{1,0:T(8,128)(2,1)S(1)} %add_convert_fusion.4), channel_id=1, source_target_pairs={{0,2},{1,3},{2,0},{3,1},{4,6},{5,7},{6,4},{7,5},{8,10},{9,11},{10,... | collective-permute-start | bytes 1769480 | tf_op jit(solution)/shard_map/ppermute | solution.py:723
  144.1 13.1 %copy-start.37 = (bf16[256,1152]{1,0:T(8,128)(2,1)}, bf16[256,1152]{1,0:T(8,128)(2,1)S(1)}, u32[]{:S(2)}) copy-start(bf16[256,1152]{1,0:T(8,128)(2,1)S(1)} %collective-permute-done.21.gn_near_ref) | copy-start | bytes 1769476
  196.0 69.7 %reduce-scatter.11.cloned.1.call-start = ((), (), s32[]{:S(2)}) async-start(), calls=%async_computation.10 | async-start | bytes 1492992
  201.4 2.5 collective-permute-start.35
  202.0 4.6 %collective-permute-start.32 = (bf16[288,1152]{1,0:T(8,128)(2,1)}, bf16[288,1152]{1,0:T(8,128)(2,1)S(1)}, u32[]{:S(2)}, u32[]{:S(2)}) collective-permute-start(bf16[288,1152]{1,0:T(8,128)(2,1)} %get-tuple-element.144), channel_id=1, source_target_pairs={{0,1},{1,0},{2,3},{3,2},{4,5},{5,4},{6,7},{7,6},{8,9},{9,8},{10,11... | collective-permute-start | bytes 1990664 | tf_op jit(solution)/shard_map/ppermute | solution.py:723
  202.1 5.1 %collective-permute-start.31 = (bf16[288,1152]{1,0:T(8,128)(2,1)}, bf16[288,1152]{1,0:T(8,128)(2,1)S(1)}, u32[]{:S(2)}, u32[]{:S(2)}) collective-permute-start(bf16[288,1152]{1,0:T(8,128)(2,1)} %get-tuple-element.142), channel_id=1, source_target_pairs={{0,1},{1,0},{2,3},{3,2},{4,5},{5,4},{6,7},{7,6},{8,9},{9,8},{10,11... | collective-permute-start | bytes 1990664 | tf_op jit(solution)/shard_map/ppermute | solution.py:723
  202.5 4.6 %collective-permute-start.34 = (bf16[288,1152]{1,0:T(8,128)(2,1)}, bf16[288,1152]{1,0:T(8,128)(2,1)S(1)}, u32[]{:S(2)}, u32[]{:S(2)}) collective-permute-start(bf16[288,1152]{1,0:T(8,128)(2,1)} %get-tuple-element.146), channel_id=1, source_target_pairs={{0,1},{1,0},{2,3},{3,2},{4,5},{5,4},{6,7},{7,6},{8,9},{9,8},{10,11... | collective-permute-start | bytes 1990664 | tf_op jit(solution)/shard_map/ppermute | solution.py:723
  204.0 31.8 %copy-start.14 = (bf16[288,1152]{1,0:T(8,128)(2,1)S(1)}, bf16[288,1152]{1,0:T(8,128)(2,1)}, u32[]{:S(2)}) copy-start(bf16[288,1152]{1,0:T(8,128)(2,1)} %get-tuple-element.141.refs_0_) | copy-start | bytes 1990660
  204.0 31.8 %copy-start.15 = (bf16[288,1152]{1,0:T(8,128)(2,1)S(1)}, bf16[288,1152]{1,0:T(8,128)(2,1)}, u32[]{:S(2)}) copy-start(bf16[288,1152]{1,0:T(8,128)(2,1)} %get-tuple-element.145.refs_3_) | copy-start | bytes 1990660
  205.4 16.3 %collective-permute-start.36 = (bf16[288,1152]{1,0:T(8,128)(2,1)S(1)}, bf16[288,1152]{1,0:T(8,128)(2,1)S(1)}, u32[]{:S(2)}, u32[]{:S(2)}) collective-permute-start(bf16[288,1152]{1,0:T(8,128)(2,1)S(1)} %add_convert_fusion), channel_id=1, source_target_pairs={{0,2},{1,3},{2,0},{3,1},{4,6},{5,7},{6,4},{7,5},{8,10},{9,11},{10,... | collective-permute-start | bytes 1990664 | tf_op jit(solution)/shard_map/ppermute | solution.py:723
  206.8 29.0 %collective-permute-start.33 = (bf16[288,1152]{1,0:T(8,128)(2,1)S(1)}, bf16[288,1152]{1,0:T(8,128)(2,1)S(1)}, u32[]{:S(2)}, u32[]{:S(2)}) collective-permute-start(bf16[288,1152]{1,0:T(8,128)(2,1)S(1)} %add_convert_fusion.1), channel_id=1, source_target_pairs={{0,2},{1,3},{2,0},{3,1},{4,6},{5,7},{6,4},{7,5},{8,10},{9,11},{10,... | collective-permute-start | bytes 1990664 | tf_op jit(solution)/shard_map/ppermute | solution.py:723
  237.3 123.2 %all-gather.7.cloned.1.call-start = ((), (), s32[]{:S(2)}) async-start(), calls=%async_computation.8 | async-start | bytes 7464960 | tf_op jit(solution)/shard_map/all_gather | solution.py:752
  241.5 14.6 %copy-start.28 = (bf16[288,384]{1,0:T(8,128)(2,1)S(1)}, bf16[288,384]{1,0:T(8,128)(2,1)}, u32[]{:S(2)}) copy-start(bf16[288,384]{1,0:T(8,128)(2,1)} %slice_bitcast_fusion.1) | copy-start | bytes 663556
  243.1 14.1 %copy-start.20 = (bf16[256,768]{1,0:T(8,128)(2,1)}, bf16[256,768]{1,0:T(8,128)(2,1)S(1)}, u32[]{:S(2)}) copy-start(bf16[256,768]{1,0:T(8,128)(2,1)S(1)} %get-tuple-element.128.gkv_ref) | copy-start | bytes 1179652
  243.1 4.5 %collective-permute-start.29 = (bf16[288,768]{1,0:T(8,128)(2,1)S(1)}, bf16[288,768]{1,0:T(8,128)(2,1)S(1)}, u32[]{:S(2)}, u32[]{:S(2)}) collective-permute-start(bf16[288,768]{1,0:T(8,128)(2,1)S(1)} %get-tuple-element.137), channel_id=1, source_target_pairs={{0,1},{1,0},{2,3},{3,2},{4,5},{5,4},{6,7},{7,6},{8,9},{9,8},{10,11... | collective-permute-start | bytes 1327112 | tf_op jit(solution)/shard_map/ppermute | solution.py:723
  244.5 11.7 %collective-permute-start.27 = (bf16[576,384]{1,0:T(8,128)(2,1)S(1)}, bf16[576,384]{1,0:T(8,128)(2,1)S(1)}, u32[]{:S(2)}, u32[]{:S(2)}) collective-permute-start(bf16[576,384]{1,0:T(8,128)(2,1)S(1)} %slice_bitcast_fusion), channel_id=1, source_target_pairs={{0,0},{1,3},{2,2},{3,1},{4,7},{5,6},{6,5},{7,4},{8,8},{9,11},{10,1... | collective-permute-start | bytes 1327112 | tf_op jit(solution)/shard_map/ppermute | solution.py:1020
  247.7 9.6 %collective-permute-start.28 = (bf16[288,768]{1,0:T(8,128)(2,1)S(1)}, bf16[288,768]{1,0:T(8,128)(2,1)S(1)}, u32[]{:S(2)}, u32[]{:S(2)}) collective-permute-start(bf16[288,768]{1,0:T(8,128)(2,1)S(1)} %get-tuple-element.135), channel_id=1, source_target_pairs={{0,1},{1,0},{2,3},{3,2},{4,5},{5,4},{6,7},{7,6},{8,9},{9,8},{10,11... | collective-permute-start | bytes 1327112 | tf_op jit(solution)/shard_map/ppermute | solution.py:723
  247.8 15.2 %collective-permute-start.30 = (bf16[288,768]{1,0:T(8,128)(2,1)S(1)}, bf16[288,768]{1,0:T(8,128)(2,1)S(1)}, u32[]{:S(2)}, u32[]{:S(2)}) collective-permute-start(bf16[288,768]{1,0:T(8,128)(2,1)S(1)} %add_convert_fusion.5), channel_id=1, source_target_pairs={{0,2},{1,3},{2,0},{3,1},{4,6},{5,7},{6,4},{7,5},{8,10},{9,11},{10,... | collective-permute-start | bytes 1327112 | tf_op jit(solution)/shard_map/ppermute | solution.py:723
  267.4 7.4 %copy-start.35 = (bf16[768,1152]{1,0:T(8,128)(2,1)S(1)}, bf16[768,1152]{1,0:T(8,128)(2,1)}, u32[]{:S(2)}) copy-start(bf16[768,1152]{1,0:T(8,128)(2,1)} %down_ref.3) | copy-start | bytes 5308420
  267.4 7.4 %copy-start.39 = (bf16[512,768]{1,0:T(8,128)(2,1)S(1)}, bf16[512,768]{1,0:T(8,128)(2,1)}, u32[]{:S(2)}) copy-start(bf16[512,768]{1,0:T(8,128)(2,1)} %get-tuple-element.104.act_in) | copy-start | bytes 2359300
  270.5 6.7 %copy-start.1 = (bf16[304,768]{1,0:T(8,128)(2,1)S(1)}, bf16[304,768]{1,0:T(8,128)(2,1)}, u32[]{:S(2)}) copy-start(bf16[304,768]{1,0:T(8,128)(2,1)} %copy-done) | copy-start | bytes 1400836
  270.5 6.7 %copy-start.2 = (bf16[1,256,1152]{2,1,0:T(8,128)(2,1)S(1)}, bf16[1,256,1152]{2,1,0:T(8,128)(2,1)}, u32[]{:S(2)}) copy-start(bf16[1,256,1152]{2,1,0:T(8,128)(2,1)} %param.13) | copy-start | bytes 1769476
  270.5 6.7 %copy-start.4 = (bf16[304,768]{1,0:T(8,128)(2,1)S(1)}, bf16[304,768]{1,0:T(8,128)(2,1)}, u32[]{:S(2)}) copy-start(bf16[304,768]{1,0:T(8,128)(2,1)} %copy-done.3) | copy-start | bytes 1400836
  270.5 6.6 %copy-start.6 = (bf16[304,768]{1,0:T(8,128)(2,1)S(1)}, bf16[304,768]{1,0:T(8,128)(2,1)}, u32[]{:S(2)}) copy-start(bf16[304,768]{1,0:T(8,128)(2,1)} %copy-done.5) | copy-start | bytes 1400836
  270.6 6.6 %copy-start.8 = (bf16[304,768]{1,0:T(8,128)(2,1)S(1)}, bf16[304,768]{1,0:T(8,128)(2,1)}, u32[]{:S(2)}) copy-start(bf16[304,768]{1,0:T(8,128)(2,1)} %copy-done.7) | copy-start | bytes 1400836
  270.6 6.6 %copy-start.19 = (bf16[256,1152]{1,0:T(8,128)(2,1)S(1)}, bf16[256,1152]{1,0:T(8,128)(2,1)}, u32[]{:S(2)}) copy-start(bf16[256,1152]{1,0:T(8,128)(2,1)} %get-tuple-element.124.gq_ref.query_ref) | copy-start | bytes 1769476
  270.6 6.6 %copy-start.21 = (bf16[256,768]{1,0:T(8,128)(2,1)S(1)}, bf16[256,768]{1,0:T(8,128)(2,1)}, u32[]{:S(2)}) copy-start(bf16[256,768]{1,0:T(8,128)(2,1)} %copy-done.20) | copy-start | bytes 1179652
  270.6 6.6 %copy-start.24 = (f32[1,1152]{1,0:T(1,128)S(1)}, f32[1,1152]{1,0:T(1,128)}, u32[]{:S(2)}) copy-start(f32[1,1152]{1,0:T(1,128)} %get-tuple-element.129.gain_ref) | copy-start | bytes 13828
  270.6 12.0 %collective-permute-start.19 = (bf16[256,1152]{1,0:T(8,128)(2,1)S(1)}, bf16[256,1152]{1,0:T(8,128)(2,1)S(1)}, u32[]{:S(2)}, u32[]{:S(2)}) collective-permute-start(bf16[256,1152]{1,0:T(8,128)(2,1)S(1)} %slice.69), channel_id=1, source_target_pairs={{0,1},{1,0},{2,3},{3,2},{4,5},{5,4},{6,7},{7,6},{8,9},{9,8},{10,11... | collective-permute-start | bytes 1769480 | tf_op jit(solution)/shard_map/ppermute | solution.py:723
  276.9 34.6 %collective-permute-start.18 = (bf16[256,1152]{1,0:T(8,128)(2,1)}, bf16[256,1152]{1,0:T(8,128)(2,1)}, u32[]{:S(2)}, u32[]{:S(2)}) collective-permute-start(bf16[256,1152]{1,0:T(8,128)(2,1)} %slice.67), channel_id=1, source_target_pairs={{0,1},{1,0},{2,3},{3,2},{4,5},{5,4},{6,7},{7,6},{8,9},{9,8},{10,11... | collective-permute-start | bytes 1769480 | tf_op jit(solution)/shard_map/ppermute | solution.py:723
  282.4 5.5 %collective-permute-start.22 = (f32[2,1152]{1,0:T(2,128)S(1)}, f32[2,1152]{1,0:T(2,128)S(1)}, u32[]{:S(2)}, u32[]{:S(2)}) collective-permute-start(f32[2,1152]{1,0:T(2,128)S(1)} %pad_maximum_fusion.2), channel_id=1, source_target_pairs={{0,1},{1,0},{2,3},{3,2},{4,5},{5,4},{6,7},{7,6},{8,9},{9,8},{10,11... | collective-permute-start | bytes 27656 | tf_op jit(solution)/shard_map/ppermute | solution.py:723
  282.8 28.7 %copy-start.26 = (f32[256,1152]{1,0:T(8,128)S(1)}, f32[256,1152]{1,0:T(8,128)}, u32[]{:S(2)}) copy-start(f32[256,1152]{1,0:T(8,128)} %get-tuple-element.99.mid_ref) | copy-start | bytes 3538948
  282.8 28.7 %collective-permute-start.20 = (bf16[256,1152]{1,0:T(8,128)(2,1)S(1)}, bf16[256,1152]{1,0:T(8,128)(2,1)S(1)}, u32[]{:S(2)}, u32[]{:S(2)}) collective-permute-start(bf16[256,1152]{1,0:T(8,128)(2,1)S(1)} %add_convert_fusion.3), channel_id=1, source_target_pairs={{0,2},{1,3},{2,0},{3,1},{4,6},{5,7},{6,4},{7,5},{8,10},{9,11},{10,... | collective-permute-start | bytes 1769480 | tf_op jit(solution)/shard_map/ppermute | solution.py:723
  284.1 21.3 %all-to-all-start = ((bf16[8,216,128]{2,1,0:T(8,128)(2,1)}), bf16[8,216,128]{2,1,0:T(8,128)(2,1)S(1)}, u32[]{:S(2)}, u32[]{:S(2)}) async-start(bf16[8,216,128]{2,1,0:T(8,128)(2,1)} %bitcast.11), calls=%async_computation.2 | async-start | bytes 884736 | tf_op jit(solution)/shard_map/all_to_all | solution.py:1148
  287.9 9.8 %collective-permute-start.23 = (f32[2,1152]{1,0:T(2,128)S(1)}, f32[2,1152]{1,0:T(2,128)S(1)}, u32[]{:S(2)}, u32[]{:S(2)}) collective-permute-start(f32[2,1152]{1,0:T(2,128)S(1)} %fusion.7), channel_id=1, source_target_pairs={{0,2},{1,3},{2,0},{3,1},{4,6},{5,7},{6,4},{7,5},{8,10},{9,11},{10,... | collective-permute-start | bytes 27656 | tf_op jit(solution)/shard_map/ppermute | solution.py:723
  297.7 3.0 collective-permute-start.24
  300.7 3.2 collective-permute-start.25
  303.9 9.9 %collective-permute-start.26 = (f32[2,1152]{1,0:T(2,128)S(1)}, f32[2,1152]{1,0:T(2,128)S(1)}, u32[]{:S(2)}, u32[]{:S(2)}) collective-permute-start(f32[2,1152]{1,0:T(2,128)S(1)} %add.136), channel_id=1, source_target_pairs={{0,16},{4,20},{8,24},{12,28},{16,0},{20,4},{24,8},{28,12},{1,17},{... | collective-permute-start | bytes 27656 | tf_op jit(solution)/shard_map/ppermute | solution.py:727
  306.2 22.0 %all-to-all-start.1 = ((bf16[8,216,128]{2,1,0:T(8,128)(2,1)}), bf16[8,216,128]{2,1,0:T(8,128)(2,1)S(1)}, u32[]{:S(2)}, u32[]{:S(2)}) async-start(bf16[8,216,128]{2,1,0:T(8,128)(2,1)} %broadcast_in_dim.40), calls=%async_computation.3 | async-start | bytes 884736 | tf_op jit(solution)/shard_map/all_to_all | solution.py:1148
  (21 other events, 39.7 us)
Sparse Core Ops, SparseCore 0:
  29.1 38.4 all-gather.4
  69.7 29.0 all-gather.8
  133.9 60.4 reduce-scatter.6
  197.1 38.1 reduce-scatter.8
  238.1 27.6 reduce-scatter.10
  267.8 92.7 all-gather.6

commit v2 on v1

--- a/solution.py
+++ b/solution.py
@@ -370,6 +370,17 @@
             gq_ref[:, start : start + LANES] = turned.astype(BF16)
 
 
+def columns_in_turn(left, right, full):
+    breadth = full.shape[1] // 3
+
+    def third(index, carry):
+        span = pl.ds(pl.multiple_of(index * breadth, LANES), breadth)
+        full[:, span] = tn(left[...], right[:, span])
+        return carry
+
+    lax.fori_loop(0, 3, third, 0)
+
+
 def kv_back_kernel(ids_ref, grad_ref, cos_ref, sin_ref, hidden_ref, out_ref, *rest, kvw):
     outs, full = rest[:-1], rest[-1]
     for start in range(0, kvw, LANES):
@@ -377,7 +388,7 @@
         turned = tile * cos_ref[...] - swap_halves(tile) * sin_ref[...]
         out_ref[:, start : start + LANES] = turned.astype(BF16)
     out_ref[:, kvw:] = grad_ref[:, kvw:]
-    full[...] = tn(hidden_ref[...], out_ref[...])
+    columns_in_turn(hidden_ref, out_ref, full)
     for index, out in enumerate(outs):
         start = row_start(ids_ref, index, out.shape[0])
         out[...] = full[pl.ds(start, out.shape[0]), :].astype(BF16)
@@ -401,14 +412,22 @@
 
 def inputs_kernel(ids_ref, gq_ref, gkv_ref, x_ref, gain_ref, gmid_ref, *rest, sizes):
     hops = len(sizes)
-    grad_ref, ggain_ref, whole_q, whole_kv, q_sems, kv_sems = rest[2 * hops :]
+    grad_ref, ggain_ref, whole_q, whole_kv, arriving, q_sems, kv_sems = rest[2 * hops :]
     copies = fetches(ids_ref, rest[:hops], whole_q, q_sems, sizes)
     copies += fetches(ids_ref, rest[hops : 2 * hops], whole_kv, kv_sems, sizes)
     for copy in copies:
         copy.start()
     for copy in copies:
         copy.wait()
-    incoming = nt(gq_ref[...], whole_q[...]) + nt(gkv_ref[...], whole_kv[...])
+    breadth = arriving.shape[1] // 3
+
+    def third(index, carry):
+        span = pl.ds(pl.multiple_of(index * breadth, LANES), breadth)
+        arriving[:, span] = nt(gq_ref[...], whole_q[span, :]) + nt(gkv_ref[...], whole_kv[span, :])
+        return carry
+
+    lax.fori_loop(0, 3, third, 0)
+    incoming = arriving[...]
     x = x_ref[...].astype(F32)
     scale = lax.rsqrt(jnp.mean(x * x, axis=-1, keepdims=True) + EPSILON)
     weighted = incoming * gain_ref[...]
@@ -481,11 +500,8 @@
                 half,
                 lanes,
             )
-    count = tokens.shape[0] // 2
     loads = [
-        pltpu.make_async_copy(
-            ref, target.at[pl.ds(index * count, count), :], token_sems.at[slot, index]
-        )
+        pltpu.make_async_copy(ref, target.at[index], token_sems.at[slot, index])
         for slot, (refs, target) in enumerate(((normed_refs, tokens), (cot_refs, cots)))
         for index, ref in enumerate(refs)
     ]
@@ -512,12 +528,16 @@
     for copy in loads:
         copy.wait()
 
-    act[...], grad_gate[...], grad_up[...] = units(
-        tokens[...], cots[...], gate_mat[...], up_mat[...], down_mat[...]
-    )
-    back[...] = (
-        nt(grad_gate[...], gate_mat[...]) + nt(grad_up[...], up_mat[...])
-    ).astype(BF16)
+    def token_block(index, carry):
+        act[index], grad_gate[index], grad_up[index] = units(
+            tokens[index], cots[index], gate_mat[...], up_mat[...], down_mat[...]
+        )
+        back[index] = (
+            nt(grad_gate[index], gate_mat[...]) + nt(grad_up[index], up_mat[...])
+        ).astype(BF16)
+        return carry
+
+    lax.fori_loop(0, 2, token_block, 0)
     for copy in outs[2:]:
         copy.start()
     for copy in outs:
@@ -535,7 +555,7 @@
     ]
     mat_sems, token_sems, cot_sems, unit_sems, out_sems, tile_sems = rest[2 * hops + 14 :]
     width, own = gate_mat.shape
-    count = tokens.shape[0] // hops
+    count = tokens.shape[1]
     places, height, tile = tiles.shape
     rows = height // 3
     mats = [
@@ -545,7 +565,7 @@
         )
     ]
     token_copies = [
-        pltpu.make_async_copy(ref, tokens.at[pl.ds(index * count, count), :], token_sems.at[index])
+        pltpu.make_async_copy(ref, tokens.at[index], token_sems.at[index])
         for index, ref in enumerate(normed_refs)
     ]
     cot_copies = [
@@ -553,10 +573,12 @@
         for index, ref in enumerate(cot_refs)
     ]
     unit_copies = [
-        pltpu.make_async_copy(source, target.at[pl.ds(0, 2 * count), :], unit_sems.at[slot])
+        pltpu.make_async_copy(source.at[index], target.at[pl.ds(index * count, count), :],
+                              unit_sems.at[slot, index])
         for slot, (source, target) in enumerate(
             ((act_in, act), (gate_in, grad_gate), (up_in, grad_up))
         )
+        for index in range(2)
     ]
     for copy in mats + token_copies[2:] + cot_copies[2:]:
         copy.start()
@@ -564,15 +586,22 @@
         copy.start()
     for copy in token_copies[:2]:
         copy.wait()
-    turned[:, : 2 * count] = tokens[: 2 * count, :].T
+    for index in range(2):
+        turned[:, index * count : (index + 1) * count] = tokens[index].T
     for copy in mats + token_copies[2:] + cot_copies[2:]:
         copy.wait()
 
+    def token_block(index, carry):
+        span = pl.ds(pl.multiple_of(index * count, count), count)
+        normed = tokens[index]
+        act[span, :], grad_gate[span, :], grad_up[span, :] = units(
+            normed, cots[span, :], gate_mat[...], up_mat[...], down_mat[...]
+        )
+        turned[:, span] = normed.T
+        return carry
+
+    lax.fori_loop(2, hops, token_block, 0)
     late = pl.ds(2 * count, 2 * count)
-    act[late, :], grad_gate[late, :], grad_up[late, :] = units(
-        tokens[late, :], cots[late, :], gate_mat[...], up_mat[...], down_mat[...]
-    )
-    turned[:, 2 * count :] = tokens[late, :].T
     outs = [
         pltpu.make_async_copy(source.at[late, :], target, out_sems.at[index])
         for index, (source, target) in enumerate(
@@ -593,39 +622,35 @@
         )
 
     def row_block(index, carry):
-        left = turned[pl.ds(pl.multiple_of(index * 2 * rows, 16), 2 * rows), :]
-        spots = [
-            lax.rem(2 * index + block + ids_ref[0], hops) * per_shard for block in range(2)
-        ]
+        left = turned[pl.ds(pl.multiple_of(index * rows, 16), rows), :]
+        spot = lax.rem(index + ids_ref[0], hops) * per_shard
         for slot, ref in ((0, grad_gate), (1, grad_up)):
             grad = nn(left, ref[...])
-            for block, spot in enumerate(spots):
-                for part in range(per_shard):
-                    tiles[spot + part, slot * rows : (slot + 1) * rows, :] = grad[
-                        block * rows : (block + 1) * rows, part * tile : (part + 1) * tile
-                    ].astype(BF16)
-        for spot in spots:
             for part in range(per_shard):
-                tile_copy(spot + part, 0).start()
+                tiles[spot + part, slot * rows : (slot + 1) * rows, :] = grad[
+                    :, part * tile : (part + 1) * tile
+                ].astype(BF16)
+        for part in range(per_shard):
+            tile_copy(spot + part, 0).start()
         return carry
 
-    lax.fori_loop(0, hops // 2, row_block, 0)
+    lax.fori_loop(0, hops, row_block, 0)
     band = own // places
     turned[:own, :] = act[...].T
 
     def down_block(index, carry):
-        left = turned[pl.ds(pl.multiple_of(index * 4 * band, 16), 4 * band), :]
+        left = turned[pl.ds(pl.multiple_of(index * 2 * band, 16), 2 * band), :]
         grad = nn(left, cots[...])
-        for part in range(4):
+        for part in range(2):
             for split in range(width // tile):
                 start = 2 * rows + split * band
-                tiles[4 * index + part, start : start + band, :] = grad[
+                tiles[2 * index + part, start : start + band, :] = grad[
                     part * band : (part + 1) * band, split * tile : (split + 1) * tile
                 ].astype(BF16)
-            tile_copy(4 * index + part, 1).start()
+            tile_copy(2 * index + part, 1).start()
         return carry
 
-    lax.fori_loop(0, places // 4, down_block, 0)
+    lax.fori_loop(0, places // 2, down_block, 0)
     for copy in outs:
         copy.wait()
     for spot in range(places):
@@ -889,9 +914,9 @@
     far_rows = after(far_rows, normed)
     all_count = n_shard * count
     if aligned:
-        two = ((2 * count, ff_own), BF16)
+        two = ((2, count, ff_own), BF16)
         mats = [((width, ff_own), BF16)] * 2
-        pair = (2 * count, width)
+        pair = (2, count, width)
         gate_mat, up_mat, *near_units, back = pl.pallas_call(
             functools.partial(feed_near_kernel, half=half, lanes=lanes),
             out_shape=tuple(
@@ -944,7 +969,7 @@
                 pltpu.VMEM((width, ff_own), BF16),
                 pltpu.VMEM((width, ff_own), BF16),
                 pltpu.VMEM((ff_own, width), BF16),
-                pltpu.VMEM((all_count, width), BF16),
+                pltpu.VMEM((n_shard, count, width), BF16),
                 pltpu.VMEM((all_count, width), BF16),
                 pltpu.VMEM((width, all_count), BF16),
                 pltpu.VMEM((all_count, ff_own), BF16),
@@ -954,7 +979,7 @@
                 pltpu.SemaphoreType.DMA((3,)),
                 pltpu.SemaphoreType.DMA((n_shard,)),
                 pltpu.SemaphoreType.DMA((n_shard,)),
-                pltpu.SemaphoreType.DMA((3,)),
+                pltpu.SemaphoreType.DMA((3, 2)),
                 pltpu.SemaphoreType.DMA((3,)),
                 pltpu.SemaphoreType.DMA((2, n_ctx)),
             ],
@@ -964,8 +989,8 @@
         )(
             ids, gate_mat, up_mat, w_down, *near_units, *normed_pieces, *cot_pieces
         )
-        to_own, to_near = back[:count], back[count:]
-        act_parts = [near_units[0], far_units[0]]
+        to_own, to_near = back[0], back[1]
+        act_parts = [near_units[0].reshape(2 * count, ff_own), far_units[0]]
         grad_gate_far, grad_up_far = far_units[1:]
     else:
         normed_pieces = [normed, normed_near, normed_far, hop(normed_far, 1)]
@@ -1162,6 +1187,7 @@
         scratch=[
             pltpu.VMEM((width, qw), BF16),
             pltpu.VMEM((width, 2 * kvw), BF16),
+            pltpu.VMEM((count, width), F32),
             fetch_sems,
             fetch_sems,
         ],

time: 384 us -> 378 us (0.984); the launches traced: 377 us -> 377 us
    unnamed x80 -> x82, local copies, waits for them, and re-layouts: 11.2 us -> 11.3 us
  transfers between devices with their start and end apart: 45 -> 45, of which waited for: 24 -> 24; matrix products, arithmetic and copies ran while one was open for 6% -> 6% of each run, Pallas kernels for 17% -> 18%
where the time goes in v2:
time: 378 us; the launch traced here: 377 us
  waiting for transfers between devices  182 us (48%)
  Pallas kernels  96.9 us (26%)
  starting transfers between devices  45.3 us (12%)
  local copies, waits for them, and re-layouts  20.5 us (5%)
  between operations  14.6 us (4%)
  other arithmetic  14 us (4%)
  matrix products  4.25 us (1%)
    ppermute x33, waiting for transfers between devices, hop(): return lax.ppermute(value, 'shard', pairs)  99.3 us
    all_gather x3, waiting for transfers between devices, collect(): lax.all_gather(value, 'ctx', axis=0, axis_index_groups=[order], tiled=True)  38.4 us
    ppermute x33, starting transfers between devices, hop(): return lax.ppermute(value, 'shard', pairs)  29.3 us
    pallas_call x8, Pallas kernels, call_once(): pl.pallas_call(kernel, out_shape=tuple((jax.ShapeDtypeStruct(shape, dtype...  27.2 us
    pallas_call x1, Pallas kernels, on_device(): pl.pallas_call(functools.partial(attend_back_kernel, **shared), out_shape...  19.5 us
    pallas_call x1, Pallas kernels, on_device(): pl.pallas_call(functools.partial(feed_far_kernel, per_shard=per_shard), o...  17.5 us
    reduce_scatter x2, waiting for transfers between devices, scatter(): lax.psum_scatter(value, 'ctx', scatter_dimension=0, axis_index_groups=[or...  16.6 us
    all_to_all x2, waiting for transfers between devices, exchange(): return lax.all_to_all(value, 'ctx', split_axis=0, concat_axis=0, tiled=True)  14 us
  transfers between devices with their start and end apart: 45, of which 24 were waited for; matrix products, arithmetic and copies ran while one was open for 6% of the time, Pallas kernels for 18%

profile of v2, /device:TPU:9, one launch (start us, length us, event | category | flops | bytes accessed | tf_op | source)
XLA Modules:
  0.0 377.3 jit_solution(8851320474935807004)
XLA Ops:
  8.0 1.1 fusion.2.rest_0_.rest_4_
  9.1 1.3 collective-permute-start.1
  11.4 1.4 dynamic-slice_select_fusion.1
  13.3 1.3 constant_dynamic-slice_fusion
  15.6 5.1 %collective-permute-done.1.rest_2_.rest_6_ = bf16[304,768]{1,0:T(8,128)(2,1)S(1)} collective-permute-done((bf16[304,768]{1,0:T(8,128)(2,1)S(1)}, bf16[304,768]{1,0:T(8,128)(2,1)S(1)}, u32[]{:S(2)}, u32[]{:S(2)}) %collective-permute-start.1) | collective-permute-done | bytes 466976 | tf_op jit(solution)/shard_map/ppermute | solution.py:748
  20.7 1.5 collective-permute-start.2
  22.3 1.3 fusion.3
  24.6 4.4 %keys.1 = (bf16[256,1152]{1,0:T(8,128)(2,1)}, bf16[256,768]{1,0:T(8,128)(2,1)}, f32[1,1152]{1,0:T(1,128)}, f32[1,1152]{1,0:T(1,128)}) custom-call(s32[2]{0:T(128)} %pad_add_fusion.ids_ref.table_ref, bf16[256,1152]{1,0:T(8,128)(2,1)} %bitcast.34, f32[256,128]{1,0:T(8,128)} %get-tuple-element.90.cos_ref, f32[256,128]{1,0:T(8,128)} %get-tuple-element.91.sin_ref, ...), custom_call_target="tpu_custom_call" | custom-call | flops 452984832 | bytes 4987648 | tf_op jit(solution)/shard_map/keys/pallas_call | solution.py:62
  29.0 1.3 collective-permute-start.4
  30.3 19.8 %collective-permute-done.4.rest_2_ = bf16[288,1536]{1,0:T(8,128)(2,1)S(1)} collective-permute-done((bf16[288,1536]{1,0:T(8,128)(2,1)S(1)}, bf16[288,1536]{1,0:T(8,128)(2,1)S(1)}, u32[]{:S(2)}, u32[]{:S(2)}) %collective-permute-start.4) | collective-permute-done | bytes 884768 | tf_op jit(solution)/shard_map/ppermute | solution.py:748
  50.1 1.0 collective-permute-start.5
  51.1 2.0 collective-permute-done.5.rest_3_
  54.6 1.2 collective-permute-start.7
  58.5 1.1 copy-done.16
  59.5 2.0 queries.1.q_ref
  62.3 8.9 %collective-permute-done.7.rest_2_ = bf16[288,1152]{1,0:T(8,128)(2,1)S(1)} collective-permute-done((bf16[288,1152]{1,0:T(8,128)(2,1)}, bf16[288,1152]{1,0:T(8,128)(2,1)S(1)}, u32[]{:S(2)}, u32[]{:S(2)}) %collective-permute-start.7) | collective-permute-done | bytes 663584 | tf_op jit(solution)/shard_map/ppermute | solution.py:748
  73.5 1.2 collective-permute-start.13
  74.7 1.1 collective-permute-done.8.rest_3_
  75.8 12.5 %attend.1 = (f32[1152,256]{1,0:T(8,128)}, bf16[256,1152]{1,0:T(8,128)(2,1)}, f32[8,768]{1,0:T(8,128)}, f32[256,1152]{1,0:T(8,128)}, bf16[256,1152]{1,0:T(8,128)(2,1)}, /*index=5*/bf16[6,64,768]{2,1,0:T(8,128)(2,1)}) custom-call(s32[2]{0:T(128)} %pad_add_fusion.ids_ref.table_ref, bf16[256,1152]{1,0:T(8,128)(2,1)} %copy-done.18, ...), custom_call_target="tpu_custom_call" | custom-call | flops 2415919104 | bytes 12000000 | tf_op jit(solution)/shard_map/attend/pallas_call | solution.py:871
  88.7 1.2 collective-permute-start.12
  89.9 8.8 %all-gather.9.cloned.1.call-done = bf16[2304,384]{1,0:T(8,128)(2,1)} async-done(((bf16[288,384]{1,0:T(8,128)(2,1)}), bf16[2304,384]{1,0:T(8,128)(2,1)}) %all-gather.9.cloned.1.call-update) | async-done | bytes 1769488 | tf_op jit(solution)/shard_map/all_gather | solution.py:777
  98.7 11.4 %feed_near.1 = (bf16[1152,768]{1,0:T(8,128)(2,1)}, bf16[1152,768]{1,0:T(8,128)(2,1)}, bf16[2,256,768]{2,1,0:T(8,128)(2,1)}, bf16[2,256,768]{2,1,0:T(8,128)(2,1)}...) custom-call(s32[2]{0:T(128)} %pad_add_fusion.ids_ref.table_ref, bf16[288,3072]{1,0:T(8,128)(2,1)} %own_gate_ref.1, ...), custom_call_target="tpu_custom_call" | custom-call | flops 4529848320 | bytes 12000000 | tf_op jit(solution)/shard_map/feed_near/pallas_call | solution.py:920
  110.2 4.4 %collective-permute-start.14 = (bf16[256,1152]{1,0:T(8,128)(2,1)}, bf16[256,1152]{1,0:T(8,128)(2,1)}, u32[]{:S(2)}, u32[]{:S(2)}) collective-permute-start(bf16[256,1152]{1,0:T(8,128)(2,1)} %collective-permute-done.12.rest_2_), channel_id=1, source_target_pairs={{0,1},{1,0},{2,3},{3,2},{4,5},{5,4},{6,7},{7,6},{8,9},{9,8},{10,11... | collective-permute-start | bytes 1769480 | tf_op jit(solution)/shard_map/ppermute | solution.py:748
  114.7 1.9 collective-permute-done.14.rest_3_
  117.4 17.5 %feed_far.1 = (bf16[8,864,384]{2,1,0:T(8,128)(2,1)}, bf16[512,768]{1,0:T(8,128)(2,1)}, bf16[512,768]{1,0:T(8,128)(2,1)}, bf16[512,768]{1,0:T(8,128)(2,1)}) custom-call(s32[2]{0:T(128)} %pad_add_fusion.ids_ref.table_ref, bf16[1152,768]{1,0:T(8,128)(2,1)} %get-tuple-element.105.gate_mat_ref, bf16[1152,768]{1,0:T(8,128)(2,1)} %get-tuple-element.106.up_mat_ref, ...), custom_call_target="tpu_custom_call" | custom-call | flops 8153726976 | bytes 25000000 | tf_op jit(solution)/shard_map/feed_far/pallas_call | solution.py:960
  135.2 5.6 %normed_back.1 = (bf16[256,1152]{1,0:T(8,128)(2,1)}, bf16[256,1152]{1,0:T(8,128)(2,1)}) custom-call(bf16[512,768]{1,0:T(8,128)(2,1)} %get-tuple-element.114.gate_ref, bf16[512,768]{1,0:T(8,128)(2,1)} %get-tuple-element.115.up_ref, bf16[1152,768]{1,0:T(8,128)(2,1)} %get-tuple-element.105.gate_mat_ref, bf16[1152,768]{1,0:T(8,128)(2,1)} %get-tuple-element.106.up_mat_ref), custom_call_target="tpu_custom_call" | custom-call | flops 1811939328 | bytes 5179648 | tf_op jit(solution)/shard_map/normed_back/pallas_call | solution.py:62
  141.2 2.1 slice_bitcast_fusion
  143.7 1.3 collective-permute-start.17
  145.4 13.1 %collective-permute-done.17.gn_far_ref = bf16[256,1152]{1,0:T(8,128)(2,1)S(1)} collective-permute-done((bf16[256,1152]{1,0:T(8,128)(2,1)S(1)}, bf16[256,1152]{1,0:T(8,128)(2,1)S(1)}, u32[]{:S(2)}, u32[]{:S(2)}) %collective-permute-start.17) | collective-permute-done | bytes 589856 | tf_op jit(solution)/shard_map/ppermute | solution.py:748
  159.3 19.5 %attend_back.1 = (bf16[256,1152]{1,0:T(8,128)(2,1)}, bf16[2048,768]{1,0:T(8,128)(2,1)}, bf16[256,1152]{1,0:T(8,128)(2,1)}, f32[256,1152]{1,0:T(8,128)}, f32[1,1152]{1,0:T(1,128)}) custom-call(s32[2]{0:T(128)} %pad_add_fusion.ids_ref.table_ref, bf16[2048,768]{1,0:T(8,128)(2,1)} %all-gather.5.cloned.1.call-done.kv_ref, ...), custom_call_target="tpu_custom_call" | custom-call | flops 6039797760 | bytes 14000000 | tf_op jit(solution)/shard_map/attend_back/pallas_call | solution.py:1066
  178.8 16.6 %reduce-scatter.7.cloned.1.call-done = bf16[1,864,384]{2,1,0:T(8,128)(2,1)} async-done(((bf16[8,864,384]{2,1,0:T(8,128)(2,1)}), bf16[1,864,384]{2,1,0:T(8,128)(2,1)}) %reduce-scatter.7.cloned.1.call-update) | async-done | bytes 663568 | tf_op jit(solution)/shard_map/reduce_scatter | solution.py:772
  195.4 1.6 slice_bitcast_fusion.3
  197.1 5.3 %weight_grads.1 = (bf16[288,1152]{1,0:T(8,128)(2,1)}, bf16[288,1152]{1,0:T(8,128)(2,1)}, bf16[288,1152]{1,0:T(8,128)(2,1)}, bf16[288,1152]{1,0:T(8,128)(2,1)}, b...) custom-call(s32[2]{0:T(128)} %pad_add_fusion.ids_ref.table_ref, ...), custom_call_target="tpu_custom_call" | custom-call | flops 1358954496 | bytes 9308416 | tf_op jit(solution)/shard_map/weight_grads/pallas_call | solution.py:62
  203.6 1.4 collective-permute-done.35
  205.0 1.4 add_convert_fusion
  206.4 1.2 collective-permute-start.36
  208.2 14.5 %collective-permute-done.36.refs_5_ = bf16[288,1152]{1,0:T(8,128)(2,1)S(1)} collective-permute-done((bf16[288,1152]{1,0:T(8,128)(2,1)S(1)}, bf16[288,1152]{1,0:T(8,128)(2,1)S(1)}, u32[]{:S(2)}, u32[]{:S(2)}) %collective-permute-start.36) | collective-permute-done | bytes 663584 | tf_op jit(solution)/shard_map/ppermute | solution.py:748
  222.7 14.1 %collective-permute-done.33.refs_2_ = bf16[288,1152]{1,0:T(8,128)(2,1)S(1)} collective-permute-done((bf16[288,1152]{1,0:T(8,128)(2,1)S(1)}, bf16[288,1152]{1,0:T(8,128)(2,1)S(1)}, u32[]{:S(2)}, u32[]{:S(2)}) %collective-permute-start.33) | collective-permute-done | bytes 663584 | tf_op jit(solution)/shard_map/ppermute | solution.py:748
  236.8 1.6 stack_mixed.1
  240.5 1.1 copy-done.17
  241.6 1.0 copy-done.25
  242.6 2.1 kv_back.1
  244.6 1.3 collective-permute-start.29
  246.0 3.1 collective-permute-start.27
  249.6 7.9 %collective-permute-done.27 = bf16[576,384]{1,0:T(8,128)(2,1)S(1)} collective-permute-done((bf16[576,384]{1,0:T(8,128)(2,1)S(1)}, bf16[576,384]{1,0:T(8,128)(2,1)S(1)}, u32[]{:S(2)}, u32[]{:S(2)}) %collective-permute-start.27) | collective-permute-done | bytes 442400 | tf_op jit(solution)/shard_map/ppermute | solution.py:1045
  257.5 1.1 maximum_maximum_fusion.1
  258.6 6.2 %collective-permute-done.30.refs_2_ = bf16[288,768]{1,0:T(8,128)(2,1)S(1)} collective-permute-done((bf16[288,768]{1,0:T(8,128)(2,1)S(1)}, bf16[288,768]{1,0:T(8,128)(2,1)S(1)}, u32[]{:S(2)}, u32[]{:S(2)}) %collective-permute-start.30) | collective-permute-done | bytes 442400 | tf_op jit(solution)/shard_map/ppermute | solution.py:748
  266.8 1.6 constant_dynamic-update-slice_fusion
  268.5 3.0 convolution_convert_fusion
  271.6 4.1 %collective-permute-start.19 = (bf16[256,1152]{1,0:T(8,128)(2,1)S(1)}, bf16[256,1152]{1,0:T(8,128)(2,1)S(1)}, u32[]{:S(2)}, u32[]{:S(2)}) collective-permute-start(bf16[256,1152]{1,0:T(8,128)(2,1)S(1)} %slice.69), channel_id=1, source_target_pairs={{0,1},{1,0},{2,3},{3,2},{4,5},{5,4},{6,7},{7,6},{8,9},{9,8},{10,11... | collective-permute-start | bytes 1769480 | tf_op jit(solution)/shard_map/ppermute | solution.py:748
  275.8 1.2 convolution_convert_fusion.1
  279.1 5.4 %grad_inputs.1 = (bf16[256,1152]{1,0:T(8,128)(2,1)}, f32[1,1152]{1,0:T(1,128)S(1)}) custom-call(s32[2]{0:T(128)S(1)} %copy-done.23, bf16[256,1152]{1,0:T(8,128)(2,1)S(1)} %copy-done.19, bf16[256,768]{1,0:T(8,128)(2,1)S(1)} %copy-done.21, bf16[256,1152]{1,0:T(8,128)(2,1)S(1)} %bitcast.36, f32[1,1152]{1,0:T(1,128)S(1)} %copy-done.24, ...), custom_call_target="tpu_custom_call" | custom-call | flops 1132462080 | bytes 4592128 | tf_op jit(solution)/shard_map/grad_inputs/pallas_call | solution.py:62
  285.6 1.2 collective-permute-start.20
  286.8 3.8 all-to-all-start
  291.2 9.4 %collective-permute-done.23 = f32[2,1152]{1,0:T(2,128)S(1)} collective-permute-done((f32[2,1152]{1,0:T(2,128)S(1)}, f32[2,1152]{1,0:T(2,128)S(1)}, u32[]{:S(2)}, u32[]{:S(2)}) %collective-permute-start.23) | collective-permute-done | bytes 9248 | tf_op jit(solution)/shard_map/ppermute | solution.py:748
  300.6 1.1 collective-permute-start.24
  301.7 1.9 collective-permute-done.24
  304.2 2.5 collective-permute-done.25
  306.7 1.4 collective-permute-start.26
  309.0 5.1 %all-to-all-start.1 = ((bf16[8,216,128]{2,1,0:T(8,128)(2,1)}), bf16[8,216,128]{2,1,0:T(8,128)(2,1)S(1)}, u32[]{:S(2)}, u32[]{:S(2)}) async-start(bf16[8,216,128]{2,1,0:T(8,128)(2,1)} %broadcast_in_dim.40), calls=%async_computation.3 | async-start | bytes 884736 | tf_op jit(solution)/shard_map/all_to_all | solution.py:1173
  314.1 2.1 fusion.1
  317.0 14.0 %all-to-all-done.1 = bf16[8,216,128]{2,1,0:T(8,128)(2,1)S(1)} async-done(((bf16[8,216,128]{2,1,0:T(8,128)(2,1)}), bf16[8,216,128]{2,1,0:T(8,128)(2,1)S(1)}, u32[]{:S(2)}, u32[]{:S(2)}) %all-to-all-start.1) | async-done | bytes 442400 | tf_op jit(solution)/shard_map/all_to_all | solution.py:1173
  332.0 29.6 %all-gather.7.cloned.1.call-done.gate_up_ref.down_in_ref.mixed_ref = bf16[8,1080,384]{2,1,0:T(8,128)(2,1)} async-done(((bf16[1,1080,384]{2,1,0:T(8,128)(2,1)}), bf16[8,1080,384]{2,1,0:T(8,128)(2,1)}) %all-gather.7.cloned.1.call-update) | async-done | bytes 6635536 | tf_op jit(solution)/shard_map/all_gather | solution.py:777
  361.6 8.9 %widen.1 = (f32[288,3072]{1,0:T(8,128)}, f32[288,3072]{1,0:T(8,128)}, f32[768,1152]{1,0:T(8,128)}, f32[288,1152]{1,0:T(8,128)}, f32[288,1152]{1,0:T(8,128)}) custom-call(s32[2]{0:T(128)} %pad_add_fusion.ids_ref.table_ref, bf16[8,1080,384]{2,1,0:T(8,128)(2,1)} %all-gather.7.cloned.1.call-done.gate_up_ref.down_in_ref.mixed_ref, ...), custom_call_target="tpu_custom_call" | custom-call | flops 1000000 | bytes 20000000 | tf_op jit(solution)/shard_map/widen/pallas_call | solution.py:1209
  (169 shorter events, 28.8 us)
Async XLA Ops:
  7.2 68.6 %all-gather.5.cloned.1.call-start = ((), (), s32[]{:S(2)}) async-start(), calls=%async_computation.5 | async-start | bytes 3538944 | tf_op jit(solution)/shard_map/all_gather | solution.py:777
  9.1 6.5 %copy-start = (bf16[304,768]{1,0:T(8,128)(2,1)}, bf16[304,768]{1,0:T(8,128)(2,1)S(1)}, u32[]{:S(2)}) copy-start(bf16[304,768]{1,0:T(8,128)(2,1)S(1)} %fusion.2.rest_0_.rest_4_) | copy-start | bytes 1400836
  9.1 11.6 %collective-permute-start.1 = (bf16[304,768]{1,0:T(8,128)(2,1)S(1)}, bf16[304,768]{1,0:T(8,128)(2,1)S(1)}, u32[]{:S(2)}, u32[]{:S(2)}) collective-permute-start(bf16[304,768]{1,0:T(8,128)(2,1)S(1)} %fusion.2.rest_0_.rest_4_), channel_id=1, source_target_pairs={{0,2},{1,3},{2,0},{3,1},{4,6},{5,7},{6,4},{7,5},{8,10},{9,11},{10,... | collective-permute-start | bytes 1400840 | tf_op jit(solution)/shard_map/ppermute | solution.py:748
  10.4 13.2 %collective-permute-start = (bf16[304,768]{1,0:T(8,128)(2,1)S(1)}, bf16[304,768]{1,0:T(8,128)(2,1)S(1)}, u32[]{:S(2)}, u32[]{:S(2)}) collective-permute-start(bf16[304,768]{1,0:T(8,128)(2,1)S(1)} %fusion.2.rest_0_.rest_4_), channel_id=1, source_target_pairs={{0,1},{1,0},{2,3},{3,2},{4,5},{5,4},{6,7},{7,6},{8,9},{9,8},{10,11... | collective-permute-start | bytes 1400840 | tf_op jit(solution)/shard_map/ppermute | solution.py:748
  13.3 10.2 %copy-start.30 = (bf16[288,1152]{1,0:T(8,128)(2,1)S(1)}, bf16[288,1152]{1,0:T(8,128)(2,1)}, u32[]{:S(2)}) copy-start(bf16[288,1152]{1,0:T(8,128)(2,1)} %param.15) | copy-start | bytes 1990660
  20.7 3.0 copy-start.3
  20.7 3.0 collective-permute-start.2
  24.6 32.1 %copy-start.22 = (s32[2]{0:T(128)S(1)}, s32[2]{0:T(128)}, u32[]{:S(2)}) copy-start(s32[2]{0:T(128)} %pad_add_fusion.ids_ref.table_ref) | copy-start | bytes 28
  28.9 69.8 %all-gather.9.cloned.1.call-start = ((), (), s32[]{:S(2)}) async-start(), calls=%async_computation.9 | async-start | bytes 1990656 | tf_op jit(solution)/shard_map/all_gather | solution.py:777
  29.0 21.1 %collective-permute-start.4 = (bf16[288,1536]{1,0:T(8,128)(2,1)S(1)}, bf16[288,1536]{1,0:T(8,128)(2,1)S(1)}, u32[]{:S(2)}, u32[]{:S(2)}) collective-permute-start(bf16[288,1536]{1,0:T(8,128)(2,1)S(1)} %maximum_maximum_fusion.rest_0_), channel_id=1, source_target_pairs={{0,2},{1,3},{2,0},{3,1},{4,6},{5,7},{6,4},{7,5},{8,10},{9,11},{10,... | collective-permute-start | bytes 2654216 | tf_op jit(solution)/shard_map/ppermute | solution.py:748
  50.1 3.1 collective-permute-start.5
  53.9 141.5 %reduce-scatter.7.cloned.1.call-start = ((), (), s32[]{:S(2)}) async-start(), calls=%async_computation.6 | async-start | bytes 5971968 | tf_op jit(solution)/shard_map/reduce_scatter | solution.py:772
  54.2 2.5 collective-permute-start.3
  54.6 16.6 %collective-permute-start.7 = (bf16[288,1152]{1,0:T(8,128)(2,1)}, bf16[288,1152]{1,0:T(8,128)(2,1)S(1)}, u32[]{:S(2)}, u32[]{:S(2)}) collective-permute-start(bf16[288,1152]{1,0:T(8,128)(2,1)} %rest_0_.3), channel_id=1, source_target_pairs={{0,2},{1,3},{2,0},{3,1},{4,6},{5,7},{6,4},{7,5},{8,10},{9,11},{10,... | collective-permute-start | bytes 1990664 | tf_op jit(solution)/shard_map/ppermute | solution.py:748
  55.8 18.9 %collective-permute-start.6 = (bf16[288,1152]{1,0:T(8,128)(2,1)}, bf16[288,1152]{1,0:T(8,128)(2,1)}, u32[]{:S(2)}, u32[]{:S(2)}) collective-permute-start(bf16[288,1152]{1,0:T(8,128)(2,1)} %rest_0_.3), channel_id=1, source_target_pairs={{0,1},{1,0},{2,3},{3,2},{4,5},{5,4},{6,7},{7,6},{8,9},{9,8},{10,11... | collective-permute-start | bytes 1990664 | tf_op jit(solution)/shard_map/ppermute | solution.py:748
  72.0 3.7 collective-permute-start.8
  73.0 25.7 %collective-permute-start.9 = (bf16[288,1536]{1,0:T(8,128)(2,1)}, bf16[288,1536]{1,0:T(8,128)(2,1)}, u32[]{:S(2)}, u32[]{:S(2)}) collective-permute-start(bf16[288,1536]{1,0:T(8,128)(2,1)} %pad_maximum_fusion), channel_id=1, source_target_pairs={{0,1},{1,0},{2,3},{3,2},{4,5},{5,4},{6,7},{7,6},{8,9},{9,8},{10,11... | collective-permute-start | bytes 2654216 | tf_op jit(solution)/shard_map/ppermute | solution.py:748
  73.0 25.7 %collective-permute-start.11 = (bf16[256,1152]{1,0:T(8,128)(2,1)}, bf16[256,1152]{1,0:T(8,128)(2,1)}, u32[]{:S(2)}, u32[]{:S(2)}) collective-permute-start(bf16[256,1152]{1,0:T(8,128)(2,1)} %bitcast.4.rest_2_.rest_4_.cot_ref), channel_id=1, source_target_pairs={{0,1},{1,0},{2,3},{3,2},{4,5},{5,4},{6,7},{7,6},{8,9},{9,8},{10,11... | collective-permute-start | bytes 1769480 | tf_op jit(solution)/shard_map/ppermute | solution.py:748
  73.5 16.4 %collective-permute-start.13 = (bf16[256,1152]{1,0:T(8,128)(2,1)}, bf16[256,1152]{1,0:T(8,128)(2,1)}, u32[]{:S(2)}, u32[]{:S(2)}) collective-permute-start(bf16[256,1152]{1,0:T(8,128)(2,1)} %bitcast.4.rest_2_.rest_4_.cot_ref), channel_id=1, source_target_pairs={{0,2},{1,3},{2,0},{3,1},{4,6},{5,7},{6,4},{7,5},{8,10},{9,11},{10,... | collective-permute-start | bytes 1769480 | tf_op jit(solution)/shard_map/ppermute | solution.py:748
  88.2 10.5 %collective-permute-start.10 = (bf16[256,1152]{1,0:T(8,128)(2,1)}, bf16[256,1152]{1,0:T(8,128)(2,1)}, u32[]{:S(2)}, u32[]{:S(2)}) collective-permute-start(bf16[256,1152]{1,0:T(8,128)(2,1)} %get-tuple-element.102.rest_0_), channel_id=1, source_target_pairs={{0,1},{1,0},{2,3},{3,2},{4,5},{5,4},{6,7},{7,6},{8,9},{9,8},{10,11... | collective-permute-start | bytes 1769480 | tf_op jit(solution)/shard_map/ppermute | solution.py:748
  88.7 21.5 %collective-permute-start.12 = (bf16[256,1152]{1,0:T(8,128)(2,1)}, bf16[256,1152]{1,0:T(8,128)(2,1)}, u32[]{:S(2)}, u32[]{:S(2)}) collective-permute-start(bf16[256,1152]{1,0:T(8,128)(2,1)} %get-tuple-element.102.rest_0_), channel_id=1, source_target_pairs={{0,2},{1,3},{2,0},{3,1},{4,6},{5,7},{6,4},{7,5},{8,10},{9,11},{10,... | collective-permute-start | bytes 1769480 | tf_op jit(solution)/shard_map/ppermute | solution.py:748
  110.2 6.4 %collective-permute-start.14 = (bf16[256,1152]{1,0:T(8,128)(2,1)}, bf16[256,1152]{1,0:T(8,128)(2,1)}, u32[]{:S(2)}, u32[]{:S(2)}) collective-permute-start(bf16[256,1152]{1,0:T(8,128)(2,1)} %collective-permute-done.12.rest_2_), channel_id=1, source_target_pairs={{0,1},{1,0},{2,3},{3,2},{4,5},{5,4},{6,7},{7,6},{8,9},{9,8},{10,11... | collective-permute-start | bytes 1769480 | tf_op jit(solution)/shard_map/ppermute | solution.py:748
  114.6 2.8 collective-permute-start.15
  135.0 103.4 %reduce-scatter.9.cloned.1.call-start = ((), (), s32[]{:S(2)}) async-start(), calls=%async_computation.7 | async-start | bytes 3538944 | tf_op jit(solution)/shard_map/reduce_scatter | solution.py:772
  140.8 2.7 copy-start.33
  140.8 2.7 collective-permute-start.16
  143.4 2.0 collective-permute-start.21
  143.7 14.8 %collective-permute-start.17 = (bf16[256,1152]{1,0:T(8,128)(2,1)S(1)}, bf16[256,1152]{1,0:T(8,128)(2,1)S(1)}, u32[]{:S(2)}, u32[]{:S(2)}) collective-permute-start(bf16[256,1152]{1,0:T(8,128)(2,1)S(1)} %add_convert_fusion.4), channel_id=1, source_target_pairs={{0,2},{1,3},{2,0},{3,1},{4,6},{5,7},{6,4},{7,5},{8,10},{9,11},{10,... | collective-permute-start | bytes 1769480 | tf_op jit(solution)/shard_map/ppermute | solution.py:748
  145.4 13.1 %copy-start.38 = (bf16[256,1152]{1,0:T(8,128)(2,1)}, bf16[256,1152]{1,0:T(8,128)(2,1)S(1)}, u32[]{:S(2)}) copy-start(bf16[256,1152]{1,0:T(8,128)(2,1)S(1)} %collective-permute-done.21.gn_near_ref) | copy-start | bytes 1769476
  197.1 69.7 %reduce-scatter.11.cloned.1.call-start = ((), (), s32[]{:S(2)}) async-start(), calls=%async_computation.10 | async-start | bytes 1492992
  202.4 5.2 %copy-start.32 = (bf16[288,1152]{1,0:T(8,128)(2,1)S(1)}, bf16[288,1152]{1,0:T(8,128)(2,1)}, u32[]{:S(2)}) copy-start(bf16[288,1152]{1,0:T(8,128)(2,1)} %get-tuple-element.143) | copy-start | bytes 1990660
  202.4 2.6 collective-permute-start.35
  203.1 4.6 %collective-permute-start.32 = (bf16[288,1152]{1,0:T(8,128)(2,1)}, bf16[288,1152]{1,0:T(8,128)(2,1)S(1)}, u32[]{:S(2)}, u32[]{:S(2)}) collective-permute-start(bf16[288,1152]{1,0:T(8,128)(2,1)} %get-tuple-element.144), channel_id=1, source_target_pairs={{0,1},{1,0},{2,3},{3,2},{4,5},{5,4},{6,7},{7,6},{8,9},{9,8},{10,11... | collective-permute-start | bytes 1990664 | tf_op jit(solution)/shard_map/ppermute | solution.py:748
  203.1 5.1 %collective-permute-start.31 = (bf16[288,1152]{1,0:T(8,128)(2,1)}, bf16[288,1152]{1,0:T(8,128)(2,1)S(1)}, u32[]{:S(2)}, u32[]{:S(2)}) collective-permute-start(bf16[288,1152]{1,0:T(8,128)(2,1)} %get-tuple-element.142), channel_id=1, source_target_pairs={{0,1},{1,0},{2,3},{3,2},{4,5},{5,4},{6,7},{7,6},{8,9},{9,8},{10,11... | collective-permute-start | bytes 1990664 | tf_op jit(solution)/shard_map/ppermute | solution.py:748
  203.6 4.6 %collective-permute-start.34 = (bf16[288,1152]{1,0:T(8,128)(2,1)}, bf16[288,1152]{1,0:T(8,128)(2,1)S(1)}, u32[]{:S(2)}, u32[]{:S(2)}) collective-permute-start(bf16[288,1152]{1,0:T(8,128)(2,1)} %get-tuple-element.146), channel_id=1, source_target_pairs={{0,1},{1,0},{2,3},{3,2},{4,5},{5,4},{6,7},{7,6},{8,9},{9,8},{10,11... | collective-permute-start | bytes 1990664 | tf_op jit(solution)/shard_map/ppermute | solution.py:748
  205.0 31.8 %copy-start.14 = (bf16[288,1152]{1,0:T(8,128)(2,1)S(1)}, bf16[288,1152]{1,0:T(8,128)(2,1)}, u32[]{:S(2)}) copy-start(bf16[288,1152]{1,0:T(8,128)(2,1)} %get-tuple-element.141.refs_0_) | copy-start | bytes 1990660
  205.0 31.8 %copy-start.15 = (bf16[288,1152]{1,0:T(8,128)(2,1)S(1)}, bf16[288,1152]{1,0:T(8,128)(2,1)}, u32[]{:S(2)}) copy-start(bf16[288,1152]{1,0:T(8,128)(2,1)} %get-tuple-element.145.refs_3_) | copy-start | bytes 1990660
  206.4 16.3 %collective-permute-start.36 = (bf16[288,1152]{1,0:T(8,128)(2,1)S(1)}, bf16[288,1152]{1,0:T(8,128)(2,1)S(1)}, u32[]{:S(2)}, u32[]{:S(2)}) collective-permute-start(bf16[288,1152]{1,0:T(8,128)(2,1)S(1)} %add_convert_fusion), channel_id=1, source_target_pairs={{0,2},{1,3},{2,0},{3,1},{4,6},{5,7},{6,4},{7,5},{8,10},{9,11},{10,... | collective-permute-start | bytes 1990664 | tf_op jit(solution)/shard_map/ppermute | solution.py:748
  207.8 29.0 %collective-permute-start.33 = (bf16[288,1152]{1,0:T(8,128)(2,1)S(1)}, bf16[288,1152]{1,0:T(8,128)(2,1)S(1)}, u32[]{:S(2)}, u32[]{:S(2)}) collective-permute-start(bf16[288,1152]{1,0:T(8,128)(2,1)S(1)} %add_convert_fusion.1), channel_id=1, source_target_pairs={{0,2},{1,3},{2,0},{3,1},{4,6},{5,7},{6,4},{7,5},{8,10},{9,11},{10,... | collective-permute-start | bytes 1990664 | tf_op jit(solution)/shard_map/ppermute | solution.py:748
  238.4 123.2 %all-gather.7.cloned.1.call-start = ((), (), s32[]{:S(2)}) async-start(), calls=%async_computation.8 | async-start | bytes 7464960 | tf_op jit(solution)/shard_map/all_gather | solution.py:777
  242.6 3.3 copy-start.31
  242.6 15.0 %copy-start.29 = (bf16[288,384]{1,0:T(8,128)(2,1)S(1)}, bf16[288,384]{1,0:T(8,128)(2,1)}, u32[]{:S(2)}) copy-start(bf16[288,384]{1,0:T(8,128)(2,1)} %slice_bitcast_fusion.3) | copy-start | bytes 663556
  244.6 14.0 %copy-start.20 = (bf16[256,768]{1,0:T(8,128)(2,1)}, bf16[256,768]{1,0:T(8,128)(2,1)S(1)}, u32[]{:S(2)}) copy-start(bf16[256,768]{1,0:T(8,128)(2,1)S(1)} %get-tuple-element.128.gkv_ref) | copy-start | bytes 1179652
  244.6 4.5 %collective-permute-start.29 = (bf16[288,768]{1,0:T(8,128)(2,1)S(1)}, bf16[288,768]{1,0:T(8,128)(2,1)S(1)}, u32[]{:S(2)}, u32[]{:S(2)}) collective-permute-start(bf16[288,768]{1,0:T(8,128)(2,1)S(1)} %get-tuple-element.137), channel_id=1, source_target_pairs={{0,1},{1,0},{2,3},{3,2},{4,5},{5,4},{6,7},{7,6},{8,9},{9,8},{10,11... | collective-permute-start | bytes 1327112 | tf_op jit(solution)/shard_map/ppermute | solution.py:748
  246.0 11.6 %collective-permute-start.27 = (bf16[576,384]{1,0:T(8,128)(2,1)S(1)}, bf16[576,384]{1,0:T(8,128)(2,1)S(1)}, u32[]{:S(2)}, u32[]{:S(2)}) collective-permute-start(bf16[576,384]{1,0:T(8,128)(2,1)S(1)} %slice_bitcast_fusion.2), channel_id=1, source_target_pairs={{0,0},{1,3},{2,2},{3,1},{4,7},{5,6},{6,5},{7,4},{8,8},{9,11},{10,1... | collective-permute-start | bytes 1327112 | tf_op jit(solution)/shard_map/ppermute | solution.py:1045
  249.1 9.5 %collective-permute-start.28 = (bf16[288,768]{1,0:T(8,128)(2,1)S(1)}, bf16[288,768]{1,0:T(8,128)(2,1)S(1)}, u32[]{:S(2)}, u32[]{:S(2)}) collective-permute-start(bf16[288,768]{1,0:T(8,128)(2,1)S(1)} %get-tuple-element.135), channel_id=1, source_target_pairs={{0,1},{1,0},{2,3},{3,2},{4,5},{5,4},{6,7},{7,6},{8,9},{9,8},{10,11... | collective-permute-start | bytes 1327112 | tf_op jit(solution)/shard_map/ppermute | solution.py:748
  249.3 15.6 %collective-permute-start.30 = (bf16[288,768]{1,0:T(8,128)(2,1)S(1)}, bf16[288,768]{1,0:T(8,128)(2,1)S(1)}, u32[]{:S(2)}, u32[]{:S(2)}) collective-permute-start(bf16[288,768]{1,0:T(8,128)(2,1)S(1)} %add_convert_fusion.5), channel_id=1, source_target_pairs={{0,2},{1,3},{2,0},{3,1},{4,6},{5,7},{6,4},{7,5},{8,10},{9,11},{10,... | collective-permute-start | bytes 1327112 | tf_op jit(solution)/shard_map/ppermute | solution.py:748
  268.4 7.3 %copy-start.36 = (bf16[768,1152]{1,0:T(8,128)(2,1)S(1)}, bf16[768,1152]{1,0:T(8,128)(2,1)}, u32[]{:S(2)}) copy-start(bf16[768,1152]{1,0:T(8,128)(2,1)} %down_ref.3) | copy-start | bytes 5308420
  268.4 7.3 %copy-start.40 = (bf16[2,256,768]{2,1,0:T(8,128)(2,1)S(1)}, bf16[2,256,768]{2,1,0:T(8,128)(2,1)}, u32[]{:S(2)}) copy-start(bf16[2,256,768]{2,1,0:T(8,128)(2,1)} %get-tuple-element.104.act_in) | copy-start | bytes 2359300
  271.6 13.1 %collective-permute-start.19 = (bf16[256,1152]{1,0:T(8,128)(2,1)S(1)}, bf16[256,1152]{1,0:T(8,128)(2,1)S(1)}, u32[]{:S(2)}, u32[]{:S(2)}) collective-permute-start(bf16[256,1152]{1,0:T(8,128)(2,1)S(1)} %slice.69), channel_id=1, source_target_pairs={{0,1},{1,0},{2,3},{3,2},{4,5},{5,4},{6,7},{7,6},{8,9},{9,8},{10,11... | collective-permute-start | bytes 1769480 | tf_op jit(solution)/shard_map/ppermute | solution.py:748
  275.7 2.5 copy-start.2
  277.9 36.2 %collective-permute-start.18 = (bf16[256,1152]{1,0:T(8,128)(2,1)}, bf16[256,1152]{1,0:T(8,128)(2,1)}, u32[]{:S(2)}, u32[]{:S(2)}) collective-permute-start(bf16[256,1152]{1,0:T(8,128)(2,1)} %slice.67), channel_id=1, source_target_pairs={{0,1},{1,0},{2,3},{3,2},{4,5},{5,4},{6,7},{7,6},{8,9},{9,8},{10,11... | collective-permute-start | bytes 1769480 | tf_op jit(solution)/shard_map/ppermute | solution.py:748
  279.1 5.4 %copy-start.34 = (f32[1,1152]{1,0:T(1,128)S(1)}, f32[1,1152]{1,0:T(1,128)}, u32[]{:S(2)}) copy-start(f32[1,1152]{1,0:T(1,128)} %get-tuple-element.133) | copy-start | bytes 13828
  284.5 6.1 %copy-start.35 = (f32[1,1152]{1,0:T(1,128)S(1)}, f32[1,1152]{1,0:T(1,128)}, u32[]{:S(2)}) copy-start(f32[1,1152]{1,0:T(1,128)} %get-tuple-element.133) | copy-start | bytes 13828
  284.6 6.0 %collective-permute-start.22 = (f32[2,1152]{1,0:T(2,128)S(1)}, f32[2,1152]{1,0:T(2,128)S(1)}, u32[]{:S(2)}, u32[]{:S(2)}) collective-permute-start(f32[2,1152]{1,0:T(2,128)S(1)} %pad_maximum_fusion.2), channel_id=1, source_target_pairs={{0,1},{1,0},{2,3},{3,2},{4,5},{5,4},{6,7},{7,6},{8,9},{9,8},{10,11... | collective-permute-start | bytes 27656 | tf_op jit(solution)/shard_map/ppermute | solution.py:748
  285.6 28.5 %copy-start.26 = (f32[256,1152]{1,0:T(8,128)S(1)}, f32[256,1152]{1,0:T(8,128)}, u32[]{:S(2)}) copy-start(f32[256,1152]{1,0:T(8,128)} %get-tuple-element.99.mid_ref) | copy-start | bytes 3538948
  285.6 28.5 %copy-start.28 = (bf16[512,1152]{1,0:T(8,128)(2,1)S(1)}, bf16[512,1152]{1,0:T(8,128)(2,1)}, u32[]{:S(2)}) copy-start(bf16[512,1152]{1,0:T(8,128)(2,1)} %copy-done.27) | copy-start | bytes 3538948
  285.6 28.5 %collective-permute-start.20 = (bf16[256,1152]{1,0:T(8,128)(2,1)}, bf16[256,1152]{1,0:T(8,128)(2,1)S(1)}, u32[]{:S(2)}, u32[]{:S(2)}) collective-permute-start(bf16[256,1152]{1,0:T(8,128)(2,1)} %add_convert_fusion.3), channel_id=1, source_target_pairs={{0,2},{1,3},{2,0},{3,1},{4,6},{5,7},{6,4},{7,5},{8,10},{9,11},{10,... | collective-permute-start | bytes 1769480 | tf_op jit(solution)/shard_map/ppermute | solution.py:748
  286.8 21.3 %all-to-all-start = ((bf16[8,216,128]{2,1,0:T(8,128)(2,1)}), bf16[8,216,128]{2,1,0:T(8,128)(2,1)S(1)}, u32[]{:S(2)}, u32[]{:S(2)}) async-start(bf16[8,216,128]{2,1,0:T(8,128)(2,1)} %bitcast.14), calls=%async_computation.2 | async-start | bytes 884736 | tf_op jit(solution)/shard_map/all_to_all | solution.py:1173
  290.6 9.9 %collective-permute-start.23 = (f32[2,1152]{1,0:T(2,128)S(1)}, f32[2,1152]{1,0:T(2,128)S(1)}, u32[]{:S(2)}, u32[]{:S(2)}) collective-permute-start(f32[2,1152]{1,0:T(2,128)S(1)} %fusion.7), channel_id=1, source_target_pairs={{0,2},{1,3},{2,0},{3,1},{4,6},{5,7},{6,4},{7,5},{8,10},{9,11},{10,... | collective-permute-start | bytes 27656 | tf_op jit(solution)/shard_map/ppermute | solution.py:748
  300.6 3.0 collective-permute-start.24
  303.6 3.2 collective-permute-start.25
  306.7 9.5 %collective-permute-start.26 = (f32[2,1152]{1,0:T(2,128)S(1)}, f32[2,1152]{1,0:T(2,128)S(1)}, u32[]{:S(2)}, u32[]{:S(2)}) collective-permute-start(f32[2,1152]{1,0:T(2,128)S(1)} %add.136), channel_id=1, source_target_pairs={{0,16},{4,20},{8,24},{12,28},{16,0},{20,4},{24,8},{28,12},{1,17},{... | collective-permute-start | bytes 27656 | tf_op jit(solution)/shard_map/ppermute | solution.py:752
  309.0 21.9 %all-to-all-start.1 = ((bf16[8,216,128]{2,1,0:T(8,128)(2,1)}), bf16[8,216,128]{2,1,0:T(8,128)(2,1)S(1)}, u32[]{:S(2)}, u32[]{:S(2)}) async-start(bf16[8,216,128]{2,1,0:T(8,128)(2,1)} %broadcast_in_dim.40), calls=%async_computation.3 | async-start | bytes 884736 | tf_op jit(solution)/shard_map/all_to_all | solution.py:1173
  (22 other events, 33.4 us)
Sparse Core Ops, SparseCore 0:
  29.1 38.4 all-gather.4
  69.7 28.9 all-gather.8
  135.1 60.2 reduce-scatter.6
  198.1 38.1 reduce-scatter.8
  239.1 27.6 reduce-scatter.10
  268.8 92.7 all-gather.6

commit v3 on v2

--- a/solution.py
+++ b/solution.py
@@ -1036,7 +1036,7 @@
         act_parts = [activated[: 2 * count], activated[2 * count :]]
     from_near = hop(to_near, 1)
     feed_sum = scatter(feed_tiles)
-    down_sum = feed_sum[2 * rows :]
+    head_sum = feed_sum[2 * rows : 2 * rows + 16]
     pairs = []
     for index in range(n_ctx):
         for source in range(n_shard):
@@ -1128,7 +1128,8 @@
         sine,
         *out_weights,
     )
-    own_kv = scatter(after(grad_kv, down_sum).reshape(n_ctx, count, 2 * kvw))
+    grad_kv, head_sum = lax.optimization_barrier((grad_kv, head_sum))
+    own_kv = scatter(grad_kv.reshape(n_ctx, count, 2 * kvw))
 
     def stack(parts, breadth, name):
         height = sum(part.shape[0] * part.shape[1] for part in parts[::3]) // breadth
@@ -1165,7 +1166,9 @@
         name="kv_back",
     )
     sum_kv = stack(reduce(kv_blocks), LANES, "stack_kv").reshape(n_ctx, -1, LANES)
-    shares = jnp.concatenate([gate_up_sum, down_sum, jnp.zeros_like(mixed_sum)])
+    shares = jnp.concatenate(
+        [gate_up_sum, head_sum, feed_sum[2 * rows + 16 :], jnp.zeros_like(mixed_sum)]
+    )
     shares = lax.dynamic_update_slice_in_dim(after(shares, sum_kv), mixed_sum, 3 * rows, 0)
     gathered = collect(shares[None])
 

time: 378 us -> 378 us (level)
    unnamed x82 -> x80, local copies, waits for them, and re-layouts: 11.3 us -> 11.3 us
where the time goes in v3:
time: 378 us; the launch traced here: 377 us
  waiting for transfers between devices  183 us (48%)
  Pallas kernels  96.9 us (26%)
  starting transfers between devices  44.5 us (12%)
  local copies, waits for them, and re-layouts  19.6 us (5%)
  between operations  14.6 us (4%)
  other arithmetic  14.2 us (4%)
  matrix products  4.25 us (1%)
    ppermute x33, waiting for transfers between devices, hop(): return lax.ppermute(value, 'shard', pairs)  98.8 us
    all_gather x3, waiting for transfers between devices, collect(): lax.all_gather(value, 'ctx', axis=0, axis_index_groups=[order], tiled=True)  38.5 us
    ppermute x33, starting transfers between devices, hop(): return lax.ppermute(value, 'shard', pairs)  29.2 us
    pallas_call x8, Pallas kernels, call_once(): pl.pallas_call(kernel, out_shape=tuple((jax.ShapeDtypeStruct(shape, dtype...  27.1 us
    pallas_call x1, Pallas kernels, on_device(): pl.pallas_call(functools.partial(attend_back_kernel, **shared), out_shape...  19.5 us
    pallas_call x1, Pallas kernels, on_device(): pl.pallas_call(functools.partial(feed_far_kernel, per_shard=per_shard), o...  17.5 us
    reduce_scatter x2, waiting for transfers between devices, scatter(): lax.psum_scatter(value, 'ctx', scatter_dimension=0, axis_index_groups=[or...  16.6 us
    all_to_all x2, waiting for transfers between devices, exchange(): return lax.all_to_all(value, 'ctx', split_axis=0, concat_axis=0, tiled=True)  13.8 us
  transfers between devices with their start and end apart: 45, of which 24 were waited for; matrix products, arithmetic and copies ran while one was open for 6% of the time, Pallas kernels for 18%

profile of v3, /device:TPU:9, one launch (start us, length us, event | category | flops | bytes accessed | tf_op | source)
XLA Modules:
  0.0 377.4 jit_solution(5348687087672897596)
XLA Ops:
  8.0 1.1 fusion.2.rest_0_.rest_4_
  9.1 1.3 collective-permute-start.1
  11.4 1.4 dynamic-slice_select_fusion.1
  13.4 1.3 constant_dynamic-slice_fusion
  14.7 1.0 pad_maximum_fusion
  15.7 5.0 %collective-permute-done.1.rest_2_.rest_6_ = bf16[304,768]{1,0:T(8,128)(2,1)S(1)} collective-permute-done((bf16[304,768]{1,0:T(8,128)(2,1)S(1)}, bf16[304,768]{1,0:T(8,128)(2,1)S(1)}, u32[]{:S(2)}, u32[]{:S(2)}) %collective-permute-start.1) | collective-permute-done | bytes 466976 | tf_op jit(solution)/shard_map/ppermute | solution.py:748
  20.7 1.5 collective-permute-start.2
  22.3 1.3 fusion.3
  24.6 4.3 %keys.1 = (bf16[256,1152]{1,0:T(8,128)(2,1)}, bf16[256,768]{1,0:T(8,128)(2,1)}, f32[1,1152]{1,0:T(1,128)}, f32[1,1152]{1,0:T(1,128)}) custom-call(s32[2]{0:T(128)} %pad_add_fusion.ids_ref.table_ref, bf16[256,1152]{1,0:T(8,128)(2,1)} %bitcast.36, f32[256,128]{1,0:T(8,128)} %get-tuple-element.91.cos_ref, f32[256,128]{1,0:T(8,128)} %get-tuple-element.92.sin_ref, ...), custom_call_target="tpu_custom_call" | custom-call | flops 452984832 | bytes 4987648 | tf_op jit(solution)/shard_map/keys/pallas_call | solution.py:62
  29.0 1.3 collective-permute-start.4
  30.3 19.8 %collective-permute-done.4.rest_2_ = bf16[288,1536]{1,0:T(8,128)(2,1)S(1)} collective-permute-done((bf16[288,1536]{1,0:T(8,128)(2,1)S(1)}, bf16[288,1536]{1,0:T(8,128)(2,1)S(1)}, u32[]{:S(2)}, u32[]{:S(2)}) %collective-permute-start.4) | collective-permute-done | bytes 884768 | tf_op jit(solution)/shard_map/ppermute | solution.py:748
  50.1 1.0 collective-permute-start.5
  51.1 2.0 collective-permute-done.5.rest_3_
  54.6 1.2 collective-permute-start.7
  58.5 1.1 copy-done.16
  59.5 2.0 queries.1.q_ref
  62.3 8.9 %collective-permute-done.7.rest_2_ = bf16[288,1152]{1,0:T(8,128)(2,1)S(1)} collective-permute-done((bf16[288,1152]{1,0:T(8,128)(2,1)}, bf16[288,1152]{1,0:T(8,128)(2,1)S(1)}, u32[]{:S(2)}, u32[]{:S(2)}) %collective-permute-start.7) | collective-permute-done | bytes 663584 | tf_op jit(solution)/shard_map/ppermute | solution.py:748
  73.5 1.2 collective-permute-start.13
  74.7 1.1 collective-permute-done.8.rest_3_
  75.8 12.5 %attend.1 = (f32[1152,256]{1,0:T(8,128)}, bf16[256,1152]{1,0:T(8,128)(2,1)}, f32[8,768]{1,0:T(8,128)}, f32[256,1152]{1,0:T(8,128)}, bf16[256,1152]{1,0:T(8,128)(2,1)}, /*index=5*/bf16[6,64,768]{2,1,0:T(8,128)(2,1)}) custom-call(s32[2]{0:T(128)} %pad_add_fusion.ids_ref.table_ref, bf16[256,1152]{1,0:T(8,128)(2,1)} %copy-done.18, ...), custom_call_target="tpu_custom_call" | custom-call | flops 2415919104 | bytes 12000000 | tf_op jit(solution)/shard_map/attend/pallas_call | solution.py:871
  88.7 1.2 collective-permute-start.12
  89.9 8.8 %all-gather.9.cloned.1.call-done = bf16[2304,384]{1,0:T(8,128)(2,1)} async-done(((bf16[288,384]{1,0:T(8,128)(2,1)}), bf16[2304,384]{1,0:T(8,128)(2,1)}) %all-gather.9.cloned.1.call-update) | async-done | bytes 1769488 | tf_op jit(solution)/shard_map/all_gather | solution.py:777
  98.7 11.4 %feed_near.1 = (bf16[1152,768]{1,0:T(8,128)(2,1)}, bf16[1152,768]{1,0:T(8,128)(2,1)}, bf16[2,256,768]{2,1,0:T(8,128)(2,1)}, bf16[2,256,768]{2,1,0:T(8,128)(2,1)}...) custom-call(s32[2]{0:T(128)} %pad_add_fusion.ids_ref.table_ref, bf16[288,3072]{1,0:T(8,128)(2,1)} %own_gate_ref.1, ...), custom_call_target="tpu_custom_call" | custom-call | flops 4529848320 | bytes 12000000 | tf_op jit(solution)/shard_map/feed_near/pallas_call | solution.py:920
  110.2 4.4 %collective-permute-start.14 = (bf16[256,1152]{1,0:T(8,128)(2,1)}, bf16[256,1152]{1,0:T(8,128)(2,1)}, u32[]{:S(2)}, u32[]{:S(2)}) collective-permute-start(bf16[256,1152]{1,0:T(8,128)(2,1)} %collective-permute-done.12.rest_2_), channel_id=1, source_target_pairs={{0,1},{1,0},{2,3},{3,2},{4,5},{5,4},{6,7},{7,6},{8,9},{9,8},{10,11... | collective-permute-start | bytes 1769480 | tf_op jit(solution)/shard_map/ppermute | solution.py:748
  114.7 1.9 collective-permute-done.14.rest_3_
  117.4 17.5 %feed_far.1 = (bf16[8,864,384]{2,1,0:T(8,128)(2,1)}, bf16[512,768]{1,0:T(8,128)(2,1)}, bf16[512,768]{1,0:T(8,128)(2,1)}, bf16[512,768]{1,0:T(8,128)(2,1)}) custom-call(s32[2]{0:T(128)} %pad_add_fusion.ids_ref.table_ref, bf16[1152,768]{1,0:T(8,128)(2,1)} %get-tuple-element.106.gate_mat_ref, bf16[1152,768]{1,0:T(8,128)(2,1)} %get-tuple-element.107.up_mat_ref, ...), custom_call_target="tpu_custom_call" | custom-call | flops 8153726976 | bytes 25000000 | tf_op jit(solution)/shard_map/feed_far/pallas_call | solution.py:960
  135.2 5.6 %normed_back.1 = (bf16[256,1152]{1,0:T(8,128)(2,1)}, bf16[256,1152]{1,0:T(8,128)(2,1)}) custom-call(bf16[512,768]{1,0:T(8,128)(2,1)} %get-tuple-element.115.gate_ref, bf16[512,768]{1,0:T(8,128)(2,1)} %get-tuple-element.116.up_ref, bf16[1152,768]{1,0:T(8,128)(2,1)} %get-tuple-element.106.gate_mat_ref, bf16[1152,768]{1,0:T(8,128)(2,1)} %get-tuple-element.107.up_mat_ref), custom_call_target="tpu_custom_call" | custom-call | flops 1811939328 | bytes 5179648 | tf_op jit(solution)/shard_map/normed_back/pallas_call | solution.py:62
  141.2 2.1 slice_bitcast_fusion
  143.7 1.2 collective-permute-start.17
  145.4 13.1 %collective-permute-done.17.gn_far_ref = bf16[256,1152]{1,0:T(8,128)(2,1)S(1)} collective-permute-done((bf16[256,1152]{1,0:T(8,128)(2,1)S(1)}, bf16[256,1152]{1,0:T(8,128)(2,1)S(1)}, u32[]{:S(2)}, u32[]{:S(2)}) %collective-permute-start.17) | collective-permute-done | bytes 589856 | tf_op jit(solution)/shard_map/ppermute | solution.py:748
  159.3 19.5 %attend_back.1 = (bf16[256,1152]{1,0:T(8,128)(2,1)}, bf16[2048,768]{1,0:T(8,128)(2,1)}, bf16[256,1152]{1,0:T(8,128)(2,1)}, f32[256,1152]{1,0:T(8,128)}, f32[1,1152]{1,0:T(1,128)}) custom-call(s32[2]{0:T(128)} %pad_add_fusion.ids_ref.table_ref, bf16[2048,768]{1,0:T(8,128)(2,1)} %all-gather.5.cloned.1.call-done.kv_ref, ...), custom_call_target="tpu_custom_call" | custom-call | flops 6039797760 | bytes 14000000 | tf_op jit(solution)/shard_map/attend_back/pallas_call | solution.py:1066
  178.8 16.6 %reduce-scatter.7.cloned.1.call-done = bf16[1,864,384]{2,1,0:T(8,128)(2,1)} async-done(((bf16[8,864,384]{2,1,0:T(8,128)(2,1)}), bf16[1,864,384]{2,1,0:T(8,128)(2,1)}) %reduce-scatter.7.cloned.1.call-update) | async-done | bytes 663568 | tf_op jit(solution)/shard_map/reduce_scatter | solution.py:772
  196.2 5.3 %weight_grads.1 = (bf16[288,1152]{1,0:T(8,128)(2,1)}, bf16[288,1152]{1,0:T(8,128)(2,1)}, bf16[288,1152]{1,0:T(8,128)(2,1)}, bf16[288,1152]{1,0:T(8,128)(2,1)}, b...) custom-call(s32[2]{0:T(128)} %pad_add_fusion.ids_ref.table_ref, ...), custom_call_target="tpu_custom_call" | custom-call | flops 1358954496 | bytes 9308416 | tf_op jit(solution)/shard_map/weight_grads/pallas_call | solution.py:62
  202.7 1.4 collective-permute-done.35
  204.1 1.5 add_convert_fusion
  205.6 1.2 collective-permute-start.36
  207.4 14.5 %collective-permute-done.36.refs_5_ = bf16[288,1152]{1,0:T(8,128)(2,1)S(1)} collective-permute-done((bf16[288,1152]{1,0:T(8,128)(2,1)S(1)}, bf16[288,1152]{1,0:T(8,128)(2,1)S(1)}, u32[]{:S(2)}, u32[]{:S(2)}) %collective-permute-start.36) | collective-permute-done | bytes 663584 | tf_op jit(solution)/shard_map/ppermute | solution.py:748
  221.9 14.2 %collective-permute-done.33.refs_2_ = bf16[288,1152]{1,0:T(8,128)(2,1)S(1)} collective-permute-done((bf16[288,1152]{1,0:T(8,128)(2,1)S(1)}, bf16[288,1152]{1,0:T(8,128)(2,1)S(1)}, u32[]{:S(2)}, u32[]{:S(2)}) %collective-permute-start.33) | collective-permute-done | bytes 663584 | tf_op jit(solution)/shard_map/ppermute | solution.py:748
  236.1 1.6 stack_mixed.1
  239.9 1.1 copy-done.17
  241.0 1.0 copy-done.25
  242.0 2.0 kv_back.1
  244.0 1.2 collective-permute-start.29
  245.3 3.1 collective-permute-start.27
  248.9 8.0 %collective-permute-done.27 = bf16[576,384]{1,0:T(8,128)(2,1)S(1)} collective-permute-done((bf16[576,384]{1,0:T(8,128)(2,1)S(1)}, bf16[576,384]{1,0:T(8,128)(2,1)S(1)}, u32[]{:S(2)}, u32[]{:S(2)}) %collective-permute-start.27) | collective-permute-done | bytes 442400 | tf_op jit(solution)/shard_map/ppermute | solution.py:1045
  256.9 1.1 maximum_maximum_fusion.1
  258.1 5.7 %collective-permute-done.30.refs_2_ = bf16[288,768]{1,0:T(8,128)(2,1)S(1)} collective-permute-done((bf16[288,768]{1,0:T(8,128)(2,1)S(1)}, bf16[288,768]{1,0:T(8,128)(2,1)S(1)}, u32[]{:S(2)}, u32[]{:S(2)}) %collective-permute-start.30) | collective-permute-done | bytes 442400 | tf_op jit(solution)/shard_map/ppermute | solution.py:748
  264.7 2.1 reduce-scatter.11.cloned.1.call-done
  266.8 1.6 constant_dynamic-update-slice_fusion
  268.5 3.0 convolution_convert_fusion
  271.6 4.2 %collective-permute-start.19 = (bf16[256,1152]{1,0:T(8,128)(2,1)S(1)}, bf16[256,1152]{1,0:T(8,128)(2,1)S(1)}, u32[]{:S(2)}, u32[]{:S(2)}) collective-permute-start(bf16[256,1152]{1,0:T(8,128)(2,1)S(1)} %slice.75), channel_id=1, source_target_pairs={{0,1},{1,0},{2,3},{3,2},{4,5},{5,4},{6,7},{7,6},{8,9},{9,8},{10,11... | collective-permute-start | bytes 1769480 | tf_op jit(solution)/shard_map/ppermute | solution.py:748
  275.8 1.2 convolution_convert_fusion.1
  279.2 5.4 %grad_inputs.1 = (bf16[256,1152]{1,0:T(8,128)(2,1)}, f32[1,1152]{1,0:T(1,128)S(1)}) custom-call(s32[2]{0:T(128)S(1)} %copy-done.23, bf16[256,1152]{1,0:T(8,128)(2,1)S(1)} %copy-done.19, bf16[256,768]{1,0:T(8,128)(2,1)S(1)} %copy-done.21, bf16[256,1152]{1,0:T(8,128)(2,1)S(1)} %bitcast.38, f32[1,1152]{1,0:T(1,128)S(1)} %copy-done.24, ...), custom_call_target="tpu_custom_call" | custom-call | flops 1132462080 | bytes 4592128 | tf_op jit(solution)/shard_map/grad_inputs/pallas_call | solution.py:62
  285.7 1.2 collective-permute-start.20
  286.9 3.8 %all-to-all-start = ((bf16[8,216,128]{2,1,0:T(8,128)(2,1)}), bf16[8,216,128]{2,1,0:T(8,128)(2,1)S(1)}, u32[]{:S(2)}, u32[]{:S(2)}) async-start(bf16[8,216,128]{2,1,0:T(8,128)(2,1)} %bitcast.15), calls=%async_computation.2 | async-start | bytes 884736 | tf_op jit(solution)/shard_map/all_to_all | solution.py:1176
  291.2 9.4 %collective-permute-done.23 = f32[2,1152]{1,0:T(2,128)S(1)} collective-permute-done((f32[2,1152]{1,0:T(2,128)S(1)}, f32[2,1152]{1,0:T(2,128)S(1)}, u32[]{:S(2)}, u32[]{:S(2)}) %collective-permute-start.23) | collective-permute-done | bytes 9248 | tf_op jit(solution)/shard_map/ppermute | solution.py:748
  301.1 2.6 collective-permute-done.24
  304.2 2.6 collective-permute-done.25
  306.8 1.4 collective-permute-start.26
  309.1 5.1 %all-to-all-start.1 = ((bf16[8,216,128]{2,1,0:T(8,128)(2,1)}), bf16[8,216,128]{2,1,0:T(8,128)(2,1)S(1)}, u32[]{:S(2)}, u32[]{:S(2)}) async-start(bf16[8,216,128]{2,1,0:T(8,128)(2,1)} %broadcast_in_dim.40), calls=%async_computation.3 | async-start | bytes 884736 | tf_op jit(solution)/shard_map/all_to_all | solution.py:1176
  314.2 2.1 fusion.1
  317.1 13.8 %all-to-all-done.1 = bf16[8,216,128]{2,1,0:T(8,128)(2,1)S(1)} async-done(((bf16[8,216,128]{2,1,0:T(8,128)(2,1)}), bf16[8,216,128]{2,1,0:T(8,128)(2,1)S(1)}, u32[]{:S(2)}, u32[]{:S(2)}) %all-to-all-start.1) | async-done | bytes 442400 | tf_op jit(solution)/shard_map/all_to_all | solution.py:1176
  332.0 29.7 %all-gather.7.cloned.1.call-done.gate_up_ref.down_in_ref.mixed_ref = bf16[8,1080,384]{2,1,0:T(8,128)(2,1)} async-done(((bf16[1,1080,384]{2,1,0:T(8,128)(2,1)}), bf16[8,1080,384]{2,1,0:T(8,128)(2,1)}) %all-gather.7.cloned.1.call-update) | async-done | bytes 6635536 | tf_op jit(solution)/shard_map/all_gather | solution.py:777
  361.7 8.9 %widen.1 = (f32[288,3072]{1,0:T(8,128)}, f32[288,3072]{1,0:T(8,128)}, f32[768,1152]{1,0:T(8,128)}, f32[288,1152]{1,0:T(8,128)}, f32[288,1152]{1,0:T(8,128)}) custom-call(s32[2]{0:T(128)} %pad_add_fusion.ids_ref.table_ref, bf16[8,1080,384]{2,1,0:T(8,128)(2,1)} %all-gather.7.cloned.1.call-done.gate_up_ref.down_in_ref.mixed_ref, ...), custom_call_target="tpu_custom_call" | custom-call | flops 1000000 | bytes 20000000 | tf_op jit(solution)/shard_map/widen/pallas_call | solution.py:1212
  (168 shorter events, 28.0 us)
Async XLA Ops:
  7.2 68.6 %all-gather.5.cloned.1.call-start = ((), (), s32[]{:S(2)}) async-start(), calls=%async_computation.5 | async-start | bytes 3538944 | tf_op jit(solution)/shard_map/all_gather | solution.py:777
  9.1 6.6 %copy-start = (bf16[304,768]{1,0:T(8,128)(2,1)}, bf16[304,768]{1,0:T(8,128)(2,1)S(1)}, u32[]{:S(2)}) copy-start(bf16[304,768]{1,0:T(8,128)(2,1)S(1)} %fusion.2.rest_0_.rest_4_) | copy-start | bytes 1400836
  9.1 11.6 %collective-permute-start.1 = (bf16[304,768]{1,0:T(8,128)(2,1)S(1)}, bf16[304,768]{1,0:T(8,128)(2,1)S(1)}, u32[]{:S(2)}, u32[]{:S(2)}) collective-permute-start(bf16[304,768]{1,0:T(8,128)(2,1)S(1)} %fusion.2.rest_0_.rest_4_), channel_id=1, source_target_pairs={{0,2},{1,3},{2,0},{3,1},{4,6},{5,7},{6,4},{7,5},{8,10},{9,11},{10,... | collective-permute-start | bytes 1400840 | tf_op jit(solution)/shard_map/ppermute | solution.py:748
  10.4 13.2 %collective-permute-start = (bf16[304,768]{1,0:T(8,128)(2,1)S(1)}, bf16[304,768]{1,0:T(8,128)(2,1)S(1)}, u32[]{:S(2)}, u32[]{:S(2)}) collective-permute-start(bf16[304,768]{1,0:T(8,128)(2,1)S(1)} %fusion.2.rest_0_.rest_4_), channel_id=1, source_target_pairs={{0,1},{1,0},{2,3},{3,2},{4,5},{5,4},{6,7},{7,6},{8,9},{9,8},{10,11... | collective-permute-start | bytes 1400840 | tf_op jit(solution)/shard_map/ppermute | solution.py:748
  13.4 10.1 %copy-start.29 = (bf16[288,1152]{1,0:T(8,128)(2,1)S(1)}, bf16[288,1152]{1,0:T(8,128)(2,1)}, u32[]{:S(2)}) copy-start(bf16[288,1152]{1,0:T(8,128)(2,1)} %param.15) | copy-start | bytes 1990660
  20.7 3.0 copy-start.3
  20.7 3.0 collective-permute-start.2
  24.6 32.1 %copy-start.22 = (s32[2]{0:T(128)S(1)}, s32[2]{0:T(128)}, u32[]{:S(2)}) copy-start(s32[2]{0:T(128)} %pad_add_fusion.ids_ref.table_ref) | copy-start | bytes 28
  28.9 69.8 %all-gather.9.cloned.1.call-start = ((), (), s32[]{:S(2)}) async-start(), calls=%async_computation.9 | async-start | bytes 1990656 | tf_op jit(solution)/shard_map/all_gather | solution.py:777
  29.0 21.1 %collective-permute-start.4 = (bf16[288,1536]{1,0:T(8,128)(2,1)S(1)}, bf16[288,1536]{1,0:T(8,128)(2,1)S(1)}, u32[]{:S(2)}, u32[]{:S(2)}) collective-permute-start(bf16[288,1536]{1,0:T(8,128)(2,1)S(1)} %maximum_maximum_fusion.rest_0_), channel_id=1, source_target_pairs={{0,2},{1,3},{2,0},{3,1},{4,6},{5,7},{6,4},{7,5},{8,10},{9,11},{10,... | collective-permute-start | bytes 2654216 | tf_op jit(solution)/shard_map/ppermute | solution.py:748
  50.1 3.1 collective-permute-start.5
  53.9 141.5 %reduce-scatter.7.cloned.1.call-start = ((), (), s32[]{:S(2)}) async-start(), calls=%async_computation.6 | async-start | bytes 5971968 | tf_op jit(solution)/shard_map/reduce_scatter | solution.py:772
  54.2 2.5 collective-permute-start.3
  54.6 16.6 %collective-permute-start.7 = (bf16[288,1152]{1,0:T(8,128)(2,1)}, bf16[288,1152]{1,0:T(8,128)(2,1)S(1)}, u32[]{:S(2)}, u32[]{:S(2)}) collective-permute-start(bf16[288,1152]{1,0:T(8,128)(2,1)} %rest_0_.3), channel_id=1, source_target_pairs={{0,2},{1,3},{2,0},{3,1},{4,6},{5,7},{6,4},{7,5},{8,10},{9,11},{10,... | collective-permute-start | bytes 1990664 | tf_op jit(solution)/shard_map/ppermute | solution.py:748
  55.8 18.9 %collective-permute-start.6 = (bf16[288,1152]{1,0:T(8,128)(2,1)}, bf16[288,1152]{1,0:T(8,128)(2,1)}, u32[]{:S(2)}, u32[]{:S(2)}) collective-permute-start(bf16[288,1152]{1,0:T(8,128)(2,1)} %rest_0_.3), channel_id=1, source_target_pairs={{0,1},{1,0},{2,3},{3,2},{4,5},{5,4},{6,7},{7,6},{8,9},{9,8},{10,11... | collective-permute-start | bytes 1990664 | tf_op jit(solution)/shard_map/ppermute | solution.py:748
  72.0 3.7 collective-permute-start.8
  73.0 25.7 %collective-permute-start.9 = (bf16[288,1536]{1,0:T(8,128)(2,1)}, bf16[288,1536]{1,0:T(8,128)(2,1)}, u32[]{:S(2)}, u32[]{:S(2)}) collective-permute-start(bf16[288,1536]{1,0:T(8,128)(2,1)} %pad_maximum_fusion), channel_id=1, source_target_pairs={{0,1},{1,0},{2,3},{3,2},{4,5},{5,4},{6,7},{7,6},{8,9},{9,8},{10,11... | collective-permute-start | bytes 2654216 | tf_op jit(solution)/shard_map/ppermute | solution.py:748
  73.0 25.7 %collective-permute-start.11 = (bf16[256,1152]{1,0:T(8,128)(2,1)}, bf16[256,1152]{1,0:T(8,128)(2,1)}, u32[]{:S(2)}, u32[]{:S(2)}) collective-permute-start(bf16[256,1152]{1,0:T(8,128)(2,1)} %bitcast.4.rest_2_.rest_4_.cot_ref), channel_id=1, source_target_pairs={{0,1},{1,0},{2,3},{3,2},{4,5},{5,4},{6,7},{7,6},{8,9},{9,8},{10,11... | collective-permute-start | bytes 1769480 | tf_op jit(solution)/shard_map/ppermute | solution.py:748
  73.5 16.4 %collective-permute-start.13 = (bf16[256,1152]{1,0:T(8,128)(2,1)}, bf16[256,1152]{1,0:T(8,128)(2,1)}, u32[]{:S(2)}, u32[]{:S(2)}) collective-permute-start(bf16[256,1152]{1,0:T(8,128)(2,1)} %bitcast.4.rest_2_.rest_4_.cot_ref), channel_id=1, source_target_pairs={{0,2},{1,3},{2,0},{3,1},{4,6},{5,7},{6,4},{7,5},{8,10},{9,11},{10,... | collective-permute-start | bytes 1769480 | tf_op jit(solution)/shard_map/ppermute | solution.py:748
  88.3 10.5 %collective-permute-start.10 = (bf16[256,1152]{1,0:T(8,128)(2,1)}, bf16[256,1152]{1,0:T(8,128)(2,1)}, u32[]{:S(2)}, u32[]{:S(2)}) collective-permute-start(bf16[256,1152]{1,0:T(8,128)(2,1)} %get-tuple-element.103.rest_0_), channel_id=1, source_target_pairs={{0,1},{1,0},{2,3},{3,2},{4,5},{5,4},{6,7},{7,6},{8,9},{9,8},{10,11... | collective-permute-start | bytes 1769480 | tf_op jit(solution)/shard_map/ppermute | solution.py:748
  88.7 21.5 %collective-permute-start.12 = (bf16[256,1152]{1,0:T(8,128)(2,1)}, bf16[256,1152]{1,0:T(8,128)(2,1)}, u32[]{:S(2)}, u32[]{:S(2)}) collective-permute-start(bf16[256,1152]{1,0:T(8,128)(2,1)} %get-tuple-element.103.rest_0_), channel_id=1, source_target_pairs={{0,2},{1,3},{2,0},{3,1},{4,6},{5,7},{6,4},{7,5},{8,10},{9,11},{10,... | collective-permute-start | bytes 1769480 | tf_op jit(solution)/shard_map/ppermute | solution.py:748
  110.2 6.4 %collective-permute-start.14 = (bf16[256,1152]{1,0:T(8,128)(2,1)}, bf16[256,1152]{1,0:T(8,128)(2,1)}, u32[]{:S(2)}, u32[]{:S(2)}) collective-permute-start(bf16[256,1152]{1,0:T(8,128)(2,1)} %collective-permute-done.12.rest_2_), channel_id=1, source_target_pairs={{0,1},{1,0},{2,3},{3,2},{4,5},{5,4},{6,7},{7,6},{8,9},{9,8},{10,11... | collective-permute-start | bytes 1769480 | tf_op jit(solution)/shard_map/ppermute | solution.py:748
  114.6 2.8 collective-permute-start.15
  135.0 102.7 %reduce-scatter.9.cloned.1.call-start = ((), (), s32[]{:S(2)}) async-start(), calls=%async_computation.7 | async-start | bytes 3538944 | tf_op jit(solution)/shard_map/reduce_scatter | solution.py:772
  140.8 2.7 copy-start.32
  140.8 2.7 collective-permute-start.16
  143.4 2.0 collective-permute-start.21
  143.7 14.8 %collective-permute-start.17 = (bf16[256,1152]{1,0:T(8,128)(2,1)S(1)}, bf16[256,1152]{1,0:T(8,128)(2,1)S(1)}, u32[]{:S(2)}, u32[]{:S(2)}) collective-permute-start(bf16[256,1152]{1,0:T(8,128)(2,1)S(1)} %add_convert_fusion.4), channel_id=1, source_target_pairs={{0,2},{1,3},{2,0},{3,1},{4,6},{5,7},{6,4},{7,5},{8,10},{9,11},{10,... | collective-permute-start | bytes 1769480 | tf_op jit(solution)/shard_map/ppermute | solution.py:748
  145.4 13.1 %copy-start.37 = (bf16[256,1152]{1,0:T(8,128)(2,1)}, bf16[256,1152]{1,0:T(8,128)(2,1)S(1)}, u32[]{:S(2)}) copy-start(bf16[256,1152]{1,0:T(8,128)(2,1)S(1)} %collective-permute-done.21.gn_near_ref) | copy-start | bytes 1769476
  196.1 70.7 %reduce-scatter.11.cloned.1.call-start = ((), (), s32[]{:S(2)}) async-start(), calls=%async_computation.10 | async-start | bytes 1492992
  201.5 5.3 %copy-start.31 = (bf16[288,1152]{1,0:T(8,128)(2,1)S(1)}, bf16[288,1152]{1,0:T(8,128)(2,1)}, u32[]{:S(2)}) copy-start(bf16[288,1152]{1,0:T(8,128)(2,1)} %get-tuple-element.145) | copy-start | bytes 1990660
  201.5 2.6 collective-permute-start.35
  202.1 4.7 %collective-permute-start.32 = (bf16[288,1152]{1,0:T(8,128)(2,1)}, bf16[288,1152]{1,0:T(8,128)(2,1)S(1)}, u32[]{:S(2)}, u32[]{:S(2)}) collective-permute-start(bf16[288,1152]{1,0:T(8,128)(2,1)} %get-tuple-element.146), channel_id=1, source_target_pairs={{0,1},{1,0},{2,3},{3,2},{4,5},{5,4},{6,7},{7,6},{8,9},{9,8},{10,11... | collective-permute-start | bytes 1990664 | tf_op jit(solution)/shard_map/ppermute | solution.py:748
  202.2 5.2 %collective-permute-start.31 = (bf16[288,1152]{1,0:T(8,128)(2,1)}, bf16[288,1152]{1,0:T(8,128)(2,1)S(1)}, u32[]{:S(2)}, u32[]{:S(2)}) collective-permute-start(bf16[288,1152]{1,0:T(8,128)(2,1)} %get-tuple-element.144), channel_id=1, source_target_pairs={{0,1},{1,0},{2,3},{3,2},{4,5},{5,4},{6,7},{7,6},{8,9},{9,8},{10,11... | collective-permute-start | bytes 1990664 | tf_op jit(solution)/shard_map/ppermute | solution.py:748
  202.7 4.7 %collective-permute-start.34 = (bf16[288,1152]{1,0:T(8,128)(2,1)}, bf16[288,1152]{1,0:T(8,128)(2,1)S(1)}, u32[]{:S(2)}, u32[]{:S(2)}) collective-permute-start(bf16[288,1152]{1,0:T(8,128)(2,1)} %get-tuple-element.148), channel_id=1, source_target_pairs={{0,1},{1,0},{2,3},{3,2},{4,5},{5,4},{6,7},{7,6},{8,9},{9,8},{10,11... | collective-permute-start | bytes 1990664 | tf_op jit(solution)/shard_map/ppermute | solution.py:748
  204.1 32.0 %copy-start.14 = (bf16[288,1152]{1,0:T(8,128)(2,1)S(1)}, bf16[288,1152]{1,0:T(8,128)(2,1)}, u32[]{:S(2)}) copy-start(bf16[288,1152]{1,0:T(8,128)(2,1)} %get-tuple-element.143.refs_0_) | copy-start | bytes 1990660
  204.1 32.0 %copy-start.15 = (bf16[288,1152]{1,0:T(8,128)(2,1)S(1)}, bf16[288,1152]{1,0:T(8,128)(2,1)}, u32[]{:S(2)}) copy-start(bf16[288,1152]{1,0:T(8,128)(2,1)} %get-tuple-element.147.refs_3_) | copy-start | bytes 1990660
  205.6 16.3 %collective-permute-start.36 = (bf16[288,1152]{1,0:T(8,128)(2,1)S(1)}, bf16[288,1152]{1,0:T(8,128)(2,1)S(1)}, u32[]{:S(2)}, u32[]{:S(2)}) collective-permute-start(bf16[288,1152]{1,0:T(8,128)(2,1)S(1)} %add_convert_fusion), channel_id=1, source_target_pairs={{0,2},{1,3},{2,0},{3,1},{4,6},{5,7},{6,4},{7,5},{8,10},{9,11},{10,... | collective-permute-start | bytes 1990664 | tf_op jit(solution)/shard_map/ppermute | solution.py:748
  207.0 29.1 %collective-permute-start.33 = (bf16[288,1152]{1,0:T(8,128)(2,1)S(1)}, bf16[288,1152]{1,0:T(8,128)(2,1)S(1)}, u32[]{:S(2)}, u32[]{:S(2)}) collective-permute-start(bf16[288,1152]{1,0:T(8,128)(2,1)S(1)} %add_convert_fusion.1), channel_id=1, source_target_pairs={{0,2},{1,3},{2,0},{3,1},{4,6},{5,7},{6,4},{7,5},{8,10},{9,11},{10,... | collective-permute-start | bytes 1990664 | tf_op jit(solution)/shard_map/ppermute | solution.py:748
  237.7 124.0 %all-gather.7.cloned.1.call-start = ((), (), s32[]{:S(2)}) async-start(), calls=%async_computation.8 | async-start | bytes 7464960 | tf_op jit(solution)/shard_map/all_gather | solution.py:777
  242.0 3.3 copy-start.30
  244.0 14.0 %copy-start.20 = (bf16[256,768]{1,0:T(8,128)(2,1)}, bf16[256,768]{1,0:T(8,128)(2,1)S(1)}, u32[]{:S(2)}) copy-start(bf16[256,768]{1,0:T(8,128)(2,1)S(1)} %get-tuple-element.129.gkv_ref) | copy-start | bytes 1179652
  244.0 4.4 %collective-permute-start.29 = (bf16[288,768]{1,0:T(8,128)(2,1)S(1)}, bf16[288,768]{1,0:T(8,128)(2,1)S(1)}, u32[]{:S(2)}, u32[]{:S(2)}) collective-permute-start(bf16[288,768]{1,0:T(8,128)(2,1)S(1)} %get-tuple-element.139), channel_id=1, source_target_pairs={{0,1},{1,0},{2,3},{3,2},{4,5},{5,4},{6,7},{7,6},{8,9},{9,8},{10,11... | collective-permute-start | bytes 1327112 | tf_op jit(solution)/shard_map/ppermute | solution.py:748
  245.3 11.7 %collective-permute-start.27 = (bf16[576,384]{1,0:T(8,128)(2,1)S(1)}, bf16[576,384]{1,0:T(8,128)(2,1)S(1)}, u32[]{:S(2)}, u32[]{:S(2)}) collective-permute-start(bf16[576,384]{1,0:T(8,128)(2,1)S(1)} %slice_bitcast_fusion.2), channel_id=1, source_target_pairs={{0,0},{1,3},{2,2},{3,1},{4,7},{5,6},{6,5},{7,4},{8,8},{9,11},{10,1... | collective-permute-start | bytes 1327112 | tf_op jit(solution)/shard_map/ppermute | solution.py:1045
  248.4 9.7 %collective-permute-start.28 = (bf16[288,768]{1,0:T(8,128)(2,1)S(1)}, bf16[288,768]{1,0:T(8,128)(2,1)S(1)}, u32[]{:S(2)}, u32[]{:S(2)}) collective-permute-start(bf16[288,768]{1,0:T(8,128)(2,1)S(1)} %get-tuple-element.137), channel_id=1, source_target_pairs={{0,1},{1,0},{2,3},{3,2},{4,5},{5,4},{6,7},{7,6},{8,9},{9,8},{10,11... | collective-permute-start | bytes 1327112 | tf_op jit(solution)/shard_map/ppermute | solution.py:748
  248.6 15.2 %collective-permute-start.30 = (bf16[288,768]{1,0:T(8,128)(2,1)S(1)}, bf16[288,768]{1,0:T(8,128)(2,1)S(1)}, u32[]{:S(2)}, u32[]{:S(2)}) collective-permute-start(bf16[288,768]{1,0:T(8,128)(2,1)S(1)} %add_convert_fusion.5), channel_id=1, source_target_pairs={{0,2},{1,3},{2,0},{3,1},{4,6},{5,7},{6,4},{7,5},{8,10},{9,11},{10,... | collective-permute-start | bytes 1327112 | tf_op jit(solution)/shard_map/ppermute | solution.py:748
  268.4 7.3 %copy-start.35 = (bf16[768,1152]{1,0:T(8,128)(2,1)S(1)}, bf16[768,1152]{1,0:T(8,128)(2,1)}, u32[]{:S(2)}) copy-start(bf16[768,1152]{1,0:T(8,128)(2,1)} %down_ref.3) | copy-start | bytes 5308420
  268.5 7.3 %copy-start.39 = (bf16[2,256,768]{2,1,0:T(8,128)(2,1)S(1)}, bf16[2,256,768]{2,1,0:T(8,128)(2,1)}, u32[]{:S(2)}) copy-start(bf16[2,256,768]{2,1,0:T(8,128)(2,1)} %get-tuple-element.105.act_in) | copy-start | bytes 2359300
  271.6 13.1 %collective-permute-start.19 = (bf16[256,1152]{1,0:T(8,128)(2,1)S(1)}, bf16[256,1152]{1,0:T(8,128)(2,1)S(1)}, u32[]{:S(2)}, u32[]{:S(2)}) collective-permute-start(bf16[256,1152]{1,0:T(8,128)(2,1)S(1)} %slice.75), channel_id=1, source_target_pairs={{0,1},{1,0},{2,3},{3,2},{4,5},{5,4},{6,7},{7,6},{8,9},{9,8},{10,11... | collective-permute-start | bytes 1769480 | tf_op jit(solution)/shard_map/ppermute | solution.py:748
  275.8 2.5 copy-start.1
  275.8 2.5 copy-start.2
  277.9 36.3 %collective-permute-start.18 = (bf16[256,1152]{1,0:T(8,128)(2,1)}, bf16[256,1152]{1,0:T(8,128)(2,1)}, u32[]{:S(2)}, u32[]{:S(2)}) collective-permute-start(bf16[256,1152]{1,0:T(8,128)(2,1)} %slice.73), channel_id=1, source_target_pairs={{0,1},{1,0},{2,3},{3,2},{4,5},{5,4},{6,7},{7,6},{8,9},{9,8},{10,11... | collective-permute-start | bytes 1769480 | tf_op jit(solution)/shard_map/ppermute | solution.py:748
  279.2 5.4 %copy-start.33 = (f32[1,1152]{1,0:T(1,128)S(1)}, f32[1,1152]{1,0:T(1,128)}, u32[]{:S(2)}) copy-start(f32[1,1152]{1,0:T(1,128)} %get-tuple-element.134) | copy-start | bytes 13828
  284.6 6.1 %copy-start.34 = (f32[1,1152]{1,0:T(1,128)S(1)}, f32[1,1152]{1,0:T(1,128)}, u32[]{:S(2)}) copy-start(f32[1,1152]{1,0:T(1,128)} %get-tuple-element.134) | copy-start | bytes 13828
  284.6 6.1 %collective-permute-start.22 = (f32[2,1152]{1,0:T(2,128)S(1)}, f32[2,1152]{1,0:T(2,128)S(1)}, u32[]{:S(2)}, u32[]{:S(2)}) collective-permute-start(f32[2,1152]{1,0:T(2,128)S(1)} %pad_maximum_fusion.2), channel_id=1, source_target_pairs={{0,1},{1,0},{2,3},{3,2},{4,5},{5,4},{6,7},{7,6},{8,9},{9,8},{10,11... | collective-permute-start | bytes 27656 | tf_op jit(solution)/shard_map/ppermute | solution.py:748
  285.7 28.5 %copy-start.26 = (f32[256,1152]{1,0:T(8,128)S(1)}, f32[256,1152]{1,0:T(8,128)}, u32[]{:S(2)}) copy-start(f32[256,1152]{1,0:T(8,128)} %get-tuple-element.100.mid_ref) | copy-start | bytes 3538948
  285.7 28.6 %copy-start.28 = (bf16[512,1152]{1,0:T(8,128)(2,1)S(1)}, bf16[512,1152]{1,0:T(8,128)(2,1)}, u32[]{:S(2)}) copy-start(bf16[512,1152]{1,0:T(8,128)(2,1)} %copy-done.27) | copy-start | bytes 3538948
  285.7 28.5 %collective-permute-start.20 = (bf16[256,1152]{1,0:T(8,128)(2,1)}, bf16[256,1152]{1,0:T(8,128)(2,1)S(1)}, u32[]{:S(2)}, u32[]{:S(2)}) collective-permute-start(bf16[256,1152]{1,0:T(8,128)(2,1)} %add_convert_fusion.3), channel_id=1, source_target_pairs={{0,2},{1,3},{2,0},{3,1},{4,6},{5,7},{6,4},{7,5},{8,10},{9,11},{10,... | collective-permute-start | bytes 1769480 | tf_op jit(solution)/shard_map/ppermute | solution.py:748
  286.9 21.3 %all-to-all-start = ((bf16[8,216,128]{2,1,0:T(8,128)(2,1)}), bf16[8,216,128]{2,1,0:T(8,128)(2,1)S(1)}, u32[]{:S(2)}, u32[]{:S(2)}) async-start(bf16[8,216,128]{2,1,0:T(8,128)(2,1)} %bitcast.15), calls=%async_computation.2 | async-start | bytes 884736 | tf_op jit(solution)/shard_map/all_to_all | solution.py:1176
  290.7 9.9 %collective-permute-start.23 = (f32[2,1152]{1,0:T(2,128)S(1)}, f32[2,1152]{1,0:T(2,128)S(1)}, u32[]{:S(2)}, u32[]{:S(2)}) collective-permute-start(f32[2,1152]{1,0:T(2,128)S(1)} %fusion.7), channel_id=1, source_target_pairs={{0,2},{1,3},{2,0},{3,1},{4,6},{5,7},{6,4},{7,5},{8,10},{9,11},{10,... | collective-permute-start | bytes 27656 | tf_op jit(solution)/shard_map/ppermute | solution.py:748
  300.6 3.0 collective-permute-start.24
  303.6 3.2 collective-permute-start.25
  306.8 9.6 %collective-permute-start.26 = (f32[2,1152]{1,0:T(2,128)S(1)}, f32[2,1152]{1,0:T(2,128)S(1)}, u32[]{:S(2)}, u32[]{:S(2)}) collective-permute-start(f32[2,1152]{1,0:T(2,128)S(1)} %add.136), channel_id=1, source_target_pairs={{0,16},{4,20},{8,24},{12,28},{16,0},{20,4},{24,8},{28,12},{1,17},{... | collective-permute-start | bytes 27656 | tf_op jit(solution)/shard_map/ppermute | solution.py:752
  309.1 21.8 %all-to-all-start.1 = ((bf16[8,216,128]{2,1,0:T(8,128)(2,1)}), bf16[8,216,128]{2,1,0:T(8,128)(2,1)S(1)}, u32[]{:S(2)}, u32[]{:S(2)}) async-start(bf16[8,216,128]{2,1,0:T(8,128)(2,1)} %broadcast_in_dim.40), calls=%async_computation.3 | async-start | bytes 884736 | tf_op jit(solution)/shard_map/all_to_all | solution.py:1176
  (21 other events, 31.0 us)
Sparse Core Ops, SparseCore 0:
  29.1 38.4 all-gather.4
  69.7 28.9 all-gather.8
  135.1 60.2 reduce-scatter.6
  198.1 38.1 reduce-scatter.8
  239.1 27.6 reduce-scatter.10
  268.9 92.7 all-gather.6

commit v4 on v3

--- a/solution.py
+++ b/solution.py
@@ -639,18 +639,18 @@
     turned[:own, :] = act[...].T
 
     def down_block(index, carry):
-        left = turned[pl.ds(pl.multiple_of(index * 2 * band, 16), 2 * band), :]
+        left = turned[pl.ds(pl.multiple_of(index * 4 * band, 16), 4 * band), :]
         grad = nn(left, cots[...])
-        for part in range(2):
+        for part in range(4):
             for split in range(width // tile):
                 start = 2 * rows + split * band
-                tiles[2 * index + part, start : start + band, :] = grad[
+                tiles[4 * index + part, start : start + band, :] = grad[
                     part * band : (part + 1) * band, split * tile : (split + 1) * tile
                 ].astype(BF16)
-            tile_copy(2 * index + part, 1).start()
+            tile_copy(4 * index + part, 1).start()
         return carry
 
-    lax.fori_loop(0, places // 2, down_block, 0)
+    lax.fori_loop(0, places // 4, down_block, 0)
     for copy in outs:
         copy.wait()
     for spot in range(places):

time: 378 us -> 378 us (level)
  no operation moved by 1% of the time
where the time goes in v4:
time: 378 us; the launch traced here: 377 us
  waiting for transfers between devices  183 us (48%)
  Pallas kernels  96.8 us (26%)
  starting transfers between devices  44.4 us (12%)
  local copies, waits for them, and re-layouts  19.7 us (5%)
  between operations  14.6 us (4%)
  other arithmetic  14.2 us (4%)
  matrix products  4.25 us (1%)
    ppermute x33, waiting for transfers between devices, hop(): return lax.ppermute(value, 'shard', pairs)  98.6 us
    all_gather x3, waiting for transfers between devices, collect(): lax.all_gather(value, 'ctx', axis=0, axis_index_groups=[order], tiled=True)  38.8 us
    ppermute x33, starting transfers between devices, hop(): return lax.ppermute(value, 'shard', pairs)  29.2 us
    pallas_call x8, Pallas kernels, call_once(): pl.pallas_call(kernel, out_shape=tuple((jax.ShapeDtypeStruct(shape, dtype...  27.3 us
    pallas_call x1, Pallas kernels, on_device(): pl.pallas_call(functools.partial(attend_back_kernel, **shared), out_shape...  19.5 us
    pallas_call x1, Pallas kernels, on_device(): pl.pallas_call(functools.partial(feed_far_kernel, per_shard=per_shard), o...  17.2 us
    reduce_scatter x2, waiting for transfers between devices, scatter(): lax.psum_scatter(value, 'ctx', scatter_dimension=0, axis_index_groups=[or...  16.3 us
    all_to_all x2, waiting for transfers between devices, exchange(): return lax.all_to_all(value, 'ctx', split_axis=0, concat_axis=0, tiled=True)  13.8 us
  transfers between devices with their start and end apart: 45, of which 24 were waited for; matrix products, arithmetic and copies ran while one was open for 6% of the time, Pallas kernels for 18%

profile of v4, /device:TPU:9, one launch (start us, length us, event | category | flops | bytes accessed | tf_op | source)
XLA Modules:
  0.0 376.8 jit_solution(3807581626790144724)
XLA Ops:
  8.0 1.1 fusion.2.rest_0_.rest_4_
  9.1 1.3 collective-permute-start.1
  11.4 1.4 dynamic-slice_select_fusion.1
  13.4 1.3 constant_dynamic-slice_fusion
  14.7 1.0 pad_maximum_fusion
  15.7 5.0 %collective-permute-done.1.rest_2_.rest_6_ = bf16[304,768]{1,0:T(8,128)(2,1)S(1)} collective-permute-done((bf16[304,768]{1,0:T(8,128)(2,1)S(1)}, bf16[304,768]{1,0:T(8,128)(2,1)S(1)}, u32[]{:S(2)}, u32[]{:S(2)}) %collective-permute-start.1) | collective-permute-done | bytes 466976 | tf_op jit(solution)/shard_map/ppermute | solution.py:748
  20.7 1.5 collective-permute-start.2
  22.3 1.3 fusion.3
  24.6 4.3 %keys.1 = (bf16[256,1152]{1,0:T(8,128)(2,1)}, bf16[256,768]{1,0:T(8,128)(2,1)}, f32[1,1152]{1,0:T(1,128)}, f32[1,1152]{1,0:T(1,128)}) custom-call(s32[2]{0:T(128)} %pad_add_fusion.ids_ref.table_ref, bf16[256,1152]{1,0:T(8,128)(2,1)} %bitcast.36, f32[256,128]{1,0:T(8,128)} %get-tuple-element.91.cos_ref, f32[256,128]{1,0:T(8,128)} %get-tuple-element.92.sin_ref, ...), custom_call_target="tpu_custom_call" | custom-call | flops 452984832 | bytes 4987648 | tf_op jit(solution)/shard_map/keys/pallas_call | solution.py:62
  29.0 1.3 collective-permute-start.4
  30.3 19.8 %collective-permute-done.4.rest_2_ = bf16[288,1536]{1,0:T(8,128)(2,1)S(1)} collective-permute-done((bf16[288,1536]{1,0:T(8,128)(2,1)S(1)}, bf16[288,1536]{1,0:T(8,128)(2,1)S(1)}, u32[]{:S(2)}, u32[]{:S(2)}) %collective-permute-start.4) | collective-permute-done | bytes 884768 | tf_op jit(solution)/shard_map/ppermute | solution.py:748
  50.1 1.0 collective-permute-start.5
  51.1 2.0 collective-permute-done.5.rest_3_
  54.4 1.2 collective-permute-start.7
  58.3 1.1 copy-done.16
  59.4 2.1 queries.1.q_ref
  62.3 8.7 %collective-permute-done.7.rest_2_ = bf16[288,1152]{1,0:T(8,128)(2,1)S(1)} collective-permute-done((bf16[288,1152]{1,0:T(8,128)(2,1)}, bf16[288,1152]{1,0:T(8,128)(2,1)S(1)}, u32[]{:S(2)}, u32[]{:S(2)}) %collective-permute-start.7) | collective-permute-done | bytes 663584 | tf_op jit(solution)/shard_map/ppermute | solution.py:748
  73.3 1.2 collective-permute-start.13
  74.5 1.1 collective-permute-done.8.rest_3_
  75.6 12.5 %attend.1 = (f32[1152,256]{1,0:T(8,128)}, bf16[256,1152]{1,0:T(8,128)(2,1)}, f32[8,768]{1,0:T(8,128)}, f32[256,1152]{1,0:T(8,128)}, bf16[256,1152]{1,0:T(8,128)(2,1)}, /*index=5*/bf16[6,64,768]{2,1,0:T(8,128)(2,1)}) custom-call(s32[2]{0:T(128)} %pad_add_fusion.ids_ref.table_ref, bf16[256,1152]{1,0:T(8,128)(2,1)} %copy-done.18, ...), custom_call_target="tpu_custom_call" | custom-call | flops 2415919104 | bytes 12000000 | tf_op jit(solution)/shard_map/attend/pallas_call | solution.py:871
  88.5 1.2 collective-permute-start.12
  89.7 9.1 %all-gather.9.cloned.1.call-done = bf16[2304,384]{1,0:T(8,128)(2,1)} async-done(((bf16[288,384]{1,0:T(8,128)(2,1)}), bf16[2304,384]{1,0:T(8,128)(2,1)}) %all-gather.9.cloned.1.call-update) | async-done | bytes 1769488 | tf_op jit(solution)/shard_map/all_gather | solution.py:777
  98.8 11.4 %feed_near.1 = (bf16[1152,768]{1,0:T(8,128)(2,1)}, bf16[1152,768]{1,0:T(8,128)(2,1)}, bf16[2,256,768]{2,1,0:T(8,128)(2,1)}, bf16[2,256,768]{2,1,0:T(8,128)(2,1)}...) custom-call(s32[2]{0:T(128)} %pad_add_fusion.ids_ref.table_ref, bf16[288,3072]{1,0:T(8,128)(2,1)} %own_gate_ref.1, ...), custom_call_target="tpu_custom_call" | custom-call | flops 4529848320 | bytes 12000000 | tf_op jit(solution)/shard_map/feed_near/pallas_call | solution.py:920
  110.3 4.5 %collective-permute-start.14 = (bf16[256,1152]{1,0:T(8,128)(2,1)}, bf16[256,1152]{1,0:T(8,128)(2,1)}, u32[]{:S(2)}, u32[]{:S(2)}) collective-permute-start(bf16[256,1152]{1,0:T(8,128)(2,1)} %collective-permute-done.12.rest_2_), channel_id=1, source_target_pairs={{0,1},{1,0},{2,3},{3,2},{4,5},{5,4},{6,7},{7,6},{8,9},{9,8},{10,11... | collective-permute-start | bytes 1769480 | tf_op jit(solution)/shard_map/ppermute | solution.py:748
  114.9 1.9 collective-permute-done.14.rest_3_
  117.6 17.2 %feed_far.1 = (bf16[8,864,384]{2,1,0:T(8,128)(2,1)}, bf16[512,768]{1,0:T(8,128)(2,1)}, bf16[512,768]{1,0:T(8,128)(2,1)}, bf16[512,768]{1,0:T(8,128)(2,1)}) custom-call(s32[2]{0:T(128)} %pad_add_fusion.ids_ref.table_ref, bf16[1152,768]{1,0:T(8,128)(2,1)} %get-tuple-element.106.gate_mat_ref, bf16[1152,768]{1,0:T(8,128)(2,1)} %get-tuple-element.107.up_mat_ref, ...), custom_call_target="tpu_custom_call" | custom-call | flops 8153726976 | bytes 25000000 | tf_op jit(solution)/shard_map/feed_far/pallas_call | solution.py:960
  135.1 5.6 %normed_back.1 = (bf16[256,1152]{1,0:T(8,128)(2,1)}, bf16[256,1152]{1,0:T(8,128)(2,1)}) custom-call(bf16[512,768]{1,0:T(8,128)(2,1)} %get-tuple-element.115.gate_ref, bf16[512,768]{1,0:T(8,128)(2,1)} %get-tuple-element.116.up_ref, bf16[1152,768]{1,0:T(8,128)(2,1)} %get-tuple-element.106.gate_mat_ref, bf16[1152,768]{1,0:T(8,128)(2,1)} %get-tuple-element.107.up_mat_ref), custom_call_target="tpu_custom_call" | custom-call | flops 1811939328 | bytes 5179648 | tf_op jit(solution)/shard_map/normed_back/pallas_call | solution.py:62
  141.1 2.1 slice_bitcast_fusion
  143.5 1.2 collective-permute-start.17
  145.2 13.1 %collective-permute-done.17.gn_far_ref = bf16[256,1152]{1,0:T(8,128)(2,1)S(1)} collective-permute-done((bf16[256,1152]{1,0:T(8,128)(2,1)S(1)}, bf16[256,1152]{1,0:T(8,128)(2,1)S(1)}, u32[]{:S(2)}, u32[]{:S(2)}) %collective-permute-start.17) | collective-permute-done | bytes 589856 | tf_op jit(solution)/shard_map/ppermute | solution.py:748
  159.1 19.5 %attend_back.1 = (bf16[256,1152]{1,0:T(8,128)(2,1)}, bf16[2048,768]{1,0:T(8,128)(2,1)}, bf16[256,1152]{1,0:T(8,128)(2,1)}, f32[256,1152]{1,0:T(8,128)}, f32[1,1152]{1,0:T(1,128)}) custom-call(s32[2]{0:T(128)} %pad_add_fusion.ids_ref.table_ref, bf16[2048,768]{1,0:T(8,128)(2,1)} %all-gather.5.cloned.1.call-done.kv_ref, ...), custom_call_target="tpu_custom_call" | custom-call | flops 6039797760 | bytes 14000000 | tf_op jit(solution)/shard_map/attend_back/pallas_call | solution.py:1066
  178.6 16.3 %reduce-scatter.7.cloned.1.call-done = bf16[1,864,384]{2,1,0:T(8,128)(2,1)} async-done(((bf16[8,864,384]{2,1,0:T(8,128)(2,1)}), bf16[1,864,384]{2,1,0:T(8,128)(2,1)}) %reduce-scatter.7.cloned.1.call-update) | async-done | bytes 663568 | tf_op jit(solution)/shard_map/reduce_scatter | solution.py:772
  195.7 5.3 %weight_grads.1 = (bf16[288,1152]{1,0:T(8,128)(2,1)}, bf16[288,1152]{1,0:T(8,128)(2,1)}, bf16[288,1152]{1,0:T(8,128)(2,1)}, bf16[288,1152]{1,0:T(8,128)(2,1)}, b...) custom-call(s32[2]{0:T(128)} %pad_add_fusion.ids_ref.table_ref, ...), custom_call_target="tpu_custom_call" | custom-call | flops 1358954496 | bytes 9308416 | tf_op jit(solution)/shard_map/weight_grads/pallas_call | solution.py:62
  202.2 1.4 collective-permute-done.35
  203.6 1.5 add_convert_fusion
  205.1 1.2 collective-permute-start.36
  206.9 14.5 %collective-permute-done.36.refs_5_ = bf16[288,1152]{1,0:T(8,128)(2,1)S(1)} collective-permute-done((bf16[288,1152]{1,0:T(8,128)(2,1)S(1)}, bf16[288,1152]{1,0:T(8,128)(2,1)S(1)}, u32[]{:S(2)}, u32[]{:S(2)}) %collective-permute-start.36) | collective-permute-done | bytes 663584 | tf_op jit(solution)/shard_map/ppermute | solution.py:748
  221.4 14.2 %collective-permute-done.33.refs_2_ = bf16[288,1152]{1,0:T(8,128)(2,1)S(1)} collective-permute-done((bf16[288,1152]{1,0:T(8,128)(2,1)S(1)}, bf16[288,1152]{1,0:T(8,128)(2,1)S(1)}, u32[]{:S(2)}, u32[]{:S(2)}) %collective-permute-start.33) | collective-permute-done | bytes 663584 | tf_op jit(solution)/shard_map/ppermute | solution.py:748
  235.6 1.6 stack_mixed.1
  239.4 1.1 copy-done.17
  240.4 1.0 copy-done.25
  241.4 2.0 kv_back.1
  243.5 1.2 collective-permute-start.29
  244.7 3.1 collective-permute-start.27
  248.4 8.0 %collective-permute-done.27 = bf16[576,384]{1,0:T(8,128)(2,1)S(1)} collective-permute-done((bf16[576,384]{1,0:T(8,128)(2,1)S(1)}, bf16[576,384]{1,0:T(8,128)(2,1)S(1)}, u32[]{:S(2)}, u32[]{:S(2)}) %collective-permute-start.27) | collective-permute-done | bytes 442400 | tf_op jit(solution)/shard_map/ppermute | solution.py:1045
  256.4 1.1 maximum_maximum_fusion.1
  257.5 5.7 %collective-permute-done.30.refs_2_ = bf16[288,768]{1,0:T(8,128)(2,1)S(1)} collective-permute-done((bf16[288,768]{1,0:T(8,128)(2,1)S(1)}, bf16[288,768]{1,0:T(8,128)(2,1)S(1)}, u32[]{:S(2)}, u32[]{:S(2)}) %collective-permute-start.30) | collective-permute-done | bytes 442400 | tf_op jit(solution)/shard_map/ppermute | solution.py:748
  264.2 2.1 reduce-scatter.11.cloned.1.call-done
  266.3 1.6 constant_dynamic-update-slice_fusion
  267.9 3.0 convolution_convert_fusion
  271.0 4.2 %collective-permute-start.19 = (bf16[256,1152]{1,0:T(8,128)(2,1)S(1)}, bf16[256,1152]{1,0:T(8,128)(2,1)S(1)}, u32[]{:S(2)}, u32[]{:S(2)}) collective-permute-start(bf16[256,1152]{1,0:T(8,128)(2,1)S(1)} %slice.75), channel_id=1, source_target_pairs={{0,1},{1,0},{2,3},{3,2},{4,5},{5,4},{6,7},{7,6},{8,9},{9,8},{10,11... | collective-permute-start | bytes 1769480 | tf_op jit(solution)/shard_map/ppermute | solution.py:748
  275.3 1.2 convolution_convert_fusion.1
  278.6 5.4 %grad_inputs.1 = (bf16[256,1152]{1,0:T(8,128)(2,1)}, f32[1,1152]{1,0:T(1,128)S(1)}) custom-call(s32[2]{0:T(128)S(1)} %copy-done.23, bf16[256,1152]{1,0:T(8,128)(2,1)S(1)} %copy-done.19, bf16[256,768]{1,0:T(8,128)(2,1)S(1)} %copy-done.21, bf16[256,1152]{1,0:T(8,128)(2,1)S(1)} %bitcast.38, f32[1,1152]{1,0:T(1,128)S(1)} %copy-done.24, ...), custom_call_target="tpu_custom_call" | custom-call | flops 1132462080 | bytes 4592128 | tf_op jit(solution)/shard_map/grad_inputs/pallas_call | solution.py:62
  285.1 1.2 collective-permute-start.20
  286.4 3.8 %all-to-all-start = ((bf16[8,216,128]{2,1,0:T(8,128)(2,1)}), bf16[8,216,128]{2,1,0:T(8,128)(2,1)S(1)}, u32[]{:S(2)}, u32[]{:S(2)}) async-start(bf16[8,216,128]{2,1,0:T(8,128)(2,1)} %bitcast.15), calls=%async_computation.2 | async-start | bytes 884736 | tf_op jit(solution)/shard_map/all_to_all | solution.py:1176
  290.6 9.4 %collective-permute-done.23 = f32[2,1152]{1,0:T(2,128)S(1)} collective-permute-done((f32[2,1152]{1,0:T(2,128)S(1)}, f32[2,1152]{1,0:T(2,128)S(1)}, u32[]{:S(2)}, u32[]{:S(2)}) %collective-permute-start.23) | collective-permute-done | bytes 9248 | tf_op jit(solution)/shard_map/ppermute | solution.py:748
  300.5 2.5 collective-permute-done.24
  303.7 2.6 collective-permute-done.25
  306.3 1.4 collective-permute-start.26
  308.5 5.2 %all-to-all-start.1 = ((bf16[8,216,128]{2,1,0:T(8,128)(2,1)}), bf16[8,216,128]{2,1,0:T(8,128)(2,1)S(1)}, u32[]{:S(2)}, u32[]{:S(2)}) async-start(bf16[8,216,128]{2,1,0:T(8,128)(2,1)} %broadcast_in_dim.40), calls=%async_computation.3 | async-start | bytes 884736 | tf_op jit(solution)/shard_map/all_to_all | solution.py:1176
  313.7 2.1 fusion.1
  316.5 13.8 %all-to-all-done.1 = bf16[8,216,128]{2,1,0:T(8,128)(2,1)S(1)} async-done(((bf16[8,216,128]{2,1,0:T(8,128)(2,1)}), bf16[8,216,128]{2,1,0:T(8,128)(2,1)S(1)}, u32[]{:S(2)}, u32[]{:S(2)}) %all-to-all-start.1) | async-done | bytes 442400 | tf_op jit(solution)/shard_map/all_to_all | solution.py:1176
  331.4 29.7 %all-gather.7.cloned.1.call-done.gate_up_ref.down_in_ref.mixed_ref = bf16[8,1080,384]{2,1,0:T(8,128)(2,1)} async-done(((bf16[1,1080,384]{2,1,0:T(8,128)(2,1)}), bf16[8,1080,384]{2,1,0:T(8,128)(2,1)}) %all-gather.7.cloned.1.call-update) | async-done | bytes 6635536 | tf_op jit(solution)/shard_map/all_gather | solution.py:777
  361.1 8.9 %widen.1 = (f32[288,3072]{1,0:T(8,128)}, f32[288,3072]{1,0:T(8,128)}, f32[768,1152]{1,0:T(8,128)}, f32[288,1152]{1,0:T(8,128)}, f32[288,1152]{1,0:T(8,128)}) custom-call(s32[2]{0:T(128)} %pad_add_fusion.ids_ref.table_ref, bf16[8,1080,384]{2,1,0:T(8,128)(2,1)} %all-gather.7.cloned.1.call-done.gate_up_ref.down_in_ref.mixed_ref, ...), custom_call_target="tpu_custom_call" | custom-call | flops 1000000 | bytes 20000000 | tf_op jit(solution)/shard_map/widen/pallas_call | solution.py:1212
  (168 shorter events, 27.9 us)
Async XLA Ops:
  7.2 68.4 %all-gather.5.cloned.1.call-start = ((), (), s32[]{:S(2)}) async-start(), calls=%async_computation.5 | async-start | bytes 3538944 | tf_op jit(solution)/shard_map/all_gather | solution.py:777
  9.1 6.6 %copy-start = (bf16[304,768]{1,0:T(8,128)(2,1)}, bf16[304,768]{1,0:T(8,128)(2,1)S(1)}, u32[]{:S(2)}) copy-start(bf16[304,768]{1,0:T(8,128)(2,1)S(1)} %fusion.2.rest_0_.rest_4_) | copy-start | bytes 1400836
  9.1 11.6 %collective-permute-start.1 = (bf16[304,768]{1,0:T(8,128)(2,1)S(1)}, bf16[304,768]{1,0:T(8,128)(2,1)S(1)}, u32[]{:S(2)}, u32[]{:S(2)}) collective-permute-start(bf16[304,768]{1,0:T(8,128)(2,1)S(1)} %fusion.2.rest_0_.rest_4_), channel_id=1, source_target_pairs={{0,2},{1,3},{2,0},{3,1},{4,6},{5,7},{6,4},{7,5},{8,10},{9,11},{10,... | collective-permute-start | bytes 1400840 | tf_op jit(solution)/shard_map/ppermute | solution.py:748
  10.4 13.2 %collective-permute-start = (bf16[304,768]{1,0:T(8,128)(2,1)S(1)}, bf16[304,768]{1,0:T(8,128)(2,1)S(1)}, u32[]{:S(2)}, u32[]{:S(2)}) collective-permute-start(bf16[304,768]{1,0:T(8,128)(2,1)S(1)} %fusion.2.rest_0_.rest_4_), channel_id=1, source_target_pairs={{0,1},{1,0},{2,3},{3,2},{4,5},{5,4},{6,7},{7,6},{8,9},{9,8},{10,11... | collective-permute-start | bytes 1400840 | tf_op jit(solution)/shard_map/ppermute | solution.py:748
  13.4 10.1 %copy-start.29 = (bf16[288,1152]{1,0:T(8,128)(2,1)S(1)}, bf16[288,1152]{1,0:T(8,128)(2,1)}, u32[]{:S(2)}) copy-start(bf16[288,1152]{1,0:T(8,128)(2,1)} %param.15) | copy-start | bytes 1990660
  20.7 3.0 copy-start.3
  20.7 3.0 collective-permute-start.2
  24.6 31.9 %copy-start.22 = (s32[2]{0:T(128)S(1)}, s32[2]{0:T(128)}, u32[]{:S(2)}) copy-start(s32[2]{0:T(128)} %pad_add_fusion.ids_ref.table_ref) | copy-start | bytes 28
  28.9 69.9 %all-gather.9.cloned.1.call-start = ((), (), s32[]{:S(2)}) async-start(), calls=%async_computation.9 | async-start | bytes 1990656 | tf_op jit(solution)/shard_map/all_gather | solution.py:777
  29.0 21.1 %collective-permute-start.4 = (bf16[288,1536]{1,0:T(8,128)(2,1)S(1)}, bf16[288,1536]{1,0:T(8,128)(2,1)S(1)}, u32[]{:S(2)}, u32[]{:S(2)}) collective-permute-start(bf16[288,1536]{1,0:T(8,128)(2,1)S(1)} %maximum_maximum_fusion.rest_0_), channel_id=1, source_target_pairs={{0,2},{1,3},{2,0},{3,1},{4,6},{5,7},{6,4},{7,5},{8,10},{9,11},{10,... | collective-permute-start | bytes 2654216 | tf_op jit(solution)/shard_map/ppermute | solution.py:748
  50.1 3.1 collective-permute-start.5
  53.9 141.0 %reduce-scatter.7.cloned.1.call-start = ((), (), s32[]{:S(2)}) async-start(), calls=%async_computation.6 | async-start | bytes 5971968 | tf_op jit(solution)/shard_map/reduce_scatter | solution.py:772
  54.0 2.5 collective-permute-start.3
  54.4 16.6 %collective-permute-start.7 = (bf16[288,1152]{1,0:T(8,128)(2,1)}, bf16[288,1152]{1,0:T(8,128)(2,1)S(1)}, u32[]{:S(2)}, u32[]{:S(2)}) collective-permute-start(bf16[288,1152]{1,0:T(8,128)(2,1)} %rest_0_.3), channel_id=1, source_target_pairs={{0,2},{1,3},{2,0},{3,1},{4,6},{5,7},{6,4},{7,5},{8,10},{9,11},{10,... | collective-permute-start | bytes 1990664 | tf_op jit(solution)/shard_map/ppermute | solution.py:748
  55.6 18.9 %collective-permute-start.6 = (bf16[288,1152]{1,0:T(8,128)(2,1)}, bf16[288,1152]{1,0:T(8,128)(2,1)}, u32[]{:S(2)}, u32[]{:S(2)}) collective-permute-start(bf16[288,1152]{1,0:T(8,128)(2,1)} %rest_0_.3), channel_id=1, source_target_pairs={{0,1},{1,0},{2,3},{3,2},{4,5},{5,4},{6,7},{7,6},{8,9},{9,8},{10,11... | collective-permute-start | bytes 1990664 | tf_op jit(solution)/shard_map/ppermute | solution.py:748
  71.9 3.7 collective-permute-start.8
  72.8 26.0 %collective-permute-start.9 = (bf16[288,1536]{1,0:T(8,128)(2,1)}, bf16[288,1536]{1,0:T(8,128)(2,1)}, u32[]{:S(2)}, u32[]{:S(2)}) collective-permute-start(bf16[288,1536]{1,0:T(8,128)(2,1)} %pad_maximum_fusion), channel_id=1, source_target_pairs={{0,1},{1,0},{2,3},{3,2},{4,5},{5,4},{6,7},{7,6},{8,9},{9,8},{10,11... | collective-permute-start | bytes 2654216 | tf_op jit(solution)/shard_map/ppermute | solution.py:748
  72.8 26.0 %collective-permute-start.11 = (bf16[256,1152]{1,0:T(8,128)(2,1)}, bf16[256,1152]{1,0:T(8,128)(2,1)}, u32[]{:S(2)}, u32[]{:S(2)}) collective-permute-start(bf16[256,1152]{1,0:T(8,128)(2,1)} %bitcast.4.rest_2_.rest_4_.cot_ref), channel_id=1, source_target_pairs={{0,1},{1,0},{2,3},{3,2},{4,5},{5,4},{6,7},{7,6},{8,9},{9,8},{10,11... | collective-permute-start | bytes 1769480 | tf_op jit(solution)/shard_map/ppermute | solution.py:748
  73.3 16.4 %collective-permute-start.13 = (bf16[256,1152]{1,0:T(8,128)(2,1)}, bf16[256,1152]{1,0:T(8,128)(2,1)}, u32[]{:S(2)}, u32[]{:S(2)}) collective-permute-start(bf16[256,1152]{1,0:T(8,128)(2,1)} %bitcast.4.rest_2_.rest_4_.cot_ref), channel_id=1, source_target_pairs={{0,2},{1,3},{2,0},{3,1},{4,6},{5,7},{6,4},{7,5},{8,10},{9,11},{10,... | collective-permute-start | bytes 1769480 | tf_op jit(solution)/shard_map/ppermute | solution.py:748
  88.1 10.7 %collective-permute-start.10 = (bf16[256,1152]{1,0:T(8,128)(2,1)}, bf16[256,1152]{1,0:T(8,128)(2,1)}, u32[]{:S(2)}, u32[]{:S(2)}) collective-permute-start(bf16[256,1152]{1,0:T(8,128)(2,1)} %get-tuple-element.103.rest_0_), channel_id=1, source_target_pairs={{0,1},{1,0},{2,3},{3,2},{4,5},{5,4},{6,7},{7,6},{8,9},{9,8},{10,11... | collective-permute-start | bytes 1769480 | tf_op jit(solution)/shard_map/ppermute | solution.py:748
  88.5 21.7 %collective-permute-start.12 = (bf16[256,1152]{1,0:T(8,128)(2,1)}, bf16[256,1152]{1,0:T(8,128)(2,1)}, u32[]{:S(2)}, u32[]{:S(2)}) collective-permute-start(bf16[256,1152]{1,0:T(8,128)(2,1)} %get-tuple-element.103.rest_0_), channel_id=1, source_target_pairs={{0,2},{1,3},{2,0},{3,1},{4,6},{5,7},{6,4},{7,5},{8,10},{9,11},{10,... | collective-permute-start | bytes 1769480 | tf_op jit(solution)/shard_map/ppermute | solution.py:748
  110.3 6.5 %collective-permute-start.14 = (bf16[256,1152]{1,0:T(8,128)(2,1)}, bf16[256,1152]{1,0:T(8,128)(2,1)}, u32[]{:S(2)}, u32[]{:S(2)}) collective-permute-start(bf16[256,1152]{1,0:T(8,128)(2,1)} %collective-permute-done.12.rest_2_), channel_id=1, source_target_pairs={{0,1},{1,0},{2,3},{3,2},{4,5},{5,4},{6,7},{7,6},{8,9},{9,8},{10,11... | collective-permute-start | bytes 1769480 | tf_op jit(solution)/shard_map/ppermute | solution.py:748
  114.8 2.8 collective-permute-start.15
  134.8 102.3 %reduce-scatter.9.cloned.1.call-start = ((), (), s32[]{:S(2)}) async-start(), calls=%async_computation.7 | async-start | bytes 3538944 | tf_op jit(solution)/shard_map/reduce_scatter | solution.py:772
  140.7 2.7 copy-start.32
  140.7 2.7 collective-permute-start.16
  143.2 2.0 collective-permute-start.21
  143.5 14.8 %collective-permute-start.17 = (bf16[256,1152]{1,0:T(8,128)(2,1)S(1)}, bf16[256,1152]{1,0:T(8,128)(2,1)S(1)}, u32[]{:S(2)}, u32[]{:S(2)}) collective-permute-start(bf16[256,1152]{1,0:T(8,128)(2,1)S(1)} %add_convert_fusion.4), channel_id=1, source_target_pairs={{0,2},{1,3},{2,0},{3,1},{4,6},{5,7},{6,4},{7,5},{8,10},{9,11},{10,... | collective-permute-start | bytes 1769480 | tf_op jit(solution)/shard_map/ppermute | solution.py:748
  145.2 13.1 %copy-start.37 = (bf16[256,1152]{1,0:T(8,128)(2,1)}, bf16[256,1152]{1,0:T(8,128)(2,1)S(1)}, u32[]{:S(2)}) copy-start(bf16[256,1152]{1,0:T(8,128)(2,1)S(1)} %collective-permute-done.21.gn_near_ref) | copy-start | bytes 1769476
  195.6 70.7 %reduce-scatter.11.cloned.1.call-start = ((), (), s32[]{:S(2)}) async-start(), calls=%async_computation.10 | async-start | bytes 1492992
  201.0 5.3 %copy-start.31 = (bf16[288,1152]{1,0:T(8,128)(2,1)S(1)}, bf16[288,1152]{1,0:T(8,128)(2,1)}, u32[]{:S(2)}) copy-start(bf16[288,1152]{1,0:T(8,128)(2,1)} %get-tuple-element.145) | copy-start | bytes 1990660
  201.0 2.6 collective-permute-start.35
  201.6 4.7 %collective-permute-start.32 = (bf16[288,1152]{1,0:T(8,128)(2,1)}, bf16[288,1152]{1,0:T(8,128)(2,1)S(1)}, u32[]{:S(2)}, u32[]{:S(2)}) collective-permute-start(bf16[288,1152]{1,0:T(8,128)(2,1)} %get-tuple-element.146), channel_id=1, source_target_pairs={{0,1},{1,0},{2,3},{3,2},{4,5},{5,4},{6,7},{7,6},{8,9},{9,8},{10,11... | collective-permute-start | bytes 1990664 | tf_op jit(solution)/shard_map/ppermute | solution.py:748
  201.7 5.2 %collective-permute-start.31 = (bf16[288,1152]{1,0:T(8,128)(2,1)}, bf16[288,1152]{1,0:T(8,128)(2,1)S(1)}, u32[]{:S(2)}, u32[]{:S(2)}) collective-permute-start(bf16[288,1152]{1,0:T(8,128)(2,1)} %get-tuple-element.144), channel_id=1, source_target_pairs={{0,1},{1,0},{2,3},{3,2},{4,5},{5,4},{6,7},{7,6},{8,9},{9,8},{10,11... | collective-permute-start | bytes 1990664 | tf_op jit(solution)/shard_map/ppermute | solution.py:748
  202.1 4.7 %collective-permute-start.34 = (bf16[288,1152]{1,0:T(8,128)(2,1)}, bf16[288,1152]{1,0:T(8,128)(2,1)S(1)}, u32[]{:S(2)}, u32[]{:S(2)}) collective-permute-start(bf16[288,1152]{1,0:T(8,128)(2,1)} %get-tuple-element.148), channel_id=1, source_target_pairs={{0,1},{1,0},{2,3},{3,2},{4,5},{5,4},{6,7},{7,6},{8,9},{9,8},{10,11... | collective-permute-start | bytes 1990664 | tf_op jit(solution)/shard_map/ppermute | solution.py:748
  203.6 32.0 %copy-start.14 = (bf16[288,1152]{1,0:T(8,128)(2,1)S(1)}, bf16[288,1152]{1,0:T(8,128)(2,1)}, u32[]{:S(2)}) copy-start(bf16[288,1152]{1,0:T(8,128)(2,1)} %get-tuple-element.143.refs_0_) | copy-start | bytes 1990660
  203.6 32.0 %copy-start.15 = (bf16[288,1152]{1,0:T(8,128)(2,1)S(1)}, bf16[288,1152]{1,0:T(8,128)(2,1)}, u32[]{:S(2)}) copy-start(bf16[288,1152]{1,0:T(8,128)(2,1)} %get-tuple-element.147.refs_3_) | copy-start | bytes 1990660
  205.1 16.3 %collective-permute-start.36 = (bf16[288,1152]{1,0:T(8,128)(2,1)S(1)}, bf16[288,1152]{1,0:T(8,128)(2,1)S(1)}, u32[]{:S(2)}, u32[]{:S(2)}) collective-permute-start(bf16[288,1152]{1,0:T(8,128)(2,1)S(1)} %add_convert_fusion), channel_id=1, source_target_pairs={{0,2},{1,3},{2,0},{3,1},{4,6},{5,7},{6,4},{7,5},{8,10},{9,11},{10,... | collective-permute-start | bytes 1990664 | tf_op jit(solution)/shard_map/ppermute | solution.py:748
  206.5 29.1 %collective-permute-start.33 = (bf16[288,1152]{1,0:T(8,128)(2,1)S(1)}, bf16[288,1152]{1,0:T(8,128)(2,1)S(1)}, u32[]{:S(2)}, u32[]{:S(2)}) collective-permute-start(bf16[288,1152]{1,0:T(8,128)(2,1)S(1)} %add_convert_fusion.1), channel_id=1, source_target_pairs={{0,2},{1,3},{2,0},{3,1},{4,6},{5,7},{6,4},{7,5},{8,10},{9,11},{10,... | collective-permute-start | bytes 1990664 | tf_op jit(solution)/shard_map/ppermute | solution.py:748
  237.2 124.0 %all-gather.7.cloned.1.call-start = ((), (), s32[]{:S(2)}) async-start(), calls=%async_computation.8 | async-start | bytes 7464960 | tf_op jit(solution)/shard_map/all_gather | solution.py:777
  241.4 3.3 copy-start.30
  243.5 14.1 %copy-start.20 = (bf16[256,768]{1,0:T(8,128)(2,1)}, bf16[256,768]{1,0:T(8,128)(2,1)S(1)}, u32[]{:S(2)}) copy-start(bf16[256,768]{1,0:T(8,128)(2,1)S(1)} %get-tuple-element.129.gkv_ref) | copy-start | bytes 1179652
  243.5 4.4 %collective-permute-start.29 = (bf16[288,768]{1,0:T(8,128)(2,1)S(1)}, bf16[288,768]{1,0:T(8,128)(2,1)S(1)}, u32[]{:S(2)}, u32[]{:S(2)}) collective-permute-start(bf16[288,768]{1,0:T(8,128)(2,1)S(1)} %get-tuple-element.139), channel_id=1, source_target_pairs={{0,1},{1,0},{2,3},{3,2},{4,5},{5,4},{6,7},{7,6},{8,9},{9,8},{10,11... | collective-permute-start | bytes 1327112 | tf_op jit(solution)/shard_map/ppermute | solution.py:748
  244.7 11.7 %collective-permute-start.27 = (bf16[576,384]{1,0:T(8,128)(2,1)S(1)}, bf16[576,384]{1,0:T(8,128)(2,1)S(1)}, u32[]{:S(2)}, u32[]{:S(2)}) collective-permute-start(bf16[576,384]{1,0:T(8,128)(2,1)S(1)} %slice_bitcast_fusion.2), channel_id=1, source_target_pairs={{0,0},{1,3},{2,2},{3,1},{4,7},{5,6},{6,5},{7,4},{8,8},{9,11},{10,1... | collective-permute-start | bytes 1327112 | tf_op jit(solution)/shard_map/ppermute | solution.py:1045
  247.9 9.7 %collective-permute-start.28 = (bf16[288,768]{1,0:T(8,128)(2,1)S(1)}, bf16[288,768]{1,0:T(8,128)(2,1)S(1)}, u32[]{:S(2)}, u32[]{:S(2)}) collective-permute-start(bf16[288,768]{1,0:T(8,128)(2,1)S(1)} %get-tuple-element.137), channel_id=1, source_target_pairs={{0,1},{1,0},{2,3},{3,2},{4,5},{5,4},{6,7},{7,6},{8,9},{9,8},{10,11... | collective-permute-start | bytes 1327112 | tf_op jit(solution)/shard_map/ppermute | solution.py:748
  248.1 15.2 %collective-permute-start.30 = (bf16[288,768]{1,0:T(8,128)(2,1)S(1)}, bf16[288,768]{1,0:T(8,128)(2,1)S(1)}, u32[]{:S(2)}, u32[]{:S(2)}) collective-permute-start(bf16[288,768]{1,0:T(8,128)(2,1)S(1)} %add_convert_fusion.5), channel_id=1, source_target_pairs={{0,2},{1,3},{2,0},{3,1},{4,6},{5,7},{6,4},{7,5},{8,10},{9,11},{10,... | collective-permute-start | bytes 1327112 | tf_op jit(solution)/shard_map/ppermute | solution.py:748
  267.9 7.3 %copy-start.35 = (bf16[768,1152]{1,0:T(8,128)(2,1)S(1)}, bf16[768,1152]{1,0:T(8,128)(2,1)}, u32[]{:S(2)}) copy-start(bf16[768,1152]{1,0:T(8,128)(2,1)} %down_ref.3) | copy-start | bytes 5308420
  267.9 7.3 %copy-start.39 = (bf16[2,256,768]{2,1,0:T(8,128)(2,1)S(1)}, bf16[2,256,768]{2,1,0:T(8,128)(2,1)}, u32[]{:S(2)}) copy-start(bf16[2,256,768]{2,1,0:T(8,128)(2,1)} %get-tuple-element.105.act_in) | copy-start | bytes 2359300
  271.0 13.1 %collective-permute-start.19 = (bf16[256,1152]{1,0:T(8,128)(2,1)S(1)}, bf16[256,1152]{1,0:T(8,128)(2,1)S(1)}, u32[]{:S(2)}, u32[]{:S(2)}) collective-permute-start(bf16[256,1152]{1,0:T(8,128)(2,1)S(1)} %slice.75), channel_id=1, source_target_pairs={{0,1},{1,0},{2,3},{3,2},{4,5},{5,4},{6,7},{7,6},{8,9},{9,8},{10,11... | collective-permute-start | bytes 1769480 | tf_op jit(solution)/shard_map/ppermute | solution.py:748
  275.2 2.5 copy-start.1
  275.2 2.5 copy-start.2
  277.4 36.3 %collective-permute-start.18 = (bf16[256,1152]{1,0:T(8,128)(2,1)}, bf16[256,1152]{1,0:T(8,128)(2,1)}, u32[]{:S(2)}, u32[]{:S(2)}) collective-permute-start(bf16[256,1152]{1,0:T(8,128)(2,1)} %slice.73), channel_id=1, source_target_pairs={{0,1},{1,0},{2,3},{3,2},{4,5},{5,4},{6,7},{7,6},{8,9},{9,8},{10,11... | collective-permute-start | bytes 1769480 | tf_op jit(solution)/shard_map/ppermute | solution.py:748
  278.6 5.4 %copy-start.33 = (f32[1,1152]{1,0:T(1,128)S(1)}, f32[1,1152]{1,0:T(1,128)}, u32[]{:S(2)}) copy-start(f32[1,1152]{1,0:T(1,128)} %get-tuple-element.134) | copy-start | bytes 13828
  284.0 6.1 %copy-start.34 = (f32[1,1152]{1,0:T(1,128)S(1)}, f32[1,1152]{1,0:T(1,128)}, u32[]{:S(2)}) copy-start(f32[1,1152]{1,0:T(1,128)} %get-tuple-element.134) | copy-start | bytes 13828
  284.1 6.1 %collective-permute-start.22 = (f32[2,1152]{1,0:T(2,128)S(1)}, f32[2,1152]{1,0:T(2,128)S(1)}, u32[]{:S(2)}, u32[]{:S(2)}) collective-permute-start(f32[2,1152]{1,0:T(2,128)S(1)} %pad_maximum_fusion.2), channel_id=1, source_target_pairs={{0,1},{1,0},{2,3},{3,2},{4,5},{5,4},{6,7},{7,6},{8,9},{9,8},{10,11... | collective-permute-start | bytes 27656 | tf_op jit(solution)/shard_map/ppermute | solution.py:748
  285.1 28.6 %copy-start.26 = (f32[256,1152]{1,0:T(8,128)S(1)}, f32[256,1152]{1,0:T(8,128)}, u32[]{:S(2)}) copy-start(f32[256,1152]{1,0:T(8,128)} %get-tuple-element.100.mid_ref) | copy-start | bytes 3538948
  285.1 28.6 %copy-start.28 = (bf16[512,1152]{1,0:T(8,128)(2,1)S(1)}, bf16[512,1152]{1,0:T(8,128)(2,1)}, u32[]{:S(2)}) copy-start(bf16[512,1152]{1,0:T(8,128)(2,1)} %copy-done.27) | copy-start | bytes 3538948
  285.1 28.6 %collective-permute-start.20 = (bf16[256,1152]{1,0:T(8,128)(2,1)}, bf16[256,1152]{1,0:T(8,128)(2,1)S(1)}, u32[]{:S(2)}, u32[]{:S(2)}) collective-permute-start(bf16[256,1152]{1,0:T(8,128)(2,1)} %add_convert_fusion.3), channel_id=1, source_target_pairs={{0,2},{1,3},{2,0},{3,1},{4,6},{5,7},{6,4},{7,5},{8,10},{9,11},{10,... | collective-permute-start | bytes 1769480 | tf_op jit(solution)/shard_map/ppermute | solution.py:748
  286.4 21.2 %all-to-all-start = ((bf16[8,216,128]{2,1,0:T(8,128)(2,1)}), bf16[8,216,128]{2,1,0:T(8,128)(2,1)S(1)}, u32[]{:S(2)}, u32[]{:S(2)}) async-start(bf16[8,216,128]{2,1,0:T(8,128)(2,1)} %bitcast.15), calls=%async_computation.2 | async-start | bytes 884736 | tf_op jit(solution)/shard_map/all_to_all | solution.py:1176
  290.2 9.9 %collective-permute-start.23 = (f32[2,1152]{1,0:T(2,128)S(1)}, f32[2,1152]{1,0:T(2,128)S(1)}, u32[]{:S(2)}, u32[]{:S(2)}) collective-permute-start(f32[2,1152]{1,0:T(2,128)S(1)} %fusion.7), channel_id=1, source_target_pairs={{0,2},{1,3},{2,0},{3,1},{4,6},{5,7},{6,4},{7,5},{8,10},{9,11},{10,... | collective-permute-start | bytes 27656 | tf_op jit(solution)/shard_map/ppermute | solution.py:748
  300.1 3.0 collective-permute-start.24
  303.1 3.2 collective-permute-start.25
  306.3 9.6 %collective-permute-start.26 = (f32[2,1152]{1,0:T(2,128)S(1)}, f32[2,1152]{1,0:T(2,128)S(1)}, u32[]{:S(2)}, u32[]{:S(2)}) collective-permute-start(f32[2,1152]{1,0:T(2,128)S(1)} %add.136), channel_id=1, source_target_pairs={{0,16},{4,20},{8,24},{12,28},{16,0},{20,4},{24,8},{28,12},{1,17},{... | collective-permute-start | bytes 27656 | tf_op jit(solution)/shard_map/ppermute | solution.py:752
  308.5 21.9 %all-to-all-start.1 = ((bf16[8,216,128]{2,1,0:T(8,128)(2,1)}), bf16[8,216,128]{2,1,0:T(8,128)(2,1)S(1)}, u32[]{:S(2)}, u32[]{:S(2)}) async-start(bf16[8,216,128]{2,1,0:T(8,128)(2,1)} %broadcast_in_dim.40), calls=%async_computation.3 | async-start | bytes 884736 | tf_op jit(solution)/shard_map/all_to_all | solution.py:1176
  (21 other events, 31.0 us)
Sparse Core Ops, SparseCore 0:
  29.1 38.4 all-gather.4
  69.7 29.0 all-gather.8
  135.0 59.9 reduce-scatter.6
  197.6 38.1 reduce-scatter.8
  238.6 27.6 reduce-scatter.10
  268.3 92.7 all-gather.6
